TPU v7x, 32 devices: a whole 2x2x4 slice. The times are simulated.
32 devices in a mesh: tok: 8 (over z, x), head: 4 (over y, core).
Axes of the slice: x: 2, y: 2, z: 4, core: 2. Of those that a mesh axis runs over, the one named last changes fastest.
Arguments:
- queries: bfloat16 [8192, 4096], P(('tok', 'head')), may hold values from -6 to 6
- key_tokens: bfloat16 [8192, 4096], P(('tok', 'head')), may hold values from -6 to 6
- values: bfloat16 [8192, 4096], P(('tok', 'head')), may hold values from -6 to 6
- out_grad: bfloat16 [8192, 4096], P(('tok', 'head')), may hold values from -6 to 6
- learn_rates: float32 [8192, 16], P('tok', 'head'), may hold values from 0.2 to 2
- w_gate: bfloat16 [16, 256, 256], P('head'), may hold values from -0.375 to 0.375
- w_up: bfloat16 [16, 256, 256], P('head'), may hold values from -0.375 to 0.375
- w_down: bfloat16 [16, 256, 256], P('head'), may hold values from -0.375 to 0.375
Outputs:
- grad_queries: bfloat16 [8192, 4096], P(('tok', 'head'))
- grad_keys: bfloat16 [8192, 4096], P(('tok', 'head'))
- grad_values: bfloat16 [8192, 4096], P(('tok', 'head'))
All inputs are finite; a program needn't handle non-finite values.
Results may differ from a plain program's by a relative error of at most 0.02.
Values may be sent and summed in bfloat16 or wider, within the bound.
No kernel may reach another device: no remote copies, remote signals or barrier semaphores. Data moves between devices by JAX's collectives and lax.ppermute only.
A program may use at most 128 MiB of HBM per device.

v0:
```python
import math

import jax
import jax.numpy as jnp
from jax import lax
from jax.sharding import PartitionSpec as P

DH = 256


def silu_slope(pre_act):
    sigmoid_val = jax.nn.sigmoid(pre_act)
    return sigmoid_val * (1.0 + pre_act * (1.0 - sigmoid_val))


def silu_curve(pre_act):
    sigmoid_val = jax.nn.sigmoid(pre_act)
    return sigmoid_val * (1.0 - sigmoid_val) * (2.0 + pre_act * (1.0 - 2.0 * sigmoid_val))


def key_forward(key_rows, scaled, gate_mat, up_mat, down_mat):
    gate_pre = jnp.dot(key_rows, gate_mat, preferred_element_type=jnp.float32)
    up_pre = jnp.dot(key_rows, up_mat, preferred_element_type=jnp.float32)
    gate_act = jax.nn.silu(gate_pre)
    hidden = (gate_act * up_pre).astype(jnp.bfloat16)
    key_dhid = jnp.dot(scaled, down_mat.T, preferred_element_type=jnp.float32)
    grad_gate = (key_dhid * up_pre * silu_slope(gate_pre)).astype(jnp.bfloat16)
    grad_upper = (key_dhid * gate_act).astype(jnp.bfloat16)
    delta_gate = jnp.dot(key_rows.T, grad_gate, preferred_element_type=jnp.float32)
    delta_up = jnp.dot(key_rows.T, grad_upper, preferred_element_type=jnp.float32)
    delta_down = jnp.dot(hidden.T, scaled, preferred_element_type=jnp.float32)
    stored = (gate_pre, up_pre, hidden, key_dhid, grad_gate, grad_upper)
    return ((delta_gate, delta_up, delta_down), stored)


def query_side(query_rows, out_rows, fresh_gate, fresh_up, fresh_down):
    gate_pre = jnp.dot(query_rows, fresh_gate, preferred_element_type=jnp.float32)
    up_pre = jnp.dot(query_rows, fresh_up, preferred_element_type=jnp.float32)
    gate_act = jax.nn.silu(gate_pre)
    hidden = (gate_act * up_pre).astype(jnp.bfloat16)
    query_dhid = jnp.dot(out_rows, fresh_down.T, preferred_element_type=jnp.float32)
    grad_gate = (query_dhid * up_pre * silu_slope(gate_pre)).astype(jnp.bfloat16)
    grad_upper = (query_dhid * gate_act).astype(jnp.bfloat16)
    query_grad = jnp.dot(grad_gate, fresh_gate.T, preferred_element_type=jnp.float32)
    query_grad = query_grad + jnp.dot(grad_upper, fresh_up.T, preferred_element_type=jnp.float32)
    sum_gate = jnp.dot(query_rows.T, grad_gate, preferred_element_type=jnp.float32)
    sum_up = jnp.dot(query_rows.T, grad_upper, preferred_element_type=jnp.float32)
    sum_down = jnp.dot(hidden.T, out_rows, preferred_element_type=jnp.float32)
    return (query_grad.astype(jnp.bfloat16), (sum_gate, sum_up, sum_down))


def key_back(
    key_rows, scaled, rate_col, gate_mat, up_mat, down_mat, stored, adj_gate, adj_up, adj_down
):
    gate_pre, up_pre, hidden, key_dhid, grad_gate, grad_upper = stored
    back_dgate = jnp.dot(key_rows, adj_gate, preferred_element_type=jnp.float32)
    back_dup = jnp.dot(key_rows, adj_up, preferred_element_type=jnp.float32)
    back_hidden = jnp.dot(scaled, adj_down.T, preferred_element_type=jnp.float32)
    back_scaled = jnp.dot(hidden, adj_down, preferred_element_type=jnp.float32)
    gate_act = jax.nn.silu(gate_pre)
    gate_slope = silu_slope(gate_pre)
    back_dhid = (back_dgate * up_pre * gate_slope + back_dup * gate_act).astype(jnp.bfloat16)
    back_gate = (
        back_dgate * key_dhid * up_pre * silu_curve(gate_pre)
        + (back_dup * key_dhid + back_hidden * up_pre) * gate_slope
    ).astype(jnp.bfloat16)
    back_upper = (back_dgate * key_dhid * gate_slope + back_hidden * gate_act).astype(jnp.bfloat16)
    key_grad = jnp.dot(grad_gate, adj_gate.T, preferred_element_type=jnp.float32)
    key_grad = key_grad + jnp.dot(grad_upper, adj_up.T, preferred_element_type=jnp.float32)
    key_grad = key_grad + jnp.dot(back_gate, gate_mat.T, preferred_element_type=jnp.float32)
    key_grad = key_grad + jnp.dot(back_upper, up_mat.T, preferred_element_type=jnp.float32)
    value_grad = rate_col[:, None] * (
        back_scaled + jnp.dot(back_dhid, down_mat, preferred_element_type=jnp.float32)
    )
    return (key_grad.astype(jnp.bfloat16), value_grad.astype(jnp.bfloat16))


def body(queries, key_tokens, values, out_grad, learn_rates, w_gate, w_up, w_down):
    query_all, key_all, value_all, out_all = (
        lax.all_to_all(queries, "head", split_axis=1, concat_axis=0, tiled=True),
        lax.all_to_all(key_tokens, "head", split_axis=1, concat_axis=0, tiled=True),
        lax.all_to_all(values, "head", split_axis=1, concat_axis=0, tiled=True),
        lax.all_to_all(out_grad, "head", split_axis=1, concat_axis=0, tiled=True),
    )
    local_heads = w_gate.shape[0]
    local_rows = query_all.shape[0]
    update_scale = 1.0 / math.sqrt(DH * local_rows * lax.axis_size("tok"))

    def by_head(matrix):
        return matrix.reshape(local_rows, local_heads, DH)

    scaled = (learn_rates[:, :, None] * by_head(value_all).astype(jnp.float32)).astype(jnp.bfloat16)
    key_heads = by_head(key_all)
    deltas, stored = jax.vmap(key_forward, in_axes=(1, 1, 0, 0, 0))(
        key_heads, scaled, w_gate, w_up, w_down
    )
    delta_gate, delta_up, delta_down = deltas
    total_gate, total_up, total_down = lax.psum((delta_gate, delta_up, delta_down), "tok")
    fresh_gate = (w_gate.astype(jnp.float32) + update_scale * total_gate).astype(jnp.bfloat16)
    fresh_up = (w_up.astype(jnp.float32) + update_scale * total_up).astype(jnp.bfloat16)
    fresh_down = (w_down.astype(jnp.float32) + update_scale * total_down).astype(jnp.bfloat16)
    query_grad, sums = jax.vmap(query_side, in_axes=(1, 1, 0, 0, 0), out_axes=(1, 0))(
        by_head(query_all), by_head(out_all), fresh_gate, fresh_up, fresh_down
    )
    query_flat = query_grad.reshape(local_rows, local_heads * DH)
    sum_gate, sum_up, sum_down = (
        lax.psum(sums[0].astype(jnp.bfloat16), "tok").astype(jnp.float32),
        lax.psum(sums[1].astype(jnp.bfloat16), "tok").astype(jnp.float32),
        lax.psum(sums[2].astype(jnp.bfloat16), "tok").astype(jnp.float32),
    )
    adj_gate = (update_scale * sum_gate).astype(jnp.bfloat16)
    adj_up = (update_scale * sum_up).astype(jnp.bfloat16)
    adj_down = (update_scale * sum_down).astype(jnp.bfloat16)
    key_grad, value_grad = jax.vmap(
        key_back, in_axes=(1, 1, 1, 0, 0, 0, 0, 0, 0, 0), out_axes=(1, 1)
    )(key_heads, scaled, learn_rates, w_gate, w_up, w_down, stored, adj_gate, adj_up, adj_down)
    key_flat = key_grad.reshape(local_rows, local_heads * DH)
    value_flat = value_grad.reshape(local_rows, local_heads * DH)
    query_home, key_home, value_home = (
        lax.all_to_all(query_flat, "head", split_axis=0, concat_axis=1, tiled=True),
        lax.all_to_all(key_flat, "head", split_axis=0, concat_axis=1, tiled=True),
        lax.all_to_all(value_flat, "head", split_axis=0, concat_axis=1, tiled=True),
    )
    return (query_home, key_home, value_home)


def solution(mesh):
    return jax.shard_map(
        body,
        mesh=mesh,
        in_specs=(
            P(("tok", "head"), None),
            P(("tok", "head"), None),
            P(("tok", "head"), None),
            P(("tok", "head"), None),
            P("tok", "head"),
            P("head", None, None),
            P("head", None, None),
            P("head", None, None),
        ),
        out_specs=(P(("tok", "head"), None), P(("tok", "head"), None), P(("tok", "head"), None)),
        check_vma=False,
    )
```

profile of v0, /device:TPU:0, one launch (start us, length us, event | category | flops | bytes accessed | tf_op | source)
XLA Modules:
  0.0 444.7 jit_solution(12690404409971239799)
XLA Ops:
  7.2 3.1 copy.159
  10.3 4.3 all-to-all-start
  14.6 3.1 copy.158
  17.7 22.5 %all-to-all-done = bf16[256,4,1024]{2,0,1:T(8,128)(2,1)S(1)} async-done(((bf16[256,4,1024]{2,0,1:T(8,128)(2,1)}), bf16[256,4,1024]{2,0,1:T(8,128)(2,1)S(1)}, u32[]{:S(2)}, u32[]{:S(2)}) %all-to-all-start) | async-done | bytes 2097184 | tf_op jit(solution)/shard_map/all_to_all | solution.py:81
  40.2 4.5 %all-to-all-start.1 = ((bf16[256,4,1024]{2,0,1:T(8,128)(2,1)}), bf16[256,4,1024]{2,0,1:T(8,128)(2,1)}, u32[]{:S(2)}, u32[]{:S(2)}) async-start(bf16[256,4,1024]{2,0,1:T(8,128)(2,1)} %bitcast.167), calls=%async_computation.1 | async-start | bytes 4194304 | tf_op jit(solution)/shard_map/all_to_all | solution.py:82
  44.7 3.1 copy.156
  47.8 2.7 reshape.51
  50.6 3.0 copy.84
  53.6 16.9 %all-to-all-done.1 = bf16[256,4,1024]{2,0,1:T(8,128)(2,1)} async-done(((bf16[256,4,1024]{2,0,1:T(8,128)(2,1)}), bf16[256,4,1024]{2,0,1:T(8,128)(2,1)}, u32[]{:S(2)}, u32[]{:S(2)}) %all-to-all-start.1) | async-done | bytes 2097184 | tf_op jit(solution)/shard_map/all_to_all | solution.py:82
  70.4 4.4 all-to-all-start.3
  74.9 4.0 convert_bitcast_fusion
  78.9 5.7 %reshape.54 = f32[1024,4,256]{2,1,0:T(4,128)} reshape(f32[4,256,1024]{2,1,0:T(8,128)} %convert_bitcast_fusion) | data formatting | bytes 8388608 | tf_op jit(solution)/shard_map/convert_element_type | solution.py:92
  84.6 3.3 fusion.21
  90.8 4.1 multiply_convert_fusion.2
  101.0 3.1 copy.157
  104.1 4.5 %all-to-all-start.2 = ((bf16[256,4,1024]{2,0,1:T(8,128)(2,1)}), bf16[256,4,1024]{2,0,1:T(8,128)(2,1)}, u32[]{:S(2)}, u32[]{:S(2)}) async-start(bf16[256,4,1024]{2,0,1:T(8,128)(2,1)} %bitcast.166), calls=%async_computation.2 | async-start | bytes 4194304 | tf_op jit(solution)/shard_map/all_to_all | solution.py:83
  109.1 4.5 %reshape.53 = bf16[1024,4,256]{2,1,0:T(4,128)(2,1)} reshape(bf16[4,256,1024]{2,1,0:T(8,128)(2,1)} %bitcast.6) | data formatting | bytes 4194304 | tf_op jit(solution)/shard_map/reshape | solution.py:90
  113.6 4.3 copy.98
  117.9 16.4 %all-to-all-done.2 = bf16[256,4,1024]{2,0,1:T(8,128)(2,1)} async-done(((bf16[256,4,1024]{2,0,1:T(8,128)(2,1)}), bf16[256,4,1024]{2,0,1:T(8,128)(2,1)}, u32[]{:S(2)}, u32[]{:S(2)}) %all-to-all-start.2) | async-done | bytes 2097184 | tf_op jit(solution)/shard_map/all_to_all | solution.py:83
  134.3 4.5 %reshape.52 = bf16[1024,4,256]{2,1,0:T(4,128)(2,1)} reshape(bf16[4,256,1024]{2,1,0:T(8,128)(2,1)} %bitcast.2) | data formatting | bytes 4194304 | tf_op jit(solution)/shard_map/reshape | solution.py:90
  138.8 93.6 %all-reduce.5.cloned.1.call-done = (f32[4,256,256]{2,1,0:T(8,128)}, f32[4,256,256]{2,1,0:T(8,128)}, f32[4,256,256]{2,1,0:T(8,128)}) async-done(((f32[4,256,256]{2,1,0:T(8,128)}, f32[4,256,256]{2,1,0:T(8,128)}, f32[4,256,256]{2,1,0:T(8,128)}), (f32[4,256,256]{2,1,0:T(8,128)}, f32[4,256,256]{2,1,0:T(8,128)}, f32[4,256,256]{2,1,0:T(8,128)})) %all-reduce.5.cloned.1.call-update) | async-done | bytes 3145744 | tf_op jit(solution)/shard_map/psum | solution.py:98
  232.4 2.9 fusion.83
  237.0 2.5 fusion.47
  246.4 2.8 fusion.82
  250.0 2.9 copy.96
  252.9 4.4 all_to_all.99
  257.4 4.7 %all-to-all-start.4 = ((bf16[4,256,1024]{2,1,0:T(8,128)(2,1)}), bf16[4,256,1024]{2,1,0:T(8,128)(2,1)}, u32[]{:S(2)}, u32[]{:S(2)}) async-start(bf16[4,256,1024]{2,1,0:T(8,128)(2,1)} %all_to_all.99), calls=%async_computation.4 | async-start | bytes 4194304 | tf_op jit(solution)/shard_map/all_to_all | solution.py:120
  262.1 73.0 %all-reduce.7.cloned.1.call-done = (bf16[4,256,256]{2,1,0:T(8,128)(2,1)}, bf16[4,256,256]{2,1,0:T(8,128)(2,1)}, bf16[4,256,256]{2,1,0:T(8,128)(2,1)}) async-done(((bf16[4,256,256]{2,1,0:T(8,128)(2,1)}, bf16[4,256,256]{2,1,0:T(8,128)(2,1)}, bf16[4,256,256]{2,1,0:T(8,128)(2,1)}), (bf16[4,256,256]{2,1,0:T(8,128)(2,1)}, bf16[4,256,256]{2,1,0:T(8,128)(2,1)}, ...) | async-done | bytes 1572880 | tf_op jit(solution)/shard_map/psum | solution.py:109
  335.0 4.5 %fusion.70 = f32[4,1024,256]{2,1,0:T(8,128)} fusion(bf16[1024,4,256]{2,0,1:T(8,128)(2,1)} %copy-done, bf16[4,256,256]{2,1,0:T(8,128)(2,1)} %get-tuple-element.9), kind=kOutput, calls=%fused_computation.83 | convolution fusion | flops 537657344 | bytes 6815744 | tf_op jit(solution)/shard_map/vmap()/dot_general | solution.py:58
  341.2 2.8 fusion.66
  345.6 2.8 fusion.68
  350.0 3.0 copy-done.3
  352.9 2.9 fusion.6
  357.5 2.7 all_to_all.107
  360.2 12.0 %fusion.34 = f32[4,1024,256]{2,1,0:T(8,128)} fusion(bf16[4,256,256]{2,1,0:T(8,128)(2,1)S(1)} %copy-done.13, f32[4,1024,256]{2,1,0:T(8,128)} %copy-done.4, f32[4,256,1024]{1,2,0:T(8,128)} %copy-done.16, f32[4,1024,256]{2,1,0:T(8,128)} %fusion.70, f32[4,1024,256]{2,1,0:T(8,128)} %get-tuple-element.17, f32[4,1024,256]{2,1,0:T(8,128)} %copy-done.2, ...), kind=kOutput, calls=%fused_computation.58 | convolution fusion | flops 559939584 | bytes 29884416 | tf_op jit(solution)/shard_map/vmap()/dot_general | solution.py:70
  372.3 3.8 all-to-all-start.6
  376.1 13.2 %fusion.40 = bf16[1024,4,256]{2,0,1:T(8,128)(2,1)} fusion(bf16[4,256,256]{2,1,0:T(8,128)(2,1)S(1)} %copy-done.12, f32[4,1024,256]{2,1,0:T(8,128)} %fusion.70, f32[4,1024,256]{2,1,0:T(8,128)} %copy-done.4, f32[4,256,1024]{1,2,0:T(8,128)} %copy-done.5, f32[4,1024,256]{2,1,0:T(8,128)} %fusion.34, f32[4,1024,256]{2,1,0:T(8,128)} %fusion.66, ...), kind=kOutput, calls=%fused_computation.63 | convolution fusion | flops 554696704 | bytes 31981568 | tf_op jit(solution)/shard_map/vmap()/dot_general | solution.py:71
  389.3 4.5 %copy.111 = bf16[1024,4,256]{2,1,0:T(4,128)(2,1)} copy(bf16[1024,4,256]{2,0,1:T(8,128)(2,1)} %fusion.40) | data formatting | bytes 4194304 | tf_op jit(solution)/shard_map/vmap()/convert_element_type | solution.py:75
  393.8 4.4 all_to_all.103
  398.3 3.5 all-to-all-done.6
  401.7 4.5 %all-to-all-start.5 = ((bf16[4,256,1024]{2,1,0:T(8,128)(2,1)}), bf16[4,256,1024]{2,1,0:T(8,128)(2,1)}, u32[]{:S(2)}, u32[]{:S(2)}) async-start(bf16[4,256,1024]{2,1,0:T(8,128)(2,1)} %all_to_all.103), calls=%async_computation.5 | async-start | bytes 4194304 | tf_op jit(solution)/shard_map/all_to_all | solution.py:121
  406.2 3.9 copy.97
  410.1 4.1 copy.115
  414.2 2.5 copy.114
  416.7 4.1 copy.117
  420.8 11.1 %all-to-all-done.5 = bf16[4,256,1024]{2,1,0:T(8,128)(2,1)} async-done(((bf16[4,256,1024]{2,1,0:T(8,128)(2,1)}), bf16[4,256,1024]{2,1,0:T(8,128)(2,1)}, u32[]{:S(2)}, u32[]{:S(2)}) %all-to-all-start.5) | async-done | bytes 2097184 | tf_op jit(solution)/shard_map/all_to_all | solution.py:121
  431.9 2.8 copy.112
  434.8 2.9 copy.116
  (79 shorter events, 25.1 us)
Async XLA Ops:
  10.3 29.9 %all-to-all-start = ((bf16[256,4,1024]{2,0,1:T(8,128)(2,1)}), bf16[256,4,1024]{2,0,1:T(8,128)(2,1)S(1)}, u32[]{:S(2)}, u32[]{:S(2)}) async-start(bf16[256,4,1024]{2,0,1:T(8,128)(2,1)} %bitcast.168), calls=%async_computation | async-start | bytes 4194304 | tf_op jit(solution)/shard_map/all_to_all | solution.py:81
  40.2 30.2 %all-to-all-start.1 = ((bf16[256,4,1024]{2,0,1:T(8,128)(2,1)}), bf16[256,4,1024]{2,0,1:T(8,128)(2,1)}, u32[]{:S(2)}, u32[]{:S(2)}) async-start(bf16[256,4,1024]{2,0,1:T(8,128)(2,1)} %bitcast.167), calls=%async_computation.1 | async-start | bytes 4194304 | tf_op jit(solution)/shard_map/all_to_all | solution.py:82
  70.4 33.7 %all-to-all-start.3 = ((bf16[256,4,1024]{2,0,1:T(8,128)(2,1)}), bf16[256,4,1024]{2,0,1:T(8,128)(2,1)}, u32[]{:S(2)}, u32[]{:S(2)}) async-start(bf16[256,4,1024]{2,0,1:T(8,128)(2,1)} %bitcast.163), calls=%async_computation.3 | async-start | bytes 4194304 | tf_op jit(solution)/shard_map/all_to_all | solution.py:80
  74.9 157.5 %all-reduce.5.cloned.1.call-start = ((), (), s32[]{:S(2)}) async-start(), calls=%async_computation.7 | async-start | bytes 6291456 | tf_op jit(solution)/shard_map/psum | solution.py:98
  78.9 5.7 %copy-start.27 = (f32[1024,4]{0,1:T(4,128)S(1)}, f32[1024,4]{0,1:T(4,128)}, u32[]{:S(2)}) copy-start(f32[1024,4]{0,1:T(4,128)} %param.12) | copy-start | bytes 49156
  84.6 3.4 copy-start.13
  88.0 7.0 %copy-start = (bf16[1024,4,256]{2,0,1:T(8,128)(2,1)}, bf16[1024,4,256]{2,0,1:T(8,128)(2,1)S(1)}, u32[]{:S(2)}) copy-start(bf16[1024,4,256]{2,0,1:T(8,128)(2,1)S(1)} %fusion.21) | copy-start | bytes 6291460
  88.0 1.4 copy-start.24
  89.4 5.6 %copy-start.2 = (f32[4,1024,256]{2,1,0:T(8,128)}, f32[4,1024,256]{2,1,0:T(8,128)S(1)}, u32[]{:S(2)}) copy-start(f32[4,1024,256]{2,1,0:T(8,128)S(1)} %fusion.89) | copy-start | bytes 12582916
  89.4 1.4 copy-start.12
  90.8 4.2 copy-start.4
  95.0 4.2 copy-start.8
  95.0 4.2 copy-start.10
  95.0 4.2 copy-start.6
  104.1 30.2 %all-to-all-start.2 = ((bf16[256,4,1024]{2,0,1:T(8,128)(2,1)}), bf16[256,4,1024]{2,0,1:T(8,128)(2,1)}, u32[]{:S(2)}, u32[]{:S(2)}) async-start(bf16[256,4,1024]{2,0,1:T(8,128)(2,1)} %bitcast.166), calls=%async_computation.2 | async-start | bytes 4194304 | tf_op jit(solution)/shard_map/all_to_all | solution.py:83
  108.6 226.5 %all-reduce.7.cloned.1.call-start = ((), (), s32[]{:S(2)}) async-start(), calls=%async_computation.8 | async-start | bytes 3145728 | tf_op jit(solution)/shard_map/psum | solution.py:109
  232.4 3.0 copy-start.1
  232.4 3.0 copy-start.14
  235.4 1.6 copy-start.19
  237.0 2.5 copy-start.25
  237.0 2.5 copy-start.28
  241.9 1.3 copy-start.17
  241.9 2.9 copy-start.20
  246.4 2.8 copy-start.15
  246.4 2.9 copy-start.18
  257.4 114.9 %all-to-all-start.4 = ((bf16[4,256,1024]{2,1,0:T(8,128)(2,1)}), bf16[4,256,1024]{2,1,0:T(8,128)(2,1)}, u32[]{:S(2)}, u32[]{:S(2)}) async-start(bf16[4,256,1024]{2,1,0:T(8,128)(2,1)} %all_to_all.99), calls=%async_computation.4 | async-start | bytes 4194304 | tf_op jit(solution)/shard_map/all_to_all | solution.py:120
  335.0 4.5 %copy-start.11 = (bf16[4,1024,256]{2,1,0:T(8,128)(2,1)S(1)}, bf16[4,1024,256]{2,1,0:T(8,128)(2,1)}, u32[]{:S(2)}) copy-start(bf16[4,1024,256]{2,1,0:T(8,128)(2,1)} %copy-done.10) | copy-start | bytes 6291460
  335.0 4.5 %copy-start.23 = (bf16[4,256,256]{2,1,0:T(8,128)(2,1)S(1)}, bf16[4,256,256]{2,1,0:T(8,128)(2,1)}, u32[]{:S(2)}) copy-start(bf16[4,256,256]{2,1,0:T(8,128)(2,1)} %get-tuple-element.9) | copy-start | bytes 1572868
  339.5 1.6 copy-start.9
  339.5 1.7 copy-start.22
  344.0 1.6 copy-start.7
  344.0 1.7 copy-start.21
  344.9 4.5 %copy-start.5 = (f32[4,256,1024]{1,2,0:T(8,128)}, f32[4,256,1024]{1,2,0:T(8,128)S(1)}, u32[]{:S(2)}) copy-start(f32[4,256,1024]{1,2,0:T(8,128)S(1)} %fusion.65) | copy-start | bytes 12582916
  345.6 4.3 copy-start.29
  348.4 4.5 %copy-start.3 = (f32[4,1024,256]{2,1,0:T(8,128)S(1)}, f32[4,1024,256]{2,1,0:T(8,128)}, u32[]{:S(2)}) copy-start(f32[4,1024,256]{2,1,0:T(8,128)} %copy-done.2) | copy-start | bytes 12582916
  348.4 4.5 %copy-start.26 = (bf16[4,256,256]{2,1,0:T(8,128)(2,1)S(1)}, bf16[4,256,256]{2,1,0:T(8,128)(2,1)}, u32[]{:S(2)}) copy-start(bf16[4,256,256]{2,1,0:T(8,128)(2,1)} %param.15) | copy-start | bytes 1572868
  349.4 6.5 %copy-start.16 = (f32[4,256,1024]{1,2,0:T(8,128)}, f32[4,256,1024]{1,2,0:T(8,128)S(1)}, u32[]{:S(2)}) copy-start(f32[4,256,1024]{1,2,0:T(8,128)S(1)} %fusion.67) | copy-start | bytes 12582916
  372.3 29.4 %all-to-all-start.6 = ((bf16[4,256,1024]{2,1,0:T(8,128)(2,1)}), bf16[4,256,1024]{2,1,0:T(8,128)(2,1)S(1)}, u32[]{:S(2)}, u32[]{:S(2)}) async-start(bf16[4,256,1024]{2,1,0:T(8,128)(2,1)} %all_to_all.107), calls=%async_computation.6 | async-start | bytes 4194304 | tf_op jit(solution)/shard_map/all_to_all | solution.py:122
  401.7 30.2 %all-to-all-start.5 = ((bf16[4,256,1024]{2,1,0:T(8,128)(2,1)}), bf16[4,256,1024]{2,1,0:T(8,128)(2,1)}, u32[]{:S(2)}, u32[]{:S(2)}) async-start(bf16[4,256,1024]{2,1,0:T(8,128)(2,1)} %all_to_all.103), calls=%async_computation.5 | async-start | bytes 4194304 | tf_op jit(solution)/shard_map/all_to_all | solution.py:121
Sparse Core Ops, SparseCore 0:
  101.1 131.2 all-reduce.4
  246.5 88.4 all-reduce.6
where the time goes:
time: 453 us; the launch traced here: 445 us
  waiting for transfers between devices  237 us (52%)
  local copies, waits for them, and re-layouts  86.5 us (19%)
  matrix products  68 us (15%)
  starting transfers between devices  31.1 us (7%)
  between operations  14.6 us (3%)
  other arithmetic  7.35 us (2%)
    psum x1, waiting for transfers between devices, body(): lax.psum((delta_gate, delta_up, delta_down), 'tok')  93.6 us
    psum x1, waiting for transfers between devices, body(): lax.psum(sums[2].astype(jnp.bfloat16), 'tok').astype(jnp.float32)  73 us
    all_to_all x1, waiting for transfers between devices, body(): lax.all_to_all(key_tokens, 'head', split_axis=1, concat_axis=0, tiled=True)  22.5 us
    unnamed x63, local copies, waits for them, and re-layouts  19.3 us
    reshape x5, local copies, waits for them, and re-layouts, by_head(): return matrix.reshape(local_rows, local_heads, DH)  19 us
    all_to_all x1, waiting for transfers between devices, body(): lax.all_to_all(values, 'head', split_axis=1, concat_axis=0, tiled=True)  16.9 us
    all_to_all x1, waiting for transfers between devices, body(): lax.all_to_all(out_grad, 'head', split_axis=1, concat_axis=0, tiled=True)  16.4 us
    dot_general x1, matrix products, key_back(): jnp.dot(back_upper, up_mat.T, preferred_element_type=jnp.float32)  13.2 us
  transfers between devices with their start and end apart: 9, of which 7 were waited for; matrix products, arithmetic and copies ran while one was open for 27% of the time, Pallas kernels for 0%

commit v1 on v0

v1 whole, which is shorter than its diff:
```python
import functools
import math

import jax
import jax.numpy as jnp
from jax import lax
from jax.experimental import pallas as pl
from jax.experimental.pallas import tpu as pltpu
from jax.sharding import Mesh, PartitionSpec as P

F32 = jnp.float32
BF16 = jnp.bfloat16


def mm(a, b):
    return lax.dot_general(a, b, (((1,), (0,)), ((), ())), preferred_element_type=F32)


def mm_nt(a, b):
    return lax.dot_general(a, b, (((1,), (1,)), ((), ())), preferred_element_type=F32)


def mm_tn(a, b):
    return lax.dot_general(a, b, (((0,), (0,)), ((), ())), preferred_element_type=F32)


def wide(rate, columns):
    return jnp.concatenate([rate] * (columns // rate.shape[1]), axis=1)


def rows_of(ref, which):
    block = ref[:, which]
    return block.reshape(block.shape[0] * block.shape[1], block.shape[2])


def put_rows(ref, which, value):
    ref[:, which] = value.reshape(ref.shape[0], ref.shape[2], ref.shape[3])


def key_kernel(s_ref, kv_ref, rate_ref, wg_ref, wu_ref, wd_ref, part_ref, sent_ref):
    step = pl.program_id(0)
    width = kv_ref.shape[-1]
    k = rows_of(kv_ref, 0)
    scaled = (wide(rate_ref[...], width) * rows_of(kv_ref, 1).astype(F32)).astype(BF16)
    gate = mm(k, wg_ref[0])
    up = mm(k, wu_ref[0])
    dhid = mm_nt(scaled, wd_ref[0])
    sig = jax.nn.sigmoid(gate)
    act = gate * sig
    hidden = (act * up).astype(BF16)
    dgate = (dhid * up * (sig * (1.0 + gate * (1.0 - sig)))).astype(BF16)
    dup = (dhid * act).astype(BF16)

    @pl.when(step == 0)
    def _():
        part_ref[...] = jnp.zeros_like(part_ref)

    part_ref[0] += mm_tn(k, dgate)
    part_ref[1] += mm_tn(k, dup)
    part_ref[2] += mm_tn(hidden, scaled)

    @pl.when(step == pl.num_programs(0) - 1)
    def _():
        sent_ref[...] = part_ref[...].astype(BF16)


def query_kernel(
    scale, s_ref, qo_ref, wg_ref, wu_ref, wd_ref, own_ref, other_ref, gq_ref, part_ref, sent_ref, fresh
):
    step = pl.program_id(0)

    @pl.when(step == 0)
    def _():
        part_ref[...] = jnp.zeros_like(part_ref)
        for i, w_ref in enumerate((wg_ref, wu_ref, wd_ref)):
            total = own_ref[i] + other_ref[i].astype(F32)
            fresh[i] = (w_ref[0].astype(F32) + scale * total).astype(BF16)

    q = rows_of(qo_ref, 0)
    o = rows_of(qo_ref, 1)
    gate = mm(q, fresh[0])
    up = mm(q, fresh[1])
    dhid = mm_nt(o, fresh[2])
    sig = jax.nn.sigmoid(gate)
    act = gate * sig
    hidden = (act * up).astype(BF16)
    dgate = (dhid * up * (sig * (1.0 + gate * (1.0 - sig)))).astype(BF16)
    dup = (dhid * act).astype(BF16)
    grad = mm_nt(dgate, fresh[0]) + mm_nt(dup, fresh[1])
    gq_ref[...] = grad.astype(BF16).reshape(gq_ref.shape)
    part_ref[0] += mm_tn(q, dgate)
    part_ref[1] += mm_tn(q, dup)
    part_ref[2] += mm_tn(hidden, o)

    @pl.when(step == pl.num_programs(0) - 1)
    def _():
        sent_ref[...] = part_ref[...].astype(BF16)


def back_kernel(
    scale, s_ref, kv_ref, rate_ref, wg_ref, wu_ref, wd_ref, own_ref, other_ref, gkv_ref, adj
):
    step = pl.program_id(0)

    @pl.when(step == 0)
    def _():
        adj[...] = (scale * (own_ref[...] + other_ref[...].astype(F32))).astype(BF16)

    width = kv_ref.shape[-1]
    k = rows_of(kv_ref, 0)
    rate = wide(rate_ref[...], width)
    scaled = (rate * rows_of(kv_ref, 1).astype(F32)).astype(BF16)
    gate = mm(k, wg_ref[0])
    up = mm(k, wu_ref[0])
    dhid = mm_nt(scaled, wd_ref[0])
    sig = jax.nn.sigmoid(gate)
    act = gate * sig
    rest = 1.0 - sig
    slope = sig * (1.0 + gate * rest)
    curve = sig * rest * (2.0 + gate * (1.0 - 2.0 * sig))
    hidden = (act * up).astype(BF16)
    dgate = (dhid * up * slope).astype(BF16)
    dup = (dhid * act).astype(BF16)
    back_dgate = mm(k, adj[0])
    back_dup = mm(k, adj[1])
    back_hidden = mm_nt(scaled, adj[2])
    back_scaled = mm(hidden, adj[2])
    back_dhid = (back_dgate * up * slope + back_dup * act).astype(BF16)
    back_gate = (
        back_dgate * dhid * up * curve + (back_dup * dhid + back_hidden * up) * slope
    ).astype(BF16)
    back_upper = (back_dgate * dhid * slope + back_hidden * act).astype(BF16)
    grad_k = mm_nt(dgate, adj[0]) + mm_nt(dup, adj[1])
    grad_k = grad_k + mm_nt(back_gate, wg_ref[0]) + mm_nt(back_upper, wu_ref[0])
    grad_v = rate * (back_scaled + mm(back_dhid, wd_ref[0]))
    put_rows(gkv_ref, 0, grad_k.astype(BF16))
    put_rows(gkv_ref, 1, grad_v.astype(BF16))


def blocks_per_step(pieces, rows, most):
    best = 1
    for n in range(1, pieces + 1):
        if pieces % n == 0 and n * rows <= most:
            best = n
    return best


def body(n_t, n_s, n_head, queries, key_tokens, values, out_grad, learn_rates, w_gate, w_up, w_down):
    rows, model = queries.shape
    heads = n_head * n_s
    dim = model // heads
    pieces = heads
    spread = ("head", "s")
    place = lax.axis_index("s").astype(jnp.int32).reshape(1)
    scale = 1.0 / math.sqrt(dim * rows * pieces * n_t)

    def by_head(x):
        return x.reshape(rows, heads, dim).transpose(1, 0, 2)

    def exchange(x):
        return lax.all_to_all(x, spread, split_axis=0, concat_axis=0, tiled=True)

    def pair(own, sent):
        if n_t == 1:
            return own, jnp.zeros_like(sent)
        if n_t == 2:
            return own, lax.ppermute(sent, "t", [(0, 1), (1, 0)])
        return jnp.zeros_like(own), lax.psum(sent, "t")

    kv = exchange(jnp.stack([by_head(key_tokens), by_head(values)], axis=1))
    rate = lax.all_to_all(learn_rates.T, "s", split_axis=0, concat_axis=0, tiled=True)
    rate = rate.reshape(n_s, n_head, rows).transpose(1, 0, 2).reshape(pieces * rows, 1)
    rate = jnp.broadcast_to(rate, (pieces * rows, min(128, dim)))
    qo = exchange(jnp.stack([by_head(queries), by_head(out_grad)], axis=1))

    per = blocks_per_step(pieces, rows, 1024)
    grid = (pieces // per,)
    two_spec = pl.BlockSpec((per, 2, rows, dim), lambda i, s: (i, 0, 0, 0))
    one_spec = pl.BlockSpec((per, rows, dim), lambda i, s: (i, 0, 0))
    rate_spec = pl.BlockSpec((per * rows, rate.shape[1]), lambda i, s: (i, 0))
    w_spec = pl.BlockSpec((1, dim, dim), lambda i, s: (s[0], 0, 0))
    sum_spec = pl.BlockSpec((3, dim, dim), lambda i, s: (0, 0, 0))
    sum_shapes = [
        jax.ShapeDtypeStruct((3, dim, dim), F32),
        jax.ShapeDtypeStruct((3, dim, dim), BF16),
    ]
    params = pltpu.CompilerParams(
        dimension_semantics=("arbitrary",), vmem_limit_bytes=56 * 1024 * 1024
    )

    part, sent = pl.pallas_call(
        key_kernel,
        out_shape=sum_shapes,
        grid_spec=pltpu.PrefetchScalarGridSpec(
            num_scalar_prefetch=1,
            grid=grid,
            in_specs=[two_spec, rate_spec, w_spec, w_spec, w_spec],
            out_specs=[sum_spec, sum_spec],
        ),
        compiler_params=params,
        name="key_forward",
    )(place, kv, rate, w_gate, w_up, w_down)
    own, other = pair(part, sent)
    grad_q, part, sent = pl.pallas_call(
        functools.partial(query_kernel, scale),
        out_shape=[jax.ShapeDtypeStruct((pieces, rows, dim), BF16)] + sum_shapes,
        grid_spec=pltpu.PrefetchScalarGridSpec(
            num_scalar_prefetch=1,
            grid=grid,
            in_specs=[two_spec, w_spec, w_spec, w_spec, sum_spec, sum_spec],
            out_specs=[one_spec, sum_spec, sum_spec],
            scratch_shapes=[pltpu.VMEM((3, dim, dim), BF16)],
        ),
        compiler_params=params,
        name="query_side",
    )(place, qo, w_gate, w_up, w_down, own, other)
    own, other = pair(part, sent)
    grad_q = exchange(grad_q)
    grad_kv = pl.pallas_call(
        functools.partial(back_kernel, scale),
        out_shape=jax.ShapeDtypeStruct((pieces, 2, rows, dim), BF16),
        grid_spec=pltpu.PrefetchScalarGridSpec(
            num_scalar_prefetch=1,
            grid=grid,
            in_specs=[two_spec, rate_spec, w_spec, w_spec, w_spec, sum_spec, sum_spec],
            out_specs=two_spec,
            scratch_shapes=[pltpu.VMEM((3, dim, dim), BF16)],
        ),
        compiler_params=params,
        name="key_back",
    )(place, kv, rate, w_gate, w_up, w_down, own, other)
    grad_kv = exchange(grad_kv)

    def home(x):
        return x.transpose(1, 0, 2).reshape(rows, model)

    return home(grad_q), home(grad_kv[:, 0]), home(grad_kv[:, 1])


def solution(mesh):
    n_tok, n_head = mesh.shape["tok"], mesh.shape["head"]

    def run(queries, key_tokens, values, out_grad, learn_rates, w_gate, w_up, w_down):
        n_s = w_gate.shape[0] // n_head
        n_t = n_tok // n_s
        split = Mesh(mesh.devices.reshape(n_t, n_s, n_head), ("t", "s", "head"))
        tokens = P(("t", "s", "head"), None)
        weights = P("head", None, None)
        return jax.shard_map(
            functools.partial(body, n_t, n_s, n_head),
            mesh=split,
            in_specs=(tokens,) * 4 + (P(("t", "s"), "head"),) + (weights,) * 3,
            out_specs=(tokens,) * 3,
            check_vma=False,
        )(queries, key_tokens, values, out_grad, learn_rates, w_gate, w_up, w_down)

    return run
```

time: 453 us -> 282 us (0.62); the launches traced: 445 us -> 281 us
  waiting for transfers between devices: 237 us -> 163 us
  matrix products: 68 us -> 0 us
  local copies, waits for them, and re-layouts: 86.5 us -> 49.9 us
  Pallas kernels: 0 us -> 31.2 us
  between operations: 14.6 us -> 0.75 us
    psum x2 -> x0, waiting for transfers between devices: 167 us -> none  [the longest x1 93.6 us: body(): lax.psum((delta_gate, delta_up, delta_down), 'tok')]
    dot_general x23 -> x0, matrix products: 68 us -> none  [the longest x1 13.2 us: key_back(): jnp.dot(back_upper, up_mat.T, preferred_element_type=jnp.float32)]
    all_to_all x7 -> x5, waiting for transfers between devices: 70.4 us -> 130 us  [the longest x4 130 us: exchange(): return lax.all_to_all(x, spread, split_axis=0, concat_axis=0, tiled=True)]
    ppermute x0 -> x2, waiting for transfers between devices: none -> 33.1 us  [pair(): return (own, lax.ppermute(sent, 't', [(0, 1), (1, 0)]))]
    all_to_all x10 -> x1, local copies, waits for them, and re-layouts: 33.4 us -> 1.33 us  [body(): lax.all_to_all(learn_rates.T, 's', split_axis=0, concat_axis=0, tiled=True)]
    pallas_call x0 -> x3, Pallas kernels: none -> 31.2 us  [the longest x1 13.3 us: body(): pl.pallas_call(functools.partial(back_kernel, scale), out_shape=jax.Shape...]
    convert_element_type x4 -> x0, local copies, waits for them, and re-layouts: 14.8 us -> none  [the longest x2 6.15 us: key_back(): return (key_grad.astype(jnp.bfloat16), value_grad.astype(jnp.bfloat16))]
    transpose x0 -> x4, local copies, waits for them, and re-layouts: none -> 12.7 us  [home(): return x.transpose(1, 0, 2).reshape(rows, model)]
  transfers between devices with their start and end apart: 9 -> 7, of which waited for: 7 -> 4; matrix products, arithmetic and copies ran while one was open for 27% -> 14% of each run, Pallas kernels for 0% -> 8%
where the time goes in v1:
time: 282 us; the launch traced here: 281 us
  waiting for transfers between devices  163 us (58%)
  local copies, waits for them, and re-layouts  49.9 us (18%)
  Pallas kernels  31.2 us (11%)
  starting transfers between devices  27.2 us (10%)
  other arithmetic  9.19 us (3%)
    all_to_all x4, waiting for transfers between devices, exchange(): return lax.all_to_all(x, spread, split_axis=0, concat_axis=0, tiled=True)  130 us
    ppermute x2, waiting for transfers between devices, pair(): return (own, lax.ppermute(sent, 't', [(0, 1), (1, 0)]))  33.1 us
    unnamed x14, local copies, waits for them, and re-layouts  24.4 us
    all_to_all x4, starting transfers between devices, exchange(): return lax.all_to_all(x, spread, split_axis=0, concat_axis=0, tiled=True)  19 us
    pallas_call x1, Pallas kernels, body(): pl.pallas_call(functools.partial(back_kernel, scale), out_shape=jax.Shape...  13.3 us
    transpose x4, local copies, waits for them, and re-layouts, home(): return x.transpose(1, 0, 2).reshape(rows, model)  12.7 us
    reshape x4, local copies, waits for them, and re-layouts, by_head(): return x.reshape(rows, heads, dim).transpose(1, 0, 2)  9.51 us
    pallas_call x1, Pallas kernels, body(): pl.pallas_call(key_kernel, out_shape=sum_shapes, grid_spec=pltpu.Prefetch...  8.94 us
  transfers between devices with their start and end apart: 7, of which 4 were waited for; matrix products, arithmetic and copies ran while one was open for 14% of the time, Pallas kernels for 8%

profile of v1, /device:TPU:0, one launch (start us, length us, event | category | flops | bytes accessed | tf_op | source)
XLA Modules:
  0.0 281.3 jit_solution(15704421466789340812)
XLA Ops:
  0.6 1.3 all_to_all.20
  2.0 5.2 %all-to-all-start.2 = ((f32[4,1,1024]{2,1,0:T(1,128)}), f32[4,1,1024]{2,1,0:T(1,128)S(1)}, u32[]{:S(2)}, u32[]{:S(2)}) async-start(f32[4,1,1024]{2,1,0:T(1,128)} %all_to_all.20), calls=%async_computation.2 | async-start | bytes 32768 | tf_op jit(solution)/shard_map/all_to_all | solution.py:171
  7.2 3.3 %copy.32 = bf16[256,4096]{0,1:T(8,128)(2,1)S(1)} copy(bf16[256,4096]{1,0:T(8,128)(2,1)} %param.10) | data formatting | bytes 4194304 | tf_op args[2]
  10.5 2.4 copy.33
  12.9 3.3 %copy.30 = bf16[256,4096]{0,1:T(8,128)(2,1)S(1)} copy(bf16[256,4096]{1,0:T(8,128)(2,1)} %param.9) | data formatting | bytes 4194304 | tf_op args[1]
  16.1 2.4 copy.31
  18.5 4.6 %pad_maximum_fusion.1 = bf16[16,2,256,256]{3,2,1,0:T(8,128)(2,1)} fusion(bf16[16,1,256,256]{3,2,1,0:T(8,128)(2,1)} %bitcast.43, bf16[16,1,256,256]{3,2,1,0:T(8,128)(2,1)} %bitcast.45), kind=kLoop, calls=%fused_computation.1 | loop fusion | flops 2097152 | bytes 8388608 | tf_op jit(solution)/shard_map/stack | solution.py:170
  23.1 0.0 all-to-all-done.2
  23.1 5.3 %all-to-all-start.1 = ((bf16[16,2,256,256]{3,2,1,0:T(8,128)(2,1)}), bf16[16,2,256,256]{3,2,1,0:T(8,128)(2,1)}, u32[]{:S(2)}, u32[]{:S(2)}) async-start(bf16[16,2,256,256]{3,2,1,0:T(8,128)(2,1)} %pad_maximum_fusion.1), calls=%async_computation.1 | async-start | bytes 8388608 | tf_op jit(solution)/shard_map/all_to_all | solution.py:161
  28.4 3.3 %copy.28 = bf16[256,4096]{0,1:T(8,128)(2,1)S(1)} copy(bf16[256,4096]{1,0:T(8,128)(2,1)} %param.11) | data formatting | bytes 4194304 | tf_op args[3]
  31.7 2.4 copy.29
  34.1 3.3 %copy.26 = bf16[256,4096]{0,1:T(8,128)(2,1)S(1)} copy(bf16[256,4096]{1,0:T(8,128)(2,1)} %param.8) | data formatting | bytes 4194304 | tf_op args[0]
  37.4 2.4 copy.27
  39.7 4.6 %pad_maximum_fusion = bf16[16,2,256,256]{3,2,1,0:T(8,128)(2,1)} fusion(bf16[16,1,256,256]{3,2,1,0:T(8,128)(2,1)} %bitcast.44, bf16[16,1,256,256]{3,2,1,0:T(8,128)(2,1)} %bitcast.46), kind=kLoop, calls=%fused_computation | loop fusion | flops 2097152 | bytes 8388608 | tf_op jit(solution)/shard_map/stack | solution.py:174
  44.3 36.7 %all-to-all-done.1.kv_ref = bf16[16,2,256,256]{3,2,1,0:T(8,128)(2,1)} async-done(((bf16[16,2,256,256]{3,2,1,0:T(8,128)(2,1)}), bf16[16,2,256,256]{3,2,1,0:T(8,128)(2,1)}, u32[]{:S(2)}, u32[]{:S(2)}) %all-to-all-start.1) | async-done | bytes 4194336 | tf_op jit(solution)/shard_map/all_to_all | solution.py:161
  81.0 4.5 %all-to-all-start = ((bf16[16,2,256,256]{3,2,1,0:T(8,128)(2,1)}), bf16[16,2,256,256]{3,2,1,0:T(8,128)(2,1)}, u32[]{:S(2)}, u32[]{:S(2)}) async-start(bf16[16,2,256,256]{3,2,1,0:T(8,128)(2,1)} %pad_maximum_fusion), calls=%async_computation | async-start | bytes 8388608 | tf_op jit(solution)/shard_map/all_to_all | solution.py:161
  85.7 1.9 broadcast_in_dim.8.rate_ref
  87.6 8.9 %key_forward.1 = (f32[3,256,256]{2,1,0:T(8,128)}, bf16[3,256,256]{2,1,0:T(8,128)(2,1)}) custom-call(s32[1]{0:T(128)} %bitcast.s_ref, bf16[16,2,256,256]{3,2,1,0:T(8,128)(2,1)} %all-to-all-done.1.kv_ref, f32[4096,128]{1,0:T(8,128)} %broadcast_in_dim.8.rate_ref, bf16[4,256,256]{2,1,0:T(8,128)(2,1)} %wg_ref.5, bf16[4,256,256]{2,1,0:T(8,128)(2,1)} %wu_ref.5, ...), custom_call_target="tpu_custom_call" | custom-call | tf_op jit(solution)/shard_map/key_forward/pallas_call | solution.py:191
  96.5 2.6 collective-permute-start
  99.1 47.1 %all-to-all-done.qo_ref = bf16[16,2,256,256]{3,2,1,0:T(8,128)(2,1)} async-done(((bf16[16,2,256,256]{3,2,1,0:T(8,128)(2,1)}), bf16[16,2,256,256]{3,2,1,0:T(8,128)(2,1)}, u32[]{:S(2)}, u32[]{:S(2)}) %all-to-all-start) | async-done | bytes 4194336 | tf_op jit(solution)/shard_map/all_to_all | solution.py:161
  146.3 0.0 collective-permute-done.other_ref
  146.3 0.0 copy-start.1
  146.3 0.7 copy-done.1
  147.0 8.9 %query_side.1 = (bf16[16,256,256]{2,1,0:T(8,128)(2,1)}, f32[3,256,256]{2,1,0:T(8,128)}, bf16[3,256,256]{2,1,0:T(8,128)(2,1)}) custom-call(s32[1]{0:T(128)} %bitcast.s_ref, bf16[16,2,256,256]{3,2,1,0:T(8,128)(2,1)} %all-to-all-done.qo_ref, bf16[4,256,256]{2,1,0:T(8,128)(2,1)} %wg_ref.5, bf16[4,256,256]{2,1,0:T(8,128)(2,1)} %wu_ref.5, ...), custom_call_target="tpu_custom_call" | custom-call | tf_op jit(solution)/shard_map/query_side/pallas_call | solution.py:204
  155.9 0.0 copy-start.2
  155.9 4.6 %all-to-all-start.3 = ((bf16[16,256,256]{2,1,0:T(8,128)(2,1)}), bf16[16,256,256]{2,1,0:T(8,128)(2,1)S(1)}, u32[]{:S(2)}, u32[]{:S(2)}) async-start(bf16[16,256,256]{2,1,0:T(8,128)(2,1)} %get-tuple-element.10), calls=%async_computation.3 | async-start | bytes 4194304 | tf_op jit(solution)/shard_map/all_to_all | solution.py:161
  160.6 0.0 copy-done.2
  160.6 0.3 collective-permute-start.1
  160.9 33.1 %collective-permute-done.1.other_ref = bf16[3,256,256]{2,1,0:T(8,128)(2,1)S(1)} collective-permute-done((bf16[3,256,256]{2,1,0:T(8,128)(2,1)S(1)}, bf16[3,256,256]{2,1,0:T(8,128)(2,1)S(1)}, u32[]{:S(2)}, u32[]{:S(2)}) %collective-permute-start.1) | collective-permute-done | bytes 393248 | tf_op jit(solution)/shard_map/ppermute | solution.py:167
  194.0 0.0 copy-start
  194.0 0.7 copy-done
  194.8 13.3 %key_back.1 = bf16[16,2,256,256]{3,2,1,0:T(8,128)(2,1)} custom-call(s32[1]{0:T(128)} %bitcast.s_ref, bf16[16,2,256,256]{3,2,1,0:T(8,128)(2,1)} %all-to-all-done.1.kv_ref, f32[4096,128]{1,0:T(8,128)} %broadcast_in_dim.8.rate_ref, bf16[4,256,256]{2,1,0:T(8,128)(2,1)} %wg_ref.5, bf16[4,256,256]{2,1,0:T(8,128)(2,1)} %wu_ref.5, bf16[4,256,256]{2,1,0:T(8,128)(2,1)} %wd_ref.5, ...), custom_call_target="tpu_custom_call" | custom-call | tf_op jit(solution)/shard_map/key_back/pallas_call | solution.py:219
  208.1 0.0 all-to-all-done.3
  208.1 4.5 %all-to-all-start.4 = ((bf16[16,2,256,256]{3,2,1,0:T(8,128)(2,1)}), bf16[16,2,256,256]{3,2,1,0:T(8,128)(2,1)}, u32[]{:S(2)}, u32[]{:S(2)}) async-start(bf16[16,2,256,256]{3,2,1,0:T(8,128)(2,1)} %key_back.1), calls=%async_computation.4 | async-start | bytes 8388608 | tf_op jit(solution)/shard_map/all_to_all | solution.py:161
  212.6 2.4 copy.35
  215.0 4.1 %copy.38 = bf16[256,4096]{1,0:T(8,128)(2,1)} copy(bf16[256,4096]{0,1:T(8,128)(2,1)} %bitcast.36) | data formatting | bytes 4194304
  219.1 46.1 %all-to-all-done.4 = bf16[16,2,256,256]{3,2,1,0:T(8,128)(2,1)} async-done(((bf16[16,2,256,256]{3,2,1,0:T(8,128)(2,1)}), bf16[16,2,256,256]{3,2,1,0:T(8,128)(2,1)}, u32[]{:S(2)}, u32[]{:S(2)}) %all-to-all-start.4) | async-done | bytes 4194336 | tf_op jit(solution)/shard_map/all_to_all | solution.py:161
  265.2 4.7 %slice_bitcast_fusion = (bf16[256,16,256]{2,0,1:T(8,128)(2,1)}, bf16[256,16,256]{2,0,1:T(8,128)(2,1)}) fusion(bf16[16,2,256,256]{3,2,1,0:T(8,128)(2,1)} %all-to-all-done.4), kind=kLoop, calls=%fused_computation.2 | loop fusion | bytes 8388608 | tf_op jit(solution)/shard_map/transpose | solution.py:235
  269.8 2.8 %copy.36 = bf16[256,16,256]{0,2,1:T(8,128)(2,1)S(1)} copy(bf16[256,16,256]{2,0,1:T(8,128)(2,1)} %get-tuple-element.20) | data formatting | bytes 4194304 | tf_op jit(solution)/shard_map/transpose | solution.py:235
  272.7 2.9 %copy.39 = bf16[256,4096]{1,0:T(8,128)(2,1)} copy(bf16[256,4096]{0,1:T(8,128)(2,1)S(1)} %bitcast.37) | data formatting | bytes 4194304
  275.5 2.8 %copy.37 = bf16[256,16,256]{0,2,1:T(8,128)(2,1)S(1)} copy(bf16[256,16,256]{2,0,1:T(8,128)(2,1)} %get-tuple-element.19) | data formatting | bytes 4194304 | tf_op jit(solution)/shard_map/transpose | solution.py:235
  278.4 2.9 %copy.40 = bf16[256,4096]{1,0:T(8,128)(2,1)} copy(bf16[256,4096]{0,1:T(8,128)(2,1)S(1)} %bitcast.38) | data formatting | bytes 4194304
  (2 shorter events, 0.1 us)
Async XLA Ops:
  2.0 21.1 %all-to-all-start.2 = ((f32[4,1,1024]{2,1,0:T(1,128)}), f32[4,1,1024]{2,1,0:T(1,128)S(1)}, u32[]{:S(2)}, u32[]{:S(2)}) async-start(f32[4,1,1024]{2,1,0:T(1,128)} %all_to_all.20), calls=%async_computation.2 | async-start | bytes 32768 | tf_op jit(solution)/shard_map/all_to_all | solution.py:171
  23.1 57.9 %all-to-all-start.1 = ((bf16[16,2,256,256]{3,2,1,0:T(8,128)(2,1)}), bf16[16,2,256,256]{3,2,1,0:T(8,128)(2,1)}, u32[]{:S(2)}, u32[]{:S(2)}) async-start(bf16[16,2,256,256]{3,2,1,0:T(8,128)(2,1)} %pad_maximum_fusion.1), calls=%async_computation.1 | async-start | bytes 8388608 | tf_op jit(solution)/shard_map/all_to_all | solution.py:161
  81.0 65.2 %all-to-all-start = ((bf16[16,2,256,256]{3,2,1,0:T(8,128)(2,1)}), bf16[16,2,256,256]{3,2,1,0:T(8,128)(2,1)}, u32[]{:S(2)}, u32[]{:S(2)}) async-start(bf16[16,2,256,256]{3,2,1,0:T(8,128)(2,1)} %pad_maximum_fusion), calls=%async_computation | async-start | bytes 8388608 | tf_op jit(solution)/shard_map/all_to_all | solution.py:161
  96.5 49.7 %collective-permute-start = (bf16[3,256,256]{2,1,0:T(8,128)(2,1)}, bf16[3,256,256]{2,1,0:T(8,128)(2,1)S(1)}, u32[]{:S(2)}, u32[]{:S(2)}) collective-permute-start(bf16[3,256,256]{2,1,0:T(8,128)(2,1)} %get-tuple-element.9), channel_id=1, source_target_pairs={{0,16},{16,0},{1,17},{17,1},{2,18},{18,2},{3,19},{19,3},{4,20},{20... | collective-permute-start | bytes 1179656 | tf_op jit(solution)/shard_map/ppermute | solution.py:167
  146.3 0.7 copy-start.1
  155.9 4.6 %copy-start.2 = (bf16[3,256,256]{2,1,0:T(8,128)(2,1)S(1)}, bf16[3,256,256]{2,1,0:T(8,128)(2,1)}, u32[]{:S(2)}) copy-start(bf16[3,256,256]{2,1,0:T(8,128)(2,1)} %get-tuple-element.12) | copy-start | bytes 1179652
  155.9 52.1 %all-to-all-start.3 = ((bf16[16,256,256]{2,1,0:T(8,128)(2,1)}), bf16[16,256,256]{2,1,0:T(8,128)(2,1)S(1)}, u32[]{:S(2)}, u32[]{:S(2)}) async-start(bf16[16,256,256]{2,1,0:T(8,128)(2,1)} %get-tuple-element.10), calls=%async_computation.3 | async-start | bytes 4194304 | tf_op jit(solution)/shard_map/all_to_all | solution.py:161
  160.6 33.5 %collective-permute-start.1 = (bf16[3,256,256]{2,1,0:T(8,128)(2,1)S(1)}, bf16[3,256,256]{2,1,0:T(8,128)(2,1)S(1)}, u32[]{:S(2)}, u32[]{:S(2)}) collective-permute-start(bf16[3,256,256]{2,1,0:T(8,128)(2,1)S(1)} %copy-done.2), channel_id=1, source_target_pairs={{0,16},{16,0},{1,17},{17,1},{2,18},{18,2},{3,19},{19,3},{4,20},{20... | collective-permute-start | bytes 1179656 | tf_op jit(solution)/shard_map/ppermute | solution.py:167
  194.0 0.7 copy-start
  208.1 57.1 %all-to-all-start.4 = ((bf16[16,2,256,256]{3,2,1,0:T(8,128)(2,1)}), bf16[16,2,256,256]{3,2,1,0:T(8,128)(2,1)}, u32[]{:S(2)}, u32[]{:S(2)}) async-start(bf16[16,2,256,256]{3,2,1,0:T(8,128)(2,1)} %key_back.1), calls=%async_computation.4 | async-start | bytes 8388608 | tf_op jit(solution)/shard_map/all_to_all | solution.py:161

commit v2 on v1

--- a/solution.py
+++ b/solution.py
@@ -8,6 +8,7 @@
 from jax.experimental.pallas import tpu as pltpu
 from jax.sharding import Mesh, PartitionSpec as P
 
+
 F32 = jnp.float32
 BF16 = jnp.bfloat16
 
@@ -24,8 +25,42 @@
     return lax.dot_general(a, b, (((0,), (0,)), ((), ())), preferred_element_type=F32)
 
 
-def wide(rate, columns):
-    return jnp.concatenate([rate] * (columns // rate.shape[1]), axis=1)
+def swap_out_kernel(first_ref, second_ref, out_ref):
+    dim = out_ref.shape[-1]
+    for h in range(out_ref.shape[0]):
+        out_ref[h, 0] = first_ref[:, h * dim : (h + 1) * dim]
+        out_ref[h, 1] = second_ref[:, h * dim : (h + 1) * dim]
+
+
+def home_two_kernel(in_ref, first_ref, second_ref):
+    dim = in_ref.shape[-1]
+    for h in range(in_ref.shape[0]):
+        first_ref[:, h * dim : (h + 1) * dim] = in_ref[h, 0]
+        second_ref[:, h * dim : (h + 1) * dim] = in_ref[h, 1]
+
+
+def home_one_kernel(in_ref, out_ref):
+    dim = in_ref.shape[-1]
+    for h in range(in_ref.shape[0]):
+        out_ref[:, h * dim : (h + 1) * dim] = in_ref[h]
+
+
+def spread_rates(s_ref, rates, n_s, per, dim):
+    n_head = rates.shape[0] // n_s
+    columns = []
+    for j in range(per):
+        piece = pl.program_id(0) * per + j
+        back = lax.rem(s_ref[0] - lax.rem(piece, n_s) + n_s, n_s)
+        row = rates[pl.ds(back * n_head + piece // n_s, 1), :]
+        columns.append(jnp.broadcast_to(row, (128, row.shape[1])).T)
+    tall = jnp.concatenate(columns, axis=0)
+    return jnp.concatenate([tall] * (dim // 128), axis=1)
+
+
+def pack_rates_kernel(*refs):
+    n_head = refs[0].shape[0]
+    for j, ref in enumerate(refs[:-1]):
+        refs[-1][j * n_head : (j + 1) * n_head, :] = ref[...]
 
 
 def rows_of(ref, which):
@@ -37,11 +72,16 @@
     ref[:, which] = value.reshape(ref.shape[0], ref.shape[2], ref.shape[3])
 
 
-def key_kernel(s_ref, kv_ref, rate_ref, wg_ref, wu_ref, wd_ref, part_ref, sent_ref):
+def key_kernel(n_s, s_ref, kv_ref, rate_ref, wg_ref, wu_ref, wd_ref, part_ref, sent_ref):
     step = pl.program_id(0)
-    width = kv_ref.shape[-1]
+
+    @pl.when(step == 0)
+    def _():
+        part_ref[...] = jnp.zeros_like(part_ref)
+
+    rate = spread_rates(s_ref, rate_ref, n_s, kv_ref.shape[0], kv_ref.shape[-1])
     k = rows_of(kv_ref, 0)
-    scaled = (wide(rate_ref[...], width) * rows_of(kv_ref, 1).astype(F32)).astype(BF16)
+    scaled = (rate * rows_of(kv_ref, 1).astype(F32)).astype(BF16)
     gate = mm(k, wg_ref[0])
     up = mm(k, wu_ref[0])
     dhid = mm_nt(scaled, wd_ref[0])
@@ -50,11 +90,6 @@
     hidden = (act * up).astype(BF16)
     dgate = (dhid * up * (sig * (1.0 + gate * (1.0 - sig)))).astype(BF16)
     dup = (dhid * act).astype(BF16)
-
-    @pl.when(step == 0)
-    def _():
-        part_ref[...] = jnp.zeros_like(part_ref)
-
     part_ref[0] += mm_tn(k, dgate)
     part_ref[1] += mm_tn(k, dup)
     part_ref[2] += mm_tn(hidden, scaled)
@@ -98,7 +133,7 @@
 
 
 def back_kernel(
-    scale, s_ref, kv_ref, rate_ref, wg_ref, wu_ref, wd_ref, own_ref, other_ref, gkv_ref, adj
+    scale, n_s, s_ref, kv_ref, rate_ref, wg_ref, wu_ref, wd_ref, own_ref, other_ref, gkv_ref, adj
 ):
     step = pl.program_id(0)
 
@@ -106,9 +141,8 @@
     def _():
         adj[...] = (scale * (own_ref[...] + other_ref[...].astype(F32))).astype(BF16)
 
-    width = kv_ref.shape[-1]
+    rate = spread_rates(s_ref, rate_ref, n_s, kv_ref.shape[0], kv_ref.shape[-1])
     k = rows_of(kv_ref, 0)
-    rate = wide(rate_ref[...], width)
     scaled = (rate * rows_of(kv_ref, 1).astype(F32)).astype(BF16)
     gate = mm(k, wg_ref[0])
     up = mm(k, wu_ref[0])
@@ -154,8 +188,20 @@
     place = lax.axis_index("s").astype(jnp.int32).reshape(1)
     scale = 1.0 / math.sqrt(dim * rows * pieces * n_t)
 
-    def by_head(x):
-        return x.reshape(rows, heads, dim).transpose(1, 0, 2)
+    block = min(rows, 128)
+    copy_grid = (rows // block,)
+    flat_spec = pl.BlockSpec((block, model), lambda i: (i, 0))
+    pair_spec = pl.BlockSpec((heads, 2, block, dim), lambda i: (0, 0, i, 0))
+
+    def by_head(first, second):
+        return pl.pallas_call(
+            swap_out_kernel,
+            out_shape=jax.ShapeDtypeStruct((heads, 2, rows, dim), BF16),
+            grid=copy_grid,
+            in_specs=[flat_spec, flat_spec],
+            out_specs=pair_spec,
+            name="by_head",
+        )(first, second)
 
     def exchange(x):
         return lax.all_to_all(x, spread, split_axis=0, concat_axis=0, tiled=True)
@@ -167,17 +213,26 @@
             return own, lax.ppermute(sent, "t", [(0, 1), (1, 0)])
         return jnp.zeros_like(own), lax.psum(sent, "t")
 
-    kv = exchange(jnp.stack([by_head(key_tokens), by_head(values)], axis=1))
-    rate = lax.all_to_all(learn_rates.T, "s", split_axis=0, concat_axis=0, tiled=True)
-    rate = rate.reshape(n_s, n_head, rows).transpose(1, 0, 2).reshape(pieces * rows, 1)
-    rate = jnp.broadcast_to(rate, (pieces * rows, min(128, dim)))
-    qo = exchange(jnp.stack([by_head(queries), by_head(out_grad)], axis=1))
+    kv = exchange(by_head(key_tokens, values))
+    by_column = learn_rates.T.reshape(n_s, n_head, rows)
+    rates = []
+    for j in range(n_s):
+        piece = by_column[lax.rem(lax.axis_index("s") + j, n_s)]
+        if j:
+            piece = lax.ppermute(piece, "s", [(i, (i + j) % n_s) for i in range(n_s)])
+        rates.append(piece)
+    rate = pl.pallas_call(
+        pack_rates_kernel,
+        out_shape=jax.ShapeDtypeStruct((n_s * n_head, rows), F32),
+        name="rate_pack",
+    )(*rates)
+    qo = exchange(by_head(queries, out_grad))
 
     per = blocks_per_step(pieces, rows, 1024)
     grid = (pieces // per,)
     two_spec = pl.BlockSpec((per, 2, rows, dim), lambda i, s: (i, 0, 0, 0))
     one_spec = pl.BlockSpec((per, rows, dim), lambda i, s: (i, 0, 0))
-    rate_spec = pl.BlockSpec((per * rows, rate.shape[1]), lambda i, s: (i, 0))
+    rate_spec = pl.BlockSpec((n_s * n_head, rows), lambda i, s: (0, 0))
     w_spec = pl.BlockSpec((1, dim, dim), lambda i, s: (s[0], 0, 0))
     sum_spec = pl.BlockSpec((3, dim, dim), lambda i, s: (0, 0, 0))
     sum_shapes = [
@@ -189,7 +244,7 @@
     )
 
     part, sent = pl.pallas_call(
-        key_kernel,
+        functools.partial(key_kernel, n_s),
         out_shape=sum_shapes,
         grid_spec=pltpu.PrefetchScalarGridSpec(
             num_scalar_prefetch=1,
@@ -217,7 +272,7 @@
     own, other = pair(part, sent)
     grad_q = exchange(grad_q)
     grad_kv = pl.pallas_call(
-        functools.partial(back_kernel, scale),
+        functools.partial(back_kernel, scale, n_s),
         out_shape=jax.ShapeDtypeStruct((pieces, 2, rows, dim), BF16),
         grid_spec=pltpu.PrefetchScalarGridSpec(
             num_scalar_prefetch=1,
@@ -230,11 +285,23 @@
         name="key_back",
     )(place, kv, rate, w_gate, w_up, w_down, own, other)
     grad_kv = exchange(grad_kv)
-
-    def home(x):
-        return x.transpose(1, 0, 2).reshape(rows, model)
-
-    return home(grad_q), home(grad_kv[:, 0]), home(grad_kv[:, 1])
+    grad_q = pl.pallas_call(
+        home_one_kernel,
+        out_shape=jax.ShapeDtypeStruct((rows, model), BF16),
+        grid=copy_grid,
+        in_specs=[pl.BlockSpec((heads, block, dim), lambda i: (0, i, 0))],
+        out_specs=flat_spec,
+        name="home_q",
+    )(grad_q)
+    grad_k, grad_v = pl.pallas_call(
+        home_two_kernel,
+        out_shape=[jax.ShapeDtypeStruct((rows, model), BF16)] * 2,
+        grid=copy_grid,
+        in_specs=[pair_spec],
+        out_specs=[flat_spec, flat_spec],
+        name="home_kv",
+    )(grad_kv)
+    return grad_q, grad_k, grad_v
 
 
 def solution(mesh):

time: 282 us -> 276 us (0.979)
  local copies, waits for them, and re-layouts: 49.9 us -> 4.06 us
  waiting for transfers between devices: 163 us -> 195 us
  Pallas kernels: 31.2 us -> 45.5 us
  other arithmetic: 9.19 us -> 0 us
  starting transfers between devices: 27.2 us -> 30.2 us
    ppermute x0 -> x3, waiting for transfers between devices: none -> 48.3 us  [body(): piece = lax.ppermute(piece, 's', [(i, (i + j) % n_s) for i in range(n_s)])]
    all_to_all x4, waiting for transfers between devices: 130 us -> 98.9 us  [exchange(): return lax.all_to_all(x, spread, split_axis=0, concat_axis=0, tiled=True)]
    unnamed x14 -> x16, local copies, waits for them, and re-layouts: 24.4 us -> 3.44 us
    ppermute x2, waiting for transfers between devices: 33.1 us -> 48.4 us  [pair(): return (own, lax.ppermute(sent, 't', [(0, 1), (1, 0)]))]
    pallas_call x2 -> x7, Pallas kernels: 22.2 us -> 36.5 us  [the longest x1 13.3 us: body(): pl.pallas_call(functools.partial(back_kernel, scale, n_s), out_shape=jax....]
    transpose x4 -> x0, local copies, waits for them, and re-layouts: 12.7 us -> none  [home(): return x.transpose(1, 0, 2).reshape(rows, model)]
    reshape x4 -> x1, local copies, waits for them, and re-layouts: 9.51 us -> 0.02 us  [body(): by_column = learn_rates.T.reshape(n_s, n_head, rows)]
    another operation x2 -> x0, other arithmetic: 9.14 us -> none  [the longest x1 4.57 us: body(): kv = exchange(jnp.stack([by_head(key_tokens), by_head(values)], axis=1))]
  transfers between devices with their start and end apart: 7 -> 9, of which waited for: 4 -> 5; matrix products, arithmetic and copies ran while one was open for 14% -> 0% of each run, Pallas kernels for 8% -> 10%
where the time goes in v2:
time: 276 us
  waiting for transfers between devices  195 us (71%)
  Pallas kernels  45.5 us (16%)
  starting transfers between devices  30.2 us (11%)
  local copies, waits for them, and re-layouts  4.06 us (1%)
    all_to_all x4, waiting for transfers between devices, exchange(): return lax.all_to_all(x, spread, split_axis=0, concat_axis=0, tiled=True)  98.9 us
    ppermute x2, waiting for transfers between devices, pair(): return (own, lax.ppermute(sent, 't', [(0, 1), (1, 0)]))  48.4 us
    ppermute x3, waiting for transfers between devices, body(): piece = lax.ppermute(piece, 's', [(i, (i + j) % n_s) for i in range(n_s)])  48.3 us
    all_to_all x4, starting transfers between devices, exchange(): return lax.all_to_all(x, spread, split_axis=0, concat_axis=0, tiled=True)  21.5 us
    pallas_call x1, Pallas kernels, body(): pl.pallas_call(functools.partial(back_kernel, scale, n_s), out_shape=jax....  13.3 us
    pallas_call x1, Pallas kernels, body(): pl.pallas_call(functools.partial(query_kernel, scale), out_shape=[jax.Sha...  8.96 us
    pallas_call x1, Pallas kernels, body(): pl.pallas_call(functools.partial(key_kernel, n_s), out_shape=sum_shapes,...  7.91 us
    pallas_call x2, Pallas kernels, by_head(): pl.pallas_call(swap_out_kernel, out_shape=jax.ShapeDtypeStruct((heads, 2,...  7.49 us
  transfers between devices with their start and end apart: 9, of which 5 were waited for; matrix products, arithmetic and copies ran while one was open for 0% of the time, Pallas kernels for 10%

profile of v2, /device:TPU:0, one launch (start us, length us, event | category | flops | bytes accessed | tf_op | source)
XLA Modules:
  0.0 276.0 jit_solution(654019573660919291)
XLA Ops:
  0.6 3.8 %by_head.3 = bf16[16,2,256,256]{3,2,1,0:T(8,128)(2,1)} custom-call(bf16[256,4096]{1,0:T(8,128)(2,1)} %first_ref.3, bf16[256,4096]{1,0:T(8,128)(2,1)} %second_ref.3), custom_call_target="tpu_custom_call" | custom-call | tf_op jit(solution)/shard_map/by_head/pallas_call | solution.py:197
  4.4 6.4 %all-to-all-start.1 = ((bf16[16,2,256,256]{3,2,1,0:T(8,128)(2,1)}), bf16[16,2,256,256]{3,2,1,0:T(8,128)(2,1)}, u32[]{:S(2)}, u32[]{:S(2)}) async-start(bf16[16,2,256,256]{3,2,1,0:T(8,128)(2,1)} %by_head.3), calls=%async_computation.1 | async-start | bytes 8388608 | tf_op jit(solution)/shard_map/all_to_all | solution.py:207
  10.8 3.7 %by_head.2 = bf16[16,2,256,256]{3,2,1,0:T(8,128)(2,1)} custom-call(bf16[256,4096]{1,0:T(8,128)(2,1)} %first_ref.2, bf16[256,4096]{1,0:T(8,128)(2,1)} %second_ref.2), custom_call_target="tpu_custom_call" | custom-call | tf_op jit(solution)/shard_map/by_head/pallas_call | solution.py:197
  14.5 0.0 copy-start.3
  14.5 48.9 %all-to-all-done.1.kv_ref = bf16[16,2,256,256]{3,2,1,0:T(8,128)(2,1)} async-done(((bf16[16,2,256,256]{3,2,1,0:T(8,128)(2,1)}), bf16[16,2,256,256]{3,2,1,0:T(8,128)(2,1)}, u32[]{:S(2)}, u32[]{:S(2)}) %all-to-all-start.1) | async-done | bytes 4194336 | tf_op jit(solution)/shard_map/all_to_all | solution.py:207
  63.4 4.6 %all-to-all-start = ((bf16[16,2,256,256]{3,2,1,0:T(8,128)(2,1)}), bf16[16,2,256,256]{3,2,1,0:T(8,128)(2,1)}, u32[]{:S(2)}, u32[]{:S(2)}) async-start(bf16[16,2,256,256]{3,2,1,0:T(8,128)(2,1)} %by_head.2), calls=%async_computation | async-start | bytes 8388608 | tf_op jit(solution)/shard_map/all_to_all | solution.py:207
  68.0 0.0 copy-done.3
  68.0 0.6 dynamic-slice_bitcast_fusion
  68.7 2.6 collective-permute-start.2
  71.3 0.5 collective-permute-start.1
  71.8 0.6 collective-permute-start
  72.4 48.2 %collective-permute-done.2.refs_3_ = f32[4,256]{1,0:T(4,128)S(1)} collective-permute-done((f32[4,256]{1,0:T(4,128)S(1)}, f32[4,256]{1,0:T(4,128)S(1)}, u32[]{:S(2)}, u32[]{:S(2)}) %collective-permute-start.2) | collective-permute-done | bytes 4128 | tf_op jit(solution)/shard_map/ppermute | solution.py:222
  120.7 0.0 copy-start.4
  120.7 0.0 collective-permute-done.1.refs_2_
  120.7 0.0 copy-start.5
  120.7 0.0 collective-permute-done.refs_1_
  120.7 0.0 copy-start.6
  120.7 0.6 copy-done.4
  121.2 0.0 copy-done.5
  121.3 0.0 copy-done.6
  121.3 1.3 rate_pack.1.rate_ref
  122.6 7.9 %key_forward.1 = (f32[3,256,256]{2,1,0:T(8,128)}, bf16[3,256,256]{2,1,0:T(8,128)(2,1)}) custom-call(s32[1]{0:T(128)} %bitcast.s_ref, bf16[16,2,256,256]{3,2,1,0:T(8,128)(2,1)} %all-to-all-done.1.kv_ref, f32[16,256]{1,0:T(8,128)} %rate_pack.1.rate_ref, bf16[4,256,256]{2,1,0:T(8,128)(2,1)} %wg_ref.5, bf16[4,256,256]{2,1,0:T(8,128)(2,1)} %wu_ref.5, ...), custom_call_target="tpu_custom_call" | custom-call | tf_op jit(solution)/shard_map/key_forward/pallas_call | solution.py:246
  130.5 2.6 collective-permute-start.3
  133.1 0.0 all-to-all-done.qo_ref
  133.1 17.6 %collective-permute-done.3.other_ref = bf16[3,256,256]{2,1,0:T(8,128)(2,1)S(1)} collective-permute-done((bf16[3,256,256]{2,1,0:T(8,128)(2,1)}, bf16[3,256,256]{2,1,0:T(8,128)(2,1)S(1)}, u32[]{:S(2)}, u32[]{:S(2)}) %collective-permute-start.3) | collective-permute-done | bytes 393248 | tf_op jit(solution)/shard_map/ppermute | solution.py:213
  150.7 0.0 copy-start.2
  150.7 0.8 copy-done.2
  151.4 9.0 %query_side.1 = (bf16[16,256,256]{2,1,0:T(8,128)(2,1)}, f32[3,256,256]{2,1,0:T(8,128)}, bf16[3,256,256]{2,1,0:T(8,128)(2,1)}) custom-call(s32[1]{0:T(128)} %bitcast.s_ref, bf16[16,2,256,256]{3,2,1,0:T(8,128)(2,1)} %all-to-all-done.qo_ref, bf16[4,256,256]{2,1,0:T(8,128)(2,1)} %wg_ref.5, bf16[4,256,256]{2,1,0:T(8,128)(2,1)} %wu_ref.5, ...), custom_call_target="tpu_custom_call" | custom-call | tf_op jit(solution)/shard_map/query_side/pallas_call | solution.py:259
  160.4 0.0 copy-start.7
  160.4 3.9 %all-to-all-start.2 = ((bf16[16,256,256]{2,1,0:T(8,128)(2,1)}), bf16[16,256,256]{2,1,0:T(8,128)(2,1)S(1)}, u32[]{:S(2)}, u32[]{:S(2)}) async-start(bf16[16,256,256]{2,1,0:T(8,128)(2,1)} %get-tuple-element.12), calls=%async_computation.2 | async-start | bytes 4194304 | tf_op jit(solution)/shard_map/all_to_all | solution.py:207
  164.3 0.0 copy-done.7
  164.3 2.4 collective-permute-start.4
  166.7 30.8 %collective-permute-done.4.other_ref = bf16[3,256,256]{2,1,0:T(8,128)(2,1)S(1)} collective-permute-done((bf16[3,256,256]{2,1,0:T(8,128)(2,1)S(1)}, bf16[3,256,256]{2,1,0:T(8,128)(2,1)S(1)}, u32[]{:S(2)}, u32[]{:S(2)}) %collective-permute-start.4) | collective-permute-done | bytes 393248 | tf_op jit(solution)/shard_map/ppermute | solution.py:213
  197.5 0.0 copy-start.1
  197.5 0.7 copy-done.1
  198.2 13.3 %key_back.1 = bf16[16,2,256,256]{3,2,1,0:T(8,128)(2,1)} custom-call(s32[1]{0:T(128)} %bitcast.s_ref, bf16[16,2,256,256]{3,2,1,0:T(8,128)(2,1)} %all-to-all-done.1.kv_ref, f32[16,256]{1,0:T(8,128)} %rate_pack.1.rate_ref, bf16[4,256,256]{2,1,0:T(8,128)(2,1)} %wg_ref.5, bf16[4,256,256]{2,1,0:T(8,128)(2,1)} %wu_ref.5, bf16[4,256,256]{2,1,0:T(8,128)(2,1)} %wd_ref.5, ...), custom_call_target="tpu_custom_call" | custom-call | tf_op jit(solution)/shard_map/key_back/pallas_call | solution.py:274
  211.5 0.0 all-to-all-done.2.in_ref
  211.5 0.0 copy-start
  211.5 1.3 copy-done
  212.8 6.7 %all-to-all-start.3 = ((bf16[16,2,256,256]{3,2,1,0:T(8,128)(2,1)}), bf16[16,2,256,256]{3,2,1,0:T(8,128)(2,1)}, u32[]{:S(2)}, u32[]{:S(2)}) async-start(bf16[16,2,256,256]{3,2,1,0:T(8,128)(2,1)} %key_back.1), calls=%async_computation.3 | async-start | bytes 8388608 | tf_op jit(solution)/shard_map/all_to_all | solution.py:207
  219.5 2.7 home_q.1
  222.1 50.0 %all-to-all-done.3.in_ref = bf16[16,2,256,256]{3,2,1,0:T(8,128)(2,1)} async-done(((bf16[16,2,256,256]{3,2,1,0:T(8,128)(2,1)}), bf16[16,2,256,256]{3,2,1,0:T(8,128)(2,1)}, u32[]{:S(2)}, u32[]{:S(2)}) %all-to-all-start.3) | async-done | bytes 4194336 | tf_op jit(solution)/shard_map/all_to_all | solution.py:207
  272.1 3.9 %home_kv.1 = (bf16[256,4096]{1,0:T(8,128)(2,1)}, bf16[256,4096]{1,0:T(8,128)(2,1)}) custom-call(bf16[16,2,256,256]{3,2,1,0:T(8,128)(2,1)} %all-to-all-done.3.in_ref), custom_call_target="tpu_custom_call" | custom-call | tf_op jit(solution)/shard_map/home_kv/pallas_call | solution.py:296
  (1 shorter events, 0.0 us)
Async XLA Ops:
  4.4 59.0 %all-to-all-start.1 = ((bf16[16,2,256,256]{3,2,1,0:T(8,128)(2,1)}), bf16[16,2,256,256]{3,2,1,0:T(8,128)(2,1)}, u32[]{:S(2)}, u32[]{:S(2)}) async-start(bf16[16,2,256,256]{3,2,1,0:T(8,128)(2,1)} %by_head.3), calls=%async_computation.1 | async-start | bytes 8388608 | tf_op jit(solution)/shard_map/all_to_all | solution.py:207
  14.5 53.5 %copy-start.3 = (f32[1024,4]{0,1:T(4,128)S(1)}, f32[1024,4]{0,1:T(4,128)}, u32[]{:S(2)}) copy-start(f32[1024,4]{0,1:T(4,128)} %param.12) | copy-start | bytes 49156
  63.4 69.7 %all-to-all-start = ((bf16[16,2,256,256]{3,2,1,0:T(8,128)(2,1)}), bf16[16,2,256,256]{3,2,1,0:T(8,128)(2,1)}, u32[]{:S(2)}, u32[]{:S(2)}) async-start(bf16[16,2,256,256]{3,2,1,0:T(8,128)(2,1)} %by_head.2), calls=%async_computation | async-start | bytes 8388608 | tf_op jit(solution)/shard_map/all_to_all | solution.py:207
  68.7 52.0 %collective-permute-start.2 = (f32[4,256]{1,0:T(4,128)S(1)}, f32[4,256]{1,0:T(4,128)S(1)}, u32[]{:S(2)}, u32[]{:S(2)}) collective-permute-start(f32[4,256]{1,0:T(4,128)S(1)} %get-tuple-element.17), channel_id=1, source_target_pairs={{0,12},{4,0},{8,4},{12,8},{1,13},{5,1},{9,5},{13,9},{2,14},{6,2},{... | collective-permute-start | bytes 12296 | tf_op jit(solution)/shard_map/ppermute | solution.py:222
  71.3 49.4 %collective-permute-start.1 = (f32[4,256]{1,0:T(4,128)S(1)}, f32[4,256]{1,0:T(4,128)S(1)}, u32[]{:S(2)}, u32[]{:S(2)}) collective-permute-start(f32[4,256]{1,0:T(4,128)S(1)} %get-tuple-element.18), channel_id=1, source_target_pairs={{0,8},{4,12},{8,0},{12,4},{1,9},{5,13},{9,1},{13,5},{2,10},{6,14},... | collective-permute-start | bytes 12296 | tf_op jit(solution)/shard_map/ppermute | solution.py:222
  71.8 48.8 %collective-permute-start = (f32[4,256]{1,0:T(4,128)S(1)}, f32[4,256]{1,0:T(4,128)S(1)}, u32[]{:S(2)}, u32[]{:S(2)}) collective-permute-start(f32[4,256]{1,0:T(4,128)S(1)} %get-tuple-element.19), channel_id=1, source_target_pairs={{0,4},{4,8},{8,12},{12,0},{1,5},{5,9},{9,13},{13,1},{2,6},{6,10},{... | collective-permute-start | bytes 12296 | tf_op jit(solution)/shard_map/ppermute | solution.py:222
  120.7 0.6 copy-start.4
  120.7 0.6 copy-start.5
  120.7 0.6 copy-start.6
  130.5 20.2 %collective-permute-start.3 = (bf16[3,256,256]{2,1,0:T(8,128)(2,1)}, bf16[3,256,256]{2,1,0:T(8,128)(2,1)S(1)}, u32[]{:S(2)}, u32[]{:S(2)}) collective-permute-start(bf16[3,256,256]{2,1,0:T(8,128)(2,1)} %get-tuple-element.11), channel_id=1, source_target_pairs={{0,16},{16,0},{1,17},{17,1},{2,18},{18,2},{3,19},{19,3},{4,20},{20... | collective-permute-start | bytes 1179656 | tf_op jit(solution)/shard_map/ppermute | solution.py:213
  150.7 0.8 copy-start.2
  160.4 3.9 %copy-start.7 = (bf16[3,256,256]{2,1,0:T(8,128)(2,1)S(1)}, bf16[3,256,256]{2,1,0:T(8,128)(2,1)}, u32[]{:S(2)}) copy-start(bf16[3,256,256]{2,1,0:T(8,128)(2,1)} %get-tuple-element.14) | copy-start | bytes 1179652
  160.4 51.1 %all-to-all-start.2 = ((bf16[16,256,256]{2,1,0:T(8,128)(2,1)}), bf16[16,256,256]{2,1,0:T(8,128)(2,1)S(1)}, u32[]{:S(2)}, u32[]{:S(2)}) async-start(bf16[16,256,256]{2,1,0:T(8,128)(2,1)} %get-tuple-element.12), calls=%async_computation.2 | async-start | bytes 4194304 | tf_op jit(solution)/shard_map/all_to_all | solution.py:207
  164.3 33.2 %collective-permute-start.4 = (bf16[3,256,256]{2,1,0:T(8,128)(2,1)S(1)}, bf16[3,256,256]{2,1,0:T(8,128)(2,1)S(1)}, u32[]{:S(2)}, u32[]{:S(2)}) collective-permute-start(bf16[3,256,256]{2,1,0:T(8,128)(2,1)S(1)} %copy-done.7), channel_id=1, source_target_pairs={{0,16},{16,0},{1,17},{17,1},{2,18},{18,2},{3,19},{19,3},{4,20},{20... | collective-permute-start | bytes 1179656 | tf_op jit(solution)/shard_map/ppermute | solution.py:213
  197.5 0.7 copy-start.1
  211.5 1.3 copy-start
  212.8 59.3 %all-to-all-start.3 = ((bf16[16,2,256,256]{3,2,1,0:T(8,128)(2,1)}), bf16[16,2,256,256]{3,2,1,0:T(8,128)(2,1)}, u32[]{:S(2)}, u32[]{:S(2)}) async-start(bf16[16,2,256,256]{3,2,1,0:T(8,128)(2,1)} %key_back.1), calls=%async_computation.3 | async-start | bytes 8388608 | tf_op jit(solution)/shard_map/all_to_all | solution.py:207

commit v3 on v1

v3 whole, which is shorter than its diff:
```python
import functools
import math

import jax
import jax.numpy as jnp
from jax import lax
from jax.experimental import pallas as pl
from jax.experimental.pallas import tpu as pltpu
from jax.sharding import Mesh, PartitionSpec as P


F32 = jnp.float32
BF16 = jnp.bfloat16
HEADS_HELD = 2


def mm(a, b):
    return lax.dot_general(a, b, (((1,), (0,)), ((), ())), preferred_element_type=F32)


def mm_nt(a, b):
    return lax.dot_general(a, b, (((1,), (1,)), ((), ())), preferred_element_type=F32)


def mm_tn(a, b):
    return lax.dot_general(a, b, (((0,), (0,)), ((), ())), preferred_element_type=F32)


def sigmoid(x):
    return jax.nn.sigmoid(x)


def stack_kernel(at_ref, gate_ref, up_ref, down_ref, out_ref):
    dim = gate_ref.shape[-1]
    out_ref[0, :dim] = gate_ref[0]
    out_ref[0, dim : 2 * dim] = up_ref[0]
    out_ref[0, 2 * dim :] = down_ref[0]


def by_head_kernel(n_group, at_ref, *refs):
    for j in range(n_group):
        out_ref = refs[2 * n_group + j]
        out_ref[0] = refs[2 * j][...]
        out_ref[1] = refs[2 * j + 1][...]


def home_kernel(n_group, n_out, at_ref, *refs):
    outs = refs[-n_out:]
    dim = refs[0].shape[-1]
    for a in range(HEADS_HELD):
        for j in range(n_group):
            piece = refs[a * n_group + j]
            head = HEADS_HELD * jnp.bitwise_xor(at_ref[0], j) + a
            columns = pl.ds(pl.multiple_of(head * dim, dim), dim)
            if n_out == 1:
                outs[0][:, columns] = piece[...]
            else:
                for i, out in enumerate(outs):
                    out[:, columns] = piece[i]


def tall_rates(at_ref, rate_refs, n_group, dim):
    n_s = len(rate_refs)
    head = at_ref[0] // n_s
    columns = []
    for j in range(n_group):
        ref = rate_refs[j % n_s]
        row = ref[0, pl.ds(jnp.bitwise_xor(head, j // n_s), 1), :]
        columns.append(jnp.broadcast_to(row, (128, row.shape[1])).T)
    tall = jnp.concatenate(columns, axis=0)
    return jnp.concatenate([tall] * (dim // 128), axis=1)


def stacked(refs, which):
    return jnp.concatenate([ref[which] for ref in refs], axis=0)


def hand_out(at_ref, acc, own_ref, sent_refs):
    rows = own_ref.shape[0]
    n_chunk = len(sent_refs) + 1
    for j, ref in enumerate((own_ref,) + tuple(sent_refs)):
        start = jnp.bitwise_xor(at_ref[1], j) * rows if n_chunk > 1 else 0
        chunk = acc[pl.ds(pl.multiple_of(start, 16), rows), :]
        ref[...] = chunk.astype(ref.dtype)


def take_in(at_ref, chunk_refs, whole):
    rows = chunk_refs[0].shape[0]
    for j, ref in enumerate(chunk_refs):
        start = jnp.bitwise_xor(at_ref[1], j) * rows if len(chunk_refs) > 1 else 0
        whole[pl.ds(pl.multiple_of(start, 16), rows), :] = ref[...]


def key_kernel(n_group, n_s, n_chunk, at_ref, *refs):
    pieces, refs = refs[:n_group], refs[n_group:]
    rate_refs, refs = refs[:n_s], refs[n_s:]
    w_ref, refs = refs[0], refs[1:]
    own_ref, sent_refs, acc = refs[-n_chunk - 1], refs[-n_chunk:-1], refs[-1]
    step = pl.program_id(0)
    dim = pieces[0].shape[-1]

    @pl.when(step == 0)
    def _():
        acc[...] = jnp.zeros_like(acc)

    k = stacked(pieces, 0)
    rate = tall_rates(at_ref, rate_refs, n_group, dim)
    scaled = (rate * stacked(pieces, 1).astype(F32)).astype(BF16)
    gate = mm(k, w_ref[0, :dim])
    up = mm(k, w_ref[0, dim : 2 * dim])
    dhid = mm_nt(scaled, w_ref[0, 2 * dim :])
    sig = sigmoid(gate)
    act = gate * sig
    hidden = (act * up).astype(BF16)
    dgate = (dhid * up * (sig * (1.0 + gate * (1.0 - sig)))).astype(BF16)
    dup = (dhid * act).astype(BF16)
    acc[:dim] += mm_tn(k, dgate)
    acc[dim : 2 * dim] += mm_tn(k, dup)
    acc[2 * dim :] += mm_tn(hidden, scaled)

    @pl.when(step == pl.num_programs(0) - 1)
    def _():
        hand_out(at_ref, acc, own_ref, sent_refs)


def fresh_kernel(scale, n_chunk, at_ref, own_ref, *refs):
    total = own_ref[...]
    for ref in refs[: n_chunk - 1]:
        total = total + ref[...].astype(F32)
    w_ref, out_ref = refs[n_chunk - 1], refs[-1]
    out_ref[...] = (w_ref[0].astype(F32) + scale * total).astype(BF16)


def adjoint_kernel(scale, n_chunk, at_ref, own_ref, *refs):
    total = own_ref[...]
    for ref in refs[: n_chunk - 1]:
        total = total + ref[...].astype(F32)
    refs[-1][...] = (scale * total).astype(BF16)


def query_kernel(n_group, n_chunk, at_ref, *refs):
    pieces, refs = refs[:n_group], refs[n_group:]
    chunk_refs = refs[:n_chunk]
    acc, fresh = refs[-2:]
    refs = refs[:-2]
    own_ref, sent_refs = refs[-n_chunk], refs[len(refs) - n_chunk + 1 :]
    grads = refs[-n_chunk - n_group : -n_chunk]
    step = pl.program_id(0)
    dim = pieces[0].shape[-1]

    @pl.when(step == 0)
    def _():
        acc[...] = jnp.zeros_like(acc)
        take_in(at_ref, chunk_refs, fresh)

    q = stacked(pieces, 0)
    o = stacked(pieces, 1)
    w_gate, w_up, w_down = fresh[:dim], fresh[dim : 2 * dim], fresh[2 * dim :]
    gate = mm(q, w_gate)
    up = mm(q, w_up)
    dhid = mm_nt(o, w_down)
    sig = sigmoid(gate)
    act = gate * sig
    hidden = (act * up).astype(BF16)
    dgate = (dhid * up * (sig * (1.0 + gate * (1.0 - sig)))).astype(BF16)
    dup = (dhid * act).astype(BF16)
    grad = (mm_nt(dgate, w_gate) + mm_nt(dup, w_up)).astype(BF16)
    rows = grads[0].shape[0]
    for j, ref in enumerate(grads):
        ref[...] = grad[j * rows : (j + 1) * rows]
    acc[:dim] += mm_tn(q, dgate)
    acc[dim : 2 * dim] += mm_tn(q, dup)
    acc[2 * dim :] += mm_tn(hidden, o)

    @pl.when(step == pl.num_programs(0) - 1)
    def _():
        hand_out(at_ref, acc, own_ref, sent_refs)


def back_kernel(n_group, n_s, n_chunk, at_ref, *refs):
    pieces, refs = refs[:n_group], refs[n_group:]
    rate_refs, refs = refs[:n_s], refs[n_s:]
    w_ref, chunk_refs, adj = refs[0], refs[1 : n_chunk + 1], refs[-1]
    outs = refs[-n_group - 1 : -1]
    dim = pieces[0].shape[-1]

    @pl.when(pl.program_id(0) == 0)
    def _():
        take_in(at_ref, chunk_refs, adj)

    k = stacked(pieces, 0)
    rate = tall_rates(at_ref, rate_refs, n_group, dim)
    scaled = (rate * stacked(pieces, 1).astype(F32)).astype(BF16)
    w_gate, w_up, w_down = w_ref[0, :dim], w_ref[0, dim : 2 * dim], w_ref[0, 2 * dim :]
    adj_gate, adj_up, adj_down = adj[:dim], adj[dim : 2 * dim], adj[2 * dim :]
    gate = mm(k, w_gate)
    up = mm(k, w_up)
    dhid = mm_nt(scaled, w_down)
    sig = sigmoid(gate)
    act = gate * sig
    rest = 1.0 - sig
    slope = sig * (1.0 + gate * rest)
    curve = sig * rest * (2.0 + gate * (1.0 - 2.0 * sig))
    hidden = (act * up).astype(BF16)
    dgate = (dhid * up * slope).astype(BF16)
    dup = (dhid * act).astype(BF16)
    back_dgate = mm(k, adj_gate)
    back_dup = mm(k, adj_up)
    back_hidden = mm_nt(scaled, adj_down)
    back_scaled = mm(hidden, adj_down)
    back_dhid = (back_dgate * up * slope + back_dup * act).astype(BF16)
    back_gate = (
        back_dgate * dhid * up * curve + (back_dup * dhid + back_hidden * up) * slope
    ).astype(BF16)
    back_upper = (back_dgate * dhid * slope + back_hidden * act).astype(BF16)
    grad_k = mm_nt(dgate, adj_gate) + mm_nt(dup, adj_up)
    grad_k = (grad_k + mm_nt(back_gate, w_gate) + mm_nt(back_upper, w_up)).astype(BF16)
    grad_v = (rate * (back_scaled + mm(back_dhid, w_down))).astype(BF16)
    rows = outs[0].shape[1]
    for j, ref in enumerate(outs):
        ref[0] = grad_k[j * rows : (j + 1) * rows]
        ref[1] = grad_v[j * rows : (j + 1) * rows]


def body(n_t, n_s, n_head, queries, key_tokens, values, out_grad, learn_rates, w_gate, w_up, w_down):
    rows, model = queries.shape
    n_group = n_head * n_s
    dim = model // (n_group * HEADS_HELD)
    held = range(HEADS_HELD)
    n_chunk = n_t if n_t in (2, 4) else 1
    part = 3 * dim // n_chunk
    tile = min(rows, 128)
    grid = (rows // tile,)
    scale = 1.0 / math.sqrt(dim * rows * n_group * n_t)
    place = lax.axis_index("head") * n_s + lax.axis_index("s")
    at = jnp.stack([place, lax.axis_index("t")]).astype(jnp.int32)

    def partners(j):
        pairs = []
        for g in range(n_group):
            ends = [(x % n_s) * n_head + x // n_s for x in (g, g ^ j)]
            pairs.append(tuple(ends))
        return pairs

    params = pltpu.CompilerParams(
        dimension_semantics=("arbitrary",), vmem_limit_bytes=56 * 1024 * 1024
    )
    free = pl.BlockSpec(memory_space=pl.ANY)

    def call(kernel, grid, in_specs, out_specs, out_shape, scratch, *args, after=()):
        n_in = len(args)
        if after:
            inner = kernel

            def kernel(*refs):
                inner(*refs[: n_in + 1], *refs[n_in + 1 + len(after) :])

        return pl.pallas_call(
            kernel,
            out_shape=out_shape,
            grid_spec=pltpu.PrefetchScalarGridSpec(
                num_scalar_prefetch=1,
                grid=grid,
                in_specs=list(in_specs) + [free] * len(after),
                out_specs=out_specs,
                scratch_shapes=scratch,
            ),
            compiler_params=params,
        )(at, *args, *after)

    def by_head(first, second, a, after=()):
        specs = []
        for j in range(n_group):
            spec = pl.BlockSpec(
                (tile, dim), lambda i, p, j=j: (i, HEADS_HELD * jnp.bitwise_xor(p[0], j) + a)
            )
            specs += [spec, spec]
        return call(
            functools.partial(by_head_kernel, n_group),
            grid,
            specs,
            [pl.BlockSpec((2, tile, dim), lambda i, p: (0, i, 0))] * n_group,
            [jax.ShapeDtypeStruct((2, rows, dim), BF16)] * n_group,
            [],
            *([first, second] * n_group),
            after=after,
        )

    def swap(pieces):
        return [pieces[0]] + [
            lax.ppermute(pieces[j], ("s", "head"), partners(j))
            for j in range(1, n_group)
        ]

    def scatter(own, sent):
        if n_chunk == 1:
            return [lax.psum(own, "t") if n_t > 1 else own]
        return [own] + [
            lax.ppermute(sent[j - 1], "t", [(i, i ^ j) for i in range(n_t)])
            for j in range(1, n_chunk)
        ]

    def gather(chunk):
        return [chunk] + [
            lax.ppermute(chunk, "t", [(i, i ^ j) for i in range(n_t)])
            for j in range(1, n_chunk)
        ]

    piece_specs = [pl.BlockSpec((2, tile, dim), lambda i, p: (0, i, 0))] * n_group
    chunk_spec = pl.BlockSpec((part, dim), lambda i, p: (0, 0))
    chunk_shapes = [jax.ShapeDtypeStruct((part, dim), F32)]
    chunk_shapes += [jax.ShapeDtypeStruct((part, dim), BF16)] * (n_chunk - 1)
    whole = (3 * dim, dim)

    def rate_specs(a):
        return [pl.BlockSpec((1, n_head, tile), lambda i, p: (a, 0, i))] * n_s

    def w_spec(a):
        return pl.BlockSpec((1,) + whole, lambda i, p: (a, 0, 0))

    kv, qo = [None] * HEADS_HELD, [None] * HEADS_HELD
    last = ()
    for a in held:
        pieces = by_head(key_tokens, values, a, after=last)
        kv[a] = swap(pieces)
        last = (pieces[0],)
    by_column = learn_rates.T.reshape(n_s, HEADS_HELD, n_head, rows)
    rates = []
    for j in range(n_s):
        piece = by_column[jnp.bitwise_xor(lax.axis_index("s"), j)]
        if j:
            piece = lax.ppermute(piece, "s", [(i, i ^ j) for i in range(n_s)])
        rates.append(piece)
    for a in held:
        pieces = by_head(queries, out_grad, a, after=last)
        qo[a] = swap(pieces)
        last = (pieces[0],)

    first_spec = pl.BlockSpec(
        (1, dim, dim), lambda i, p: (HEADS_HELD * lax.rem(p[0], n_s) + i, 0, 0)
    )
    w = call(
        stack_kernel,
        (HEADS_HELD,),
        [first_spec] * 3,
        pl.BlockSpec((1,) + whole, lambda i, p: (i, 0, 0)),
        jax.ShapeDtypeStruct((HEADS_HELD,) + whole, BF16),
        [],
        w_gate,
        w_up,
        w_down,
        after=last,
    )

    def key_forward(a, after=()):
        own, *sent = call(
            functools.partial(key_kernel, n_group, n_s, n_chunk),
            grid,
            piece_specs + rate_specs(a) + [w_spec(a)],
            [chunk_spec] * n_chunk,
            chunk_shapes,
            [pltpu.VMEM(whole, F32)],
            *kv[a],
            *rates,
            w,
            after=after,
        )
        return own, scatter(own, sent)

    def make_fresh(a, chunks, after=()):
        out = call(
            functools.partial(fresh_kernel, scale, n_chunk),
            (1,),
            [chunk_spec] * n_chunk
            + [pl.BlockSpec((1, part, dim), lambda i, p: (a, p[1] if n_chunk > 1 else 0, 0))],
            chunk_spec,
            jax.ShapeDtypeStruct((part, dim), BF16),
            [],
            *chunks,
            w,
            after=after,
        )
        return out, gather(out)

    def query_side(a, fresh, after=()):
        outs = call(
            functools.partial(query_kernel, n_group, n_chunk),
            grid,
            piece_specs + [chunk_spec] * n_chunk,
            [pl.BlockSpec((tile, dim), lambda i, p: (i, 0))] * n_group + [chunk_spec] * n_chunk,
            [jax.ShapeDtypeStruct((rows, dim), BF16)] * n_group + chunk_shapes,
            [pltpu.VMEM(whole, F32), pltpu.VMEM(whole, BF16)],
            *qo[a],
            *fresh,
            after=after,
        )
        grads, own, sent = outs[:n_group], outs[n_group], outs[n_group + 1 :]
        chunks = scatter(own, sent)
        return own, chunks, swap(grads)

    def make_adjoint(chunks, after=()):
        out = call(
            functools.partial(adjoint_kernel, scale, n_chunk),
            (1,),
            [chunk_spec] * n_chunk,
            chunk_spec,
            jax.ShapeDtypeStruct((part, dim), BF16),
            [],
            *chunks,
            after=after,
        )
        return out, gather(out)

    def key_back(a, adjoint, after=()):
        outs = call(
            functools.partial(back_kernel, n_group, n_s, n_chunk),
            grid,
            piece_specs + rate_specs(a) + [w_spec(a)] + [chunk_spec] * n_chunk,
            piece_specs,
            [jax.ShapeDtypeStruct((2, rows, dim), BF16)] * n_group,
            [pltpu.VMEM(whole, BF16)],
            *kv[a],
            *rates,
            w,
            *adjoint,
            after=after,
        )
        return outs[0], swap(outs)

    mark, chunks_a = key_forward(0)
    mark, chunks_b = key_forward(1, (mark,))
    mark, fresh_a = make_fresh(0, chunks_a, (mark,))
    mark, fresh_b = make_fresh(1, chunks_b, (mark,))
    mark, sums_a, gq_a = query_side(0, fresh_a, (mark,))
    mark, adjoint_a = make_adjoint(sums_a, (mark,))
    mark, sums_b, gq_b = query_side(1, fresh_b, (mark,))
    mark, gkv_a = key_back(0, adjoint_a, (mark,))
    mark, adjoint_b = make_adjoint(sums_b, (mark,))
    mark, gkv_b = key_back(1, adjoint_b, (mark,))
    flat_spec = pl.BlockSpec((tile, model), lambda i, p: (i, 0))
    flat_shape = jax.ShapeDtypeStruct((rows, model), BF16)
    grad_q = call(
        functools.partial(home_kernel, n_group, 1),
        grid,
        [pl.BlockSpec((tile, dim), lambda i, p: (i, 0))] * (2 * n_group),
        [flat_spec],
        [flat_shape],
        [],
        *gq_a,
        *gq_b,
        after=(mark,),
    )[0]
    grad_k, grad_v = call(
        functools.partial(home_kernel, n_group, 2),
        grid,
        piece_specs * 2,
        [flat_spec] * 2,
        [flat_shape] * 2,
        [],
        *gkv_a,
        *gkv_b,
    )
    return grad_q, grad_k, grad_v


def solution(mesh):
    n_tok, n_head = mesh.shape["tok"], mesh.shape["head"]

    def run(queries, key_tokens, values, out_grad, learn_rates, w_gate, w_up, w_down):
        n_s = w_gate.shape[0] // (n_head * HEADS_HELD)
        n_t = n_tok // n_s
        split = Mesh(mesh.devices.reshape(n_t, n_s, n_head), ("t", "s", "head"))
        tokens = P(("t", "s", "head"), None)
        weights = P("head", None, None)
        return jax.shard_map(
            functools.partial(body, n_t, n_s, n_head),
            mesh=split,
            in_specs=(tokens,) * 4 + (P(("t", "s"), "head"),) + (weights,) * 3,
            out_specs=(tokens,) * 3,
            check_vma=False,
        )(queries, key_tokens, values, out_grad, learn_rates, w_gate, w_up, w_down)


    return run
```

time: 282 us -> 272 us (0.965)
  waiting for transfers between devices: 163 us -> 90.7 us
  starting transfers between devices: 27.2 us -> 98.7 us
  local copies, waits for them, and re-layouts: 49.9 us -> 3.36 us
  Pallas kernels: 31.2 us -> 76.1 us
  other arithmetic: 9.19 us -> 0.59 us
    all_to_all x5 -> x0, waiting for transfers between devices: 130 us -> none  [the longest x4 130 us: exchange(): return lax.all_to_all(x, spread, split_axis=0, concat_axis=0, tiled=True)]
    ppermute x2 -> x81, starting transfers between devices: 2.93 us -> 98.7 us  [the longest x56 57.6 us: swap(): lax.ppermute(pieces[j], ('s', 'head'), partners(j))]
    ppermute x2 -> x81, waiting for transfers between devices: 33.1 us -> 90.7 us  [the longest x56 62 us: swap(): lax.ppermute(pieces[j], ('s', 'head'), partners(j))]
    pallas_call x3 -> x17, Pallas kernels: 31.2 us -> 76.1 us  [call(): pl.pallas_call(kernel, out_shape=out_shape, grid_spec=pltpu.PrefetchScala...]
    all_to_all x5 -> x0, starting transfers between devices: 24.2 us -> none  [the longest x4 19 us: exchange(): return lax.all_to_all(x, spread, split_axis=0, concat_axis=0, tiled=True)]
    unnamed x14 -> x176, local copies, waits for them, and re-layouts: 24.4 us -> 2.74 us
    transpose x4 -> x0, local copies, waits for them, and re-layouts: 12.7 us -> none  [home(): return x.transpose(1, 0, 2).reshape(rows, model)]
    reshape x4 -> x1, local copies, waits for them, and re-layouts: 9.51 us -> 0.02 us  [body(): by_column = learn_rates.T.reshape(n_s, HEADS_HELD, n_head, rows)]
  transfers between devices with their start and end apart: 7 -> 81, of which waited for: 4 -> 20; matrix products, arithmetic and copies ran while one was open for 14% -> 0% of each run, Pallas kernels for 8% -> 25%
where the time goes in v3:
time: 272 us; the launch traced here: 271 us
  starting transfers between devices  98.7 us (36%)
  waiting for transfers between devices  90.7 us (33%)
  Pallas kernels  76.1 us (28%)
  local copies, waits for them, and re-layouts  3.36 us (1%)
    pallas_call x17, Pallas kernels, call(): pl.pallas_call(kernel, out_shape=out_shape, grid_spec=pltpu.PrefetchScala...  76.1 us
    ppermute x56, waiting for transfers between devices, swap(): lax.ppermute(pieces[j], ('s', 'head'), partners(j))  62 us
    ppermute x56, starting transfers between devices, swap(): lax.ppermute(pieces[j], ('s', 'head'), partners(j))  57.6 us
    ppermute x12, starting transfers between devices, scatter(): lax.ppermute(sent[j - 1], 't', [(i, i ^ j) for i in range(n_t)])  19.8 us
    ppermute x12, starting transfers between devices, gather(): lax.ppermute(chunk, 't', [(i, i ^ j) for i in range(n_t)])  19.4 us
    ppermute x12, waiting for transfers between devices, gather(): lax.ppermute(chunk, 't', [(i, i ^ j) for i in range(n_t)])  11.4 us
    ppermute x12, waiting for transfers between devices, scatter(): lax.ppermute(sent[j - 1], 't', [(i, i ^ j) for i in range(n_t)])  8.9 us
    ppermute x1, waiting for transfers between devices, body(): piece = lax.ppermute(piece, 's', [(i, i ^ j) for i in range(n_s)])  8.33 us
  transfers between devices with their start and end apart: 81, of which 20 were waited for; matrix products, arithmetic and copies ran while one was open for 0% of the time, Pallas kernels for 25%

profile of v3, /device:TPU:0, one launch (start us, length us, event | category | flops | bytes accessed | tf_op | source)
XLA Modules:
  0.0 271.2 jit_solution(5158325569403427609)
XLA Ops:
  1.2 3.6 %shard_map.103 = (bf16[2,256,256]{2,1,0:T(8,128)(2,1)}, bf16[2,256,256]{2,1,0:T(8,128)(2,1)}, bf16[2,256,256]{2,1,0:T(8,128)(2,1)}, bf16[2,256,256]{2,1,0:T(8,12...) custom-call(s32[2]{0:T(128)} %pad_add_fusion.at_ref.refs_0_, ...), custom_call_target="tpu_custom_call" | custom-call | tf_op jit(solution)/shard_map/pallas_call | solution.py:258
  4.8 3.1 %collective-permute-start.10 = (bf16[2,256,256]{2,1,0:T(8,128)(2,1)}, bf16[2,256,256]{2,1,0:T(8,128)(2,1)S(1)}, u32[]{:S(2)}, u32[]{:S(2)}) collective-permute-start(bf16[2,256,256]{2,1,0:T(8,128)(2,1)} %get-tuple-element.98), channel_id=1, source_target_pairs={{0,2},{4,6},{1,3},{5,7},{2,0},{6,4},{3,1},{7,5},{8,10},{12,14},{9,... | collective-permute-start | bytes 786440 | tf_op jit(solution)/shard_map/ppermute | solution.py:291
  13.2 8.3 %collective-permute-done.14.refs_9_.refs_10_ = f32[2,4,256]{2,1,0:T(4,128)S(1)} collective-permute-done((f32[2,4,256]{2,1,0:T(4,128)S(1)}, f32[2,4,256]{2,1,0:T(4,128)S(1)}, u32[]{:S(2)}, u32[]{:S(2)}) %collective-permute-start.14) | collective-permute-done | bytes 8224 | tf_op jit(solution)/shard_map/ppermute | solution.py:332
  23.1 3.3 %collective-permute-done.10.refs_4_.refs_5_ = bf16[2,256,256]{2,1,0:T(8,128)(2,1)S(1)} collective-permute-done((bf16[2,256,256]{2,1,0:T(8,128)(2,1)}, bf16[2,256,256]{2,1,0:T(8,128)(2,1)S(1)}, u32[]{:S(2)}, u32[]{:S(2)}) %collective-permute-start.10) | collective-permute-done | bytes 262176 | tf_op jit(solution)/shard_map/ppermute | solution.py:291
  28.6 3.5 %shard_map.104 = (bf16[2,256,256]{2,1,0:T(8,128)(2,1)}, bf16[2,256,256]{2,1,0:T(8,128)(2,1)}, bf16[2,256,256]{2,1,0:T(8,128)(2,1)}, bf16[2,256,256]{2,1,0:T(8,12...) custom-call(s32[2]{0:T(128)} %pad_add_fusion.at_ref.refs_0_, ...), custom_call_target="tpu_custom_call" | custom-call | tf_op jit(solution)/shard_map/pallas_call | solution.py:258
  37.7 3.9 %collective-permute-done.18.refs_2_ = bf16[2,256,256]{2,1,0:T(8,128)(2,1)S(1)} collective-permute-done((bf16[2,256,256]{2,1,0:T(8,128)(2,1)}, bf16[2,256,256]{2,1,0:T(8,128)(2,1)S(1)}, u32[]{:S(2)}, u32[]{:S(2)}) %collective-permute-start.18) | collective-permute-done | bytes 262176 | tf_op jit(solution)/shard_map/ppermute | solution.py:291
  42.1 2.7 %collective-permute-start.24 = (bf16[2,256,256]{2,1,0:T(8,128)(2,1)}, bf16[2,256,256]{2,1,0:T(8,128)(2,1)S(1)}, u32[]{:S(2)}, u32[]{:S(2)}) collective-permute-start(bf16[2,256,256]{2,1,0:T(8,128)(2,1)} %get-tuple-element.113), channel_id=1, source_target_pairs={{0,7},{4,3},{1,6},{5,2},{2,5},{6,1},{3,4},{7,0},{8,15},{12,11},{9,... | collective-permute-start | bytes 786440 | tf_op jit(solution)/shard_map/ppermute | solution.py:291
  44.8 3.5 %shard_map.105 = (bf16[2,256,256]{2,1,0:T(8,128)(2,1)}, bf16[2,256,256]{2,1,0:T(8,128)(2,1)}, bf16[2,256,256]{2,1,0:T(8,128)(2,1)}, bf16[2,256,256]{2,1,0:T(8,12...) custom-call(s32[2]{0:T(128)} %pad_add_fusion.at_ref.refs_0_, ...), custom_call_target="tpu_custom_call" | custom-call | tf_op jit(solution)/shard_map/pallas_call | solution.py:258
  49.1 5.3 %collective-permute-done.22.refs_6_ = bf16[2,256,256]{2,1,0:T(8,128)(2,1)S(1)} collective-permute-done((bf16[2,256,256]{2,1,0:T(8,128)(2,1)}, bf16[2,256,256]{2,1,0:T(8,128)(2,1)S(1)}, u32[]{:S(2)}, u32[]{:S(2)}) %collective-permute-start.22) | collective-permute-done | bytes 262176 | tf_op jit(solution)/shard_map/ppermute | solution.py:291
  54.4 6.8 %collective-permute-done.23.refs_7_ = bf16[2,256,256]{2,1,0:T(8,128)(2,1)S(1)} collective-permute-done((bf16[2,256,256]{2,1,0:T(8,128)(2,1)}, bf16[2,256,256]{2,1,0:T(8,128)(2,1)S(1)}, u32[]{:S(2)}, u32[]{:S(2)}) %collective-permute-start.23) | collective-permute-done | bytes 262176 | tf_op jit(solution)/shard_map/ppermute | solution.py:291
  62.7 2.4 collective-permute-start.4
  65.1 2.2 collective-permute-start.6
  67.3 3.5 %shard_map.106 = (bf16[2,256,256]{2,1,0:T(8,128)(2,1)}, bf16[2,256,256]{2,1,0:T(8,128)(2,1)}, bf16[2,256,256]{2,1,0:T(8,128)(2,1)}, bf16[2,256,256]{2,1,0:T(8,12...) custom-call(s32[2]{0:T(128)} %pad_add_fusion.at_ref.refs_0_, ...), custom_call_target="tpu_custom_call" | custom-call | tf_op jit(solution)/shard_map/pallas_call | solution.py:258
  72.0 8.5 %collective-permute-done.3.refs_5_ = bf16[2,256,256]{2,1,0:T(8,128)(2,1)S(1)} collective-permute-done((bf16[2,256,256]{2,1,0:T(8,128)(2,1)}, bf16[2,256,256]{2,1,0:T(8,128)(2,1)S(1)}, u32[]{:S(2)}, u32[]{:S(2)}) %collective-permute-start.3) | collective-permute-done | bytes 262176 | tf_op jit(solution)/shard_map/ppermute | solution.py:291
  80.5 3.9 %collective-permute-start.40 = (bf16[2,256,256]{2,1,0:T(8,128)(2,1)}, bf16[2,256,256]{2,1,0:T(8,128)(2,1)S(1)}, u32[]{:S(2)}, u32[]{:S(2)}) collective-permute-start(bf16[2,256,256]{2,1,0:T(8,128)(2,1)} %get-tuple-element.128), channel_id=1, source_target_pairs={{0,5},{4,1},{1,4},{5,0},{2,7},{6,3},{3,6},{7,2},{8,13},{12,9},{9,1... | collective-permute-start | bytes 786440 | tf_op jit(solution)/shard_map/ppermute | solution.py:291
  84.4 2.4 collective-permute-done.5.refs_7_
  86.8 3.0 %collective-permute-start.42 = (bf16[2,256,256]{2,1,0:T(8,128)(2,1)}, bf16[2,256,256]{2,1,0:T(8,128)(2,1)S(1)}, u32[]{:S(2)}, u32[]{:S(2)}) collective-permute-start(bf16[2,256,256]{2,1,0:T(8,128)(2,1)} %get-tuple-element.130), channel_id=1, source_target_pairs={{0,6},{4,2},{1,7},{5,3},{2,4},{6,0},{3,5},{7,1},{8,14},{12,10},{9,... | collective-permute-start | bytes 786440 | tf_op jit(solution)/shard_map/ppermute | solution.py:291
  89.7 2.7 shard_map.107.refs_10_.refs_11_.refs_5_
  92.4 5.8 %shard_map.108 = (f32[192,256]{1,0:T(8,128)}, bf16[192,256]{1,0:T(8,128)(2,1)}, bf16[192,256]{1,0:T(8,128)(2,1)}, bf16[192,256]{1,0:T(8,128)(2,1)}) custom-call(s32[2]{0:T(128)} %pad_add_fusion.at_ref.refs_0_, bf16[2,256,256]{2,1,0:T(8,128)(2,1)} %get-tuple-element.85.refs_17_.refs_0_.refs_1_, bf16[2,256,256]{2,1,0:T(8,128)(2,1)} %copy-done.11, ...), custom_call_target="tpu_custom_call" | custom-call | tf_op jit(solution)/shard_map/pallas_call | solution.py:258
  99.9 2.6 collective-permute-start.16
  102.8 5.8 %shard_map.109 = (f32[192,256]{1,0:T(8,128)}, bf16[192,256]{1,0:T(8,128)(2,1)}, bf16[192,256]{1,0:T(8,128)(2,1)}, bf16[192,256]{1,0:T(8,128)(2,1)}) custom-call(s32[2]{0:T(128)} %pad_add_fusion.at_ref.refs_0_, bf16[2,256,256]{2,1,0:T(8,128)(2,1)} %get-tuple-element.86.refs_17_.refs_1_, bf16[2,256,256]{2,1,0:T(8,128)(2,1)} %copy-done, ...), custom_call_target="tpu_custom_call" | custom-call | tf_op jit(solution)/shard_map/pallas_call | solution.py:258
  109.3 3.5 %collective-permute-start.29 = (bf16[192,256]{1,0:T(8,128)(2,1)}, bf16[192,256]{1,0:T(8,128)(2,1)S(1)}, u32[]{:S(2)}, u32[]{:S(2)}) collective-permute-start(bf16[192,256]{1,0:T(8,128)(2,1)} %get-tuple-element.116), channel_id=1, source_target_pairs={{0,16},{8,24},{16,0},{24,8},{1,17},{9,25},{17,1},{25,9},{2,18},{10... | collective-permute-start | bytes 294920 | tf_op jit(solution)/shard_map/ppermute | solution.py:299
  115.3 2.5 shard_map.110.refs_6_.refs_9_
  118.0 3.7 %collective-permute-start.26 = (bf16[192,256]{1,0:T(8,128)(2,1)}, bf16[192,256]{1,0:T(8,128)(2,1)S(1)}, u32[]{:S(2)}, u32[]{:S(2)}) collective-permute-start(bf16[192,256]{1,0:T(8,128)(2,1)} %shard_map.110.refs_6_.refs_9_), channel_id=1, source_target_pairs={{0,16},{8,24},{16,0},{24,8},{1,17},{9,25},{17,1},{25,9},{2,18},{10... | collective-permute-start | bytes 294920 | tf_op jit(solution)/shard_map/ppermute | solution.py:305
  123.0 2.5 shard_map.111.refs_13_.refs_9_
  129.2 4.4 %collective-permute-start.47 = (bf16[192,256]{1,0:T(8,128)(2,1)}, bf16[192,256]{1,0:T(8,128)(2,1)S(1)}, u32[]{:S(2)}, u32[]{:S(2)}) collective-permute-start(bf16[192,256]{1,0:T(8,128)(2,1)} %shard_map.111.refs_13_.refs_9_), channel_id=1, source_target_pairs={{0,24},{8,16},{16,8},{24,0},{1,25},{9,17},{17,9},{25,1},{2,26},{10... | collective-permute-start | bytes 294920 | tf_op jit(solution)/shard_map/ppermute | solution.py:305
  133.6 6.2 %shard_map.112 = (bf16[256,256]{1,0:T(8,128)(2,1)}, bf16[256,256]{1,0:T(8,128)(2,1)}, bf16[256,256]{1,0:T(8,128)(2,1)}, bf16[256,256]{1,0:T(8,128)(2,1)}, bf16[2...) custom-call(s32[2]{0:T(128)} %pad_add_fusion.at_ref.refs_0_, ...), custom_call_target="tpu_custom_call" | custom-call | tf_op jit(solution)/shard_map/pallas_call | solution.py:258
  140.0 3.8 %collective-permute-start.48 = (bf16[192,256]{1,0:T(8,128)(2,1)}, bf16[192,256]{1,0:T(8,128)(2,1)S(1)}, u32[]{:S(2)}, u32[]{:S(2)}) collective-permute-start(bf16[192,256]{1,0:T(8,128)(2,1)} %get-tuple-element.134), channel_id=1, source_target_pairs={{0,8},{8,0},{16,24},{24,16},{1,9},{9,1},{17,25},{25,17},{2,10},{10... | collective-permute-start | bytes 294920 | tf_op jit(solution)/shard_map/ppermute | solution.py:299
  143.9 2.3 collective-permute-start.50
  147.3 3.9 %collective-permute-done.49.refs_3_ = bf16[192,256]{1,0:T(8,128)(2,1)S(1)} collective-permute-done((bf16[192,256]{1,0:T(8,128)(2,1)}, bf16[192,256]{1,0:T(8,128)(2,1)S(1)}, u32[]{:S(2)}, u32[]{:S(2)}) %collective-permute-start.49) | collective-permute-done | bytes 98336 | tf_op jit(solution)/shard_map/ppermute | solution.py:299
  153.7 2.2 collective-permute-start.37
  155.9 2.4 shard_map.113.refs_13_.refs_12_
  162.8 6.4 %shard_map.114 = (bf16[256,256]{1,0:T(8,128)(2,1)}, bf16[256,256]{1,0:T(8,128)(2,1)}, bf16[256,256]{1,0:T(8,128)(2,1)}, bf16[256,256]{1,0:T(8,128)(2,1)}, bf16[2...) custom-call(s32[2]{0:T(128)} %pad_add_fusion.at_ref.refs_0_, ...), custom_call_target="tpu_custom_call" | custom-call | tf_op jit(solution)/shard_map/pallas_call | solution.py:258
  170.4 2.3 collective-permute-start.59
  175.8 4.1 %collective-permute-done.59.refs_3_ = bf16[192,256]{1,0:T(8,128)(2,1)S(1)} collective-permute-done((bf16[192,256]{1,0:T(8,128)(2,1)}, bf16[192,256]{1,0:T(8,128)(2,1)S(1)}, u32[]{:S(2)}, u32[]{:S(2)}) %collective-permute-start.59) | collective-permute-done | bytes 98336 | tf_op jit(solution)/shard_map/ppermute | solution.py:299
  180.8 2.1 collective-permute-start.55
  183.0 8.7 %shard_map.115 = (bf16[2,256,256]{2,1,0:T(8,128)(2,1)}, bf16[2,256,256]{2,1,0:T(8,128)(2,1)}, bf16[2,256,256]{2,1,0:T(8,128)(2,1)}, bf16[2,256,256]{2,1,0:T(8,12...) custom-call(s32[2]{0:T(128)} %pad_add_fusion.at_ref.refs_0_, ...), custom_call_target="tpu_custom_call" | custom-call | tf_op jit(solution)/shard_map/pallas_call | solution.py:258
  191.8 2.6 shard_map.116.refs_12_.refs_16_
  194.8 2.2 collective-permute-start.65
  199.1 2.2 collective-permute-done.64.refs_13_
  205.4 4.9 %collective-permute-done.66.refs_15_ = bf16[192,256]{1,0:T(8,128)(2,1)S(1)} collective-permute-done((bf16[192,256]{1,0:T(8,128)(2,1)}, bf16[192,256]{1,0:T(8,128)(2,1)S(1)}, u32[]{:S(2)}, u32[]{:S(2)}) %collective-permute-start.66) | collective-permute-done | bytes 98336 | tf_op jit(solution)/shard_map/ppermute | solution.py:305
  211.0 8.5 %shard_map.117 = (bf16[2,256,256]{2,1,0:T(8,128)(2,1)}, bf16[2,256,256]{2,1,0:T(8,128)(2,1)}, bf16[2,256,256]{2,1,0:T(8,128)(2,1)}, bf16[2,256,256]{2,1,0:T(8,12...) custom-call(s32[2]{0:T(128)} %pad_add_fusion.at_ref.refs_0_, ...), custom_call_target="tpu_custom_call" | custom-call | tf_op jit(solution)/shard_map/pallas_call | solution.py:258
  224.8 4.9 %collective-permute-done.71.refs_5_ = bf16[2,256,256]{2,1,0:T(8,128)(2,1)S(1)} collective-permute-done((bf16[2,256,256]{2,1,0:T(8,128)(2,1)S(1)}, bf16[2,256,256]{2,1,0:T(8,128)(2,1)S(1)}, u32[]{:S(2)}, u32[]{:S(2)}) %collective-permute-start.71) | collective-permute-done | bytes 262176 | tf_op jit(solution)/shard_map/ppermute | solution.py:291
  230.1 10.1 %collective-permute-done.72.refs_6_ = bf16[2,256,256]{2,1,0:T(8,128)(2,1)S(1)} collective-permute-done((bf16[2,256,256]{2,1,0:T(8,128)(2,1)S(1)}, bf16[2,256,256]{2,1,0:T(8,128)(2,1)S(1)}, u32[]{:S(2)}, u32[]{:S(2)}) %collective-permute-start.72) | collective-permute-done | bytes 262176 | tf_op jit(solution)/shard_map/ppermute | solution.py:291
  245.0 3.4 %shard_map.118 = bf16[256,4096]{1,0:T(8,128)(2,1)} custom-call(s32[2]{0:T(128)} %pad_add_fusion.at_ref.refs_0_, bf16[256,256]{1,0:T(8,128)(2,1)} %get-tuple-element.118.refs_1_, bf16[256,256]{1,0:T(8,128)(2,1)} %copy-done.43, bf16[256,256]{1,0:T(8,128)(2,1)} %copy-done.44, bf16[256,256]{1,0:T(8,128)(2,1)} %copy-done.45, bf16[256,256]{1,0:T(8,128)(2,1)} %copy-done.46, ...), custom_call_target="tpu_custom_call" | custom-call | tf_op jit(solution)/shard_map/pallas_call | solution.py:258
  248.5 12.4 %collective-permute-done.77.refs_12_ = bf16[2,256,256]{2,1,0:T(8,128)(2,1)S(1)} collective-permute-done((bf16[2,256,256]{2,1,0:T(8,128)(2,1)}, bf16[2,256,256]{2,1,0:T(8,128)(2,1)S(1)}, u32[]{:S(2)}, u32[]{:S(2)}) %collective-permute-start.77) | collective-permute-done | bytes 262176 | tf_op jit(solution)/shard_map/ppermute | solution.py:291
  260.9 4.1 %collective-permute-done.79.refs_14_ = bf16[2,256,256]{2,1,0:T(8,128)(2,1)S(1)} collective-permute-done((bf16[2,256,256]{2,1,0:T(8,128)(2,1)}, bf16[2,256,256]{2,1,0:T(8,128)(2,1)S(1)}, u32[]{:S(2)}, u32[]{:S(2)}) %collective-permute-start.79) | collective-permute-done | bytes 262176 | tf_op jit(solution)/shard_map/ppermute | solution.py:291
  266.4 4.6 %shard_map.119 = (bf16[256,4096]{1,0:T(8,128)(2,1)}, bf16[256,4096]{1,0:T(8,128)(2,1)}) custom-call(s32[2]{0:T(128)} %pad_add_fusion.at_ref.refs_0_, bf16[2,256,256]{2,1,0:T(8,128)(2,1)} %get-tuple-element.149.refs_5_.refs_0_, bf16[2,256,256]{2,1,0:T(8,128)(2,1)} %copy-done.14, bf16[2,256,256]{2,1,0:T(8,128)(2,1)} %copy-done.15, ...), custom_call_target="tpu_custom_call" | custom-call | tf_op jit(solution)/shard_map/pallas_call | solution.py:258
  (310 shorter events, 61.7 us)
Async XLA Ops:
  4.8 21.7 %collective-permute-start.10 = (bf16[2,256,256]{2,1,0:T(8,128)(2,1)}, bf16[2,256,256]{2,1,0:T(8,128)(2,1)S(1)}, u32[]{:S(2)}, u32[]{:S(2)}) collective-permute-start(bf16[2,256,256]{2,1,0:T(8,128)(2,1)} %get-tuple-element.98), channel_id=1, source_target_pairs={{0,2},{4,6},{1,3},{5,7},{2,0},{6,4},{3,1},{7,5},{8,10},{12,14},{9,... | collective-permute-start | bytes 786440 | tf_op jit(solution)/shard_map/ppermute | solution.py:291
  7.9 18.6 %collective-permute-start.11 = (bf16[2,256,256]{2,1,0:T(8,128)(2,1)}, bf16[2,256,256]{2,1,0:T(8,128)(2,1)S(1)}, u32[]{:S(2)}, u32[]{:S(2)}) collective-permute-start(bf16[2,256,256]{2,1,0:T(8,128)(2,1)} %get-tuple-element.99), channel_id=1, source_target_pairs={{0,6},{4,2},{1,7},{5,3},{2,4},{6,0},{3,5},{7,1},{8,14},{12,10},{9,... | collective-permute-start | bytes 786440 | tf_op jit(solution)/shard_map/ppermute | solution.py:291
  9.3 22.8 %collective-permute-start.12 = (bf16[2,256,256]{2,1,0:T(8,128)(2,1)}, bf16[2,256,256]{2,1,0:T(8,128)(2,1)S(1)}, u32[]{:S(2)}, u32[]{:S(2)}) collective-permute-start(bf16[2,256,256]{2,1,0:T(8,128)(2,1)} %get-tuple-element.100), channel_id=1, source_target_pairs={{0,3},{4,7},{1,2},{5,6},{2,1},{6,5},{3,0},{7,4},{8,11},{12,15},{9,... | collective-permute-start | bytes 786440 | tf_op jit(solution)/shard_map/ppermute | solution.py:291
  9.7 22.6 %collective-permute-start.13 = (bf16[2,256,256]{2,1,0:T(8,128)(2,1)}, bf16[2,256,256]{2,1,0:T(8,128)(2,1)S(1)}, u32[]{:S(2)}, u32[]{:S(2)}) collective-permute-start(bf16[2,256,256]{2,1,0:T(8,128)(2,1)} %get-tuple-element.101), channel_id=1, source_target_pairs={{0,7},{4,3},{1,6},{5,2},{2,5},{6,1},{3,4},{7,0},{8,15},{12,11},{9,... | collective-permute-start | bytes 786440 | tf_op jit(solution)/shard_map/ppermute | solution.py:291
  32.8 15.5 %collective-permute-start.20 = (bf16[2,256,256]{2,1,0:T(8,128)(2,1)}, bf16[2,256,256]{2,1,0:T(8,128)(2,1)S(1)}, u32[]{:S(2)}, u32[]{:S(2)}) collective-permute-start(bf16[2,256,256]{2,1,0:T(8,128)(2,1)} %get-tuple-element.109), channel_id=1, source_target_pairs={{0,5},{4,1},{1,4},{5,0},{2,7},{6,3},{3,6},{7,2},{8,13},{12,9},{9,1... | collective-permute-start | bytes 786440 | tf_op jit(solution)/shard_map/ppermute | solution.py:291
  34.4 14.1 %collective-permute-start.21 = (bf16[2,256,256]{2,1,0:T(8,128)(2,1)}, bf16[2,256,256]{2,1,0:T(8,128)(2,1)S(1)}, u32[]{:S(2)}, u32[]{:S(2)}) collective-permute-start(bf16[2,256,256]{2,1,0:T(8,128)(2,1)} %get-tuple-element.110), channel_id=1, source_target_pairs={{0,2},{4,6},{1,3},{5,7},{2,0},{6,4},{3,1},{7,5},{8,10},{12,14},{9,... | collective-permute-start | bytes 786440 | tf_op jit(solution)/shard_map/ppermute | solution.py:291
  35.9 18.4 %collective-permute-start.22 = (bf16[2,256,256]{2,1,0:T(8,128)(2,1)}, bf16[2,256,256]{2,1,0:T(8,128)(2,1)S(1)}, u32[]{:S(2)}, u32[]{:S(2)}) collective-permute-start(bf16[2,256,256]{2,1,0:T(8,128)(2,1)} %get-tuple-element.111), channel_id=1, source_target_pairs={{0,6},{4,2},{1,7},{5,3},{2,4},{6,0},{3,5},{7,1},{8,14},{12,10},{9,... | collective-permute-start | bytes 786440 | tf_op jit(solution)/shard_map/ppermute | solution.py:291
  41.7 19.6 %collective-permute-start.23 = (bf16[2,256,256]{2,1,0:T(8,128)(2,1)}, bf16[2,256,256]{2,1,0:T(8,128)(2,1)S(1)}, u32[]{:S(2)}, u32[]{:S(2)}) collective-permute-start(bf16[2,256,256]{2,1,0:T(8,128)(2,1)} %get-tuple-element.112), channel_id=1, source_target_pairs={{0,3},{4,7},{1,2},{5,6},{2,1},{6,5},{3,0},{7,4},{8,11},{12,15},{9,... | collective-permute-start | bytes 786440 | tf_op jit(solution)/shard_map/ppermute | solution.py:291
  42.1 20.6 %collective-permute-start.24 = (bf16[2,256,256]{2,1,0:T(8,128)(2,1)}, bf16[2,256,256]{2,1,0:T(8,128)(2,1)S(1)}, u32[]{:S(2)}, u32[]{:S(2)}) collective-permute-start(bf16[2,256,256]{2,1,0:T(8,128)(2,1)} %get-tuple-element.113), channel_id=1, source_target_pairs={{0,7},{4,3},{1,6},{5,2},{2,5},{6,1},{3,4},{7,0},{8,15},{12,11},{9,... | collective-permute-start | bytes 786440 | tf_op jit(solution)/shard_map/ppermute | solution.py:291
  48.4 16.7 %collective-permute-start = (bf16[2,256,256]{2,1,0:T(8,128)(2,1)}, bf16[2,256,256]{2,1,0:T(8,128)(2,1)S(1)}, u32[]{:S(2)}, u32[]{:S(2)}) collective-permute-start(bf16[2,256,256]{2,1,0:T(8,128)(2,1)} %get-tuple-element.88), channel_id=1, source_target_pairs={{0,4},{4,0},{1,5},{5,1},{2,6},{6,2},{3,7},{7,3},{8,12},{12,8},{9,1... | collective-permute-start | bytes 786440 | tf_op jit(solution)/shard_map/ppermute | solution.py:291
  48.5 16.6 %collective-permute-start.1 = (bf16[2,256,256]{2,1,0:T(8,128)(2,1)}, bf16[2,256,256]{2,1,0:T(8,128)(2,1)S(1)}, u32[]{:S(2)}, u32[]{:S(2)}) collective-permute-start(bf16[2,256,256]{2,1,0:T(8,128)(2,1)} %get-tuple-element.89), channel_id=1, source_target_pairs={{0,1},{4,5},{1,0},{5,4},{2,3},{6,7},{3,2},{7,6},{8,9},{12,13},{9,8... | collective-permute-start | bytes 786440 | tf_op jit(solution)/shard_map/ppermute | solution.py:291
  54.4 16.5 %collective-permute-start.2 = (bf16[2,256,256]{2,1,0:T(8,128)(2,1)}, bf16[2,256,256]{2,1,0:T(8,128)(2,1)S(1)}, u32[]{:S(2)}, u32[]{:S(2)}) collective-permute-start(bf16[2,256,256]{2,1,0:T(8,128)(2,1)} %get-tuple-element.90), channel_id=1, source_target_pairs={{0,5},{4,1},{1,4},{5,0},{2,7},{6,3},{3,6},{7,2},{8,13},{12,9},{9,1... | collective-permute-start | bytes 786440 | tf_op jit(solution)/shard_map/ppermute | solution.py:291
  61.2 19.2 %collective-permute-start.3 = (bf16[2,256,256]{2,1,0:T(8,128)(2,1)}, bf16[2,256,256]{2,1,0:T(8,128)(2,1)S(1)}, u32[]{:S(2)}, u32[]{:S(2)}) collective-permute-start(bf16[2,256,256]{2,1,0:T(8,128)(2,1)} %get-tuple-element.91), channel_id=1, source_target_pairs={{0,2},{4,6},{1,3},{5,7},{2,0},{6,4},{3,1},{7,5},{8,10},{12,14},{9,... | collective-permute-start | bytes 786440 | tf_op jit(solution)/shard_map/ppermute | solution.py:291
  62.7 17.7 %collective-permute-start.4 = (bf16[2,256,256]{2,1,0:T(8,128)(2,1)}, bf16[2,256,256]{2,1,0:T(8,128)(2,1)S(1)}, u32[]{:S(2)}, u32[]{:S(2)}) collective-permute-start(bf16[2,256,256]{2,1,0:T(8,128)(2,1)} %get-tuple-element.92), channel_id=1, source_target_pairs={{0,6},{4,2},{1,7},{5,3},{2,4},{6,0},{3,5},{7,1},{8,14},{12,10},{9,... | collective-permute-start | bytes 786440 | tf_op jit(solution)/shard_map/ppermute | solution.py:291
  65.1 21.7 %collective-permute-start.5 = (bf16[2,256,256]{2,1,0:T(8,128)(2,1)}, bf16[2,256,256]{2,1,0:T(8,128)(2,1)S(1)}, u32[]{:S(2)}, u32[]{:S(2)}) collective-permute-start(bf16[2,256,256]{2,1,0:T(8,128)(2,1)} %get-tuple-element.93), channel_id=1, source_target_pairs={{0,3},{4,7},{1,2},{5,6},{2,1},{6,5},{3,0},{7,4},{8,11},{12,15},{9,... | collective-permute-start | bytes 786440 | tf_op jit(solution)/shard_map/ppermute | solution.py:291
  65.1 21.6 %collective-permute-start.6 = (bf16[2,256,256]{2,1,0:T(8,128)(2,1)}, bf16[2,256,256]{2,1,0:T(8,128)(2,1)S(1)}, u32[]{:S(2)}, u32[]{:S(2)}) collective-permute-start(bf16[2,256,256]{2,1,0:T(8,128)(2,1)} %get-tuple-element.94), channel_id=1, source_target_pairs={{0,7},{4,3},{1,6},{5,2},{2,5},{6,1},{3,4},{7,0},{8,15},{12,11},{9,... | collective-permute-start | bytes 786440 | tf_op jit(solution)/shard_map/ppermute | solution.py:291
  70.9 27.3 %collective-permute-start.38 = (bf16[2,256,256]{2,1,0:T(8,128)(2,1)}, bf16[2,256,256]{2,1,0:T(8,128)(2,1)S(1)}, u32[]{:S(2)}, u32[]{:S(2)}) collective-permute-start(bf16[2,256,256]{2,1,0:T(8,128)(2,1)} %get-tuple-element.126), channel_id=1, source_target_pairs={{0,4},{4,0},{1,5},{5,1},{2,6},{6,2},{3,7},{7,3},{8,12},{12,8},{9,1... | collective-permute-start | bytes 786440 | tf_op jit(solution)/shard_map/ppermute | solution.py:291
  80.5 19.5 %collective-permute-start.39 = (bf16[2,256,256]{2,1,0:T(8,128)(2,1)}, bf16[2,256,256]{2,1,0:T(8,128)(2,1)S(1)}, u32[]{:S(2)}, u32[]{:S(2)}) collective-permute-start(bf16[2,256,256]{2,1,0:T(8,128)(2,1)} %get-tuple-element.127), channel_id=1, source_target_pairs={{0,1},{4,5},{1,0},{5,4},{2,3},{6,7},{3,2},{7,6},{8,9},{12,13},{9,8... | collective-permute-start | bytes 786440 | tf_op jit(solution)/shard_map/ppermute | solution.py:291
  80.5 22.1 %collective-permute-start.40 = (bf16[2,256,256]{2,1,0:T(8,128)(2,1)}, bf16[2,256,256]{2,1,0:T(8,128)(2,1)S(1)}, u32[]{:S(2)}, u32[]{:S(2)}) collective-permute-start(bf16[2,256,256]{2,1,0:T(8,128)(2,1)} %get-tuple-element.128), channel_id=1, source_target_pairs={{0,5},{4,1},{1,4},{5,0},{2,7},{6,3},{3,6},{7,2},{8,13},{12,9},{9,1... | collective-permute-start | bytes 786440 | tf_op jit(solution)/shard_map/ppermute | solution.py:291
  86.7 21.8 %collective-permute-start.41 = (bf16[2,256,256]{2,1,0:T(8,128)(2,1)}, bf16[2,256,256]{2,1,0:T(8,128)(2,1)S(1)}, u32[]{:S(2)}, u32[]{:S(2)}) collective-permute-start(bf16[2,256,256]{2,1,0:T(8,128)(2,1)} %get-tuple-element.129), channel_id=1, source_target_pairs={{0,2},{4,6},{1,3},{5,7},{2,0},{6,4},{3,1},{7,5},{8,10},{12,14},{9,... | collective-permute-start | bytes 786440 | tf_op jit(solution)/shard_map/ppermute | solution.py:291
  86.8 22.6 %collective-permute-start.42 = (bf16[2,256,256]{2,1,0:T(8,128)(2,1)}, bf16[2,256,256]{2,1,0:T(8,128)(2,1)S(1)}, u32[]{:S(2)}, u32[]{:S(2)}) collective-permute-start(bf16[2,256,256]{2,1,0:T(8,128)(2,1)} %get-tuple-element.130), channel_id=1, source_target_pairs={{0,6},{4,2},{1,7},{5,3},{2,4},{6,0},{3,5},{7,1},{8,14},{12,10},{9,... | collective-permute-start | bytes 786440 | tf_op jit(solution)/shard_map/ppermute | solution.py:291
  98.3 14.5 %collective-permute-start.15 = (bf16[192,256]{1,0:T(8,128)(2,1)}, bf16[192,256]{1,0:T(8,128)(2,1)S(1)}, u32[]{:S(2)}, u32[]{:S(2)}) collective-permute-start(bf16[192,256]{1,0:T(8,128)(2,1)} %get-tuple-element.104), channel_id=1, source_target_pairs={{0,8},{8,0},{16,24},{24,16},{1,9},{9,1},{17,25},{25,17},{2,10},{10... | collective-permute-start | bytes 294920 | tf_op jit(solution)/shard_map/ppermute | solution.py:299
  112.8 27.0 %collective-permute-start.43 = (bf16[2,256,256]{2,1,0:T(8,128)(2,1)S(1)}, bf16[2,256,256]{2,1,0:T(8,128)(2,1)S(1)}, u32[]{:S(2)}, u32[]{:S(2)}) collective-permute-start(bf16[2,256,256]{2,1,0:T(8,128)(2,1)S(1)} %copy-done.83), channel_id=1, source_target_pairs={{0,3},{4,7},{1,2},{5,6},{2,1},{6,5},{3,0},{7,4},{8,11},{12,15},{9,... | collective-permute-start | bytes 786440 | tf_op jit(solution)/shard_map/ppermute | solution.py:291
  112.9 27.0 %collective-permute-start.44 = (bf16[2,256,256]{2,1,0:T(8,128)(2,1)S(1)}, bf16[2,256,256]{2,1,0:T(8,128)(2,1)S(1)}, u32[]{:S(2)}, u32[]{:S(2)}) collective-permute-start(bf16[2,256,256]{2,1,0:T(8,128)(2,1)S(1)} %copy-done.82), channel_id=1, source_target_pairs={{0,7},{4,3},{1,6},{5,2},{2,5},{6,1},{3,4},{7,0},{8,15},{12,11},{9,... | collective-permute-start | bytes 786440 | tf_op jit(solution)/shard_map/ppermute | solution.py:291
  125.5 18.3 %collective-permute-start.45 = (bf16[192,256]{1,0:T(8,128)(2,1)}, bf16[192,256]{1,0:T(8,128)(2,1)S(1)}, u32[]{:S(2)}, u32[]{:S(2)}) collective-permute-start(bf16[192,256]{1,0:T(8,128)(2,1)} %shard_map.111.refs_13_.refs_9_), channel_id=1, source_target_pairs={{0,8},{8,0},{16,24},{24,16},{1,9},{9,1},{17,25},{25,17},{2,10},{10... | collective-permute-start | bytes 294920 | tf_op jit(solution)/shard_map/ppermute | solution.py:305
  128.7 15.1 %collective-permute-start.46 = (bf16[192,256]{1,0:T(8,128)(2,1)}, bf16[192,256]{1,0:T(8,128)(2,1)S(1)}, u32[]{:S(2)}, u32[]{:S(2)}) collective-permute-start(bf16[192,256]{1,0:T(8,128)(2,1)} %shard_map.111.refs_13_.refs_9_), channel_id=1, source_target_pairs={{0,16},{8,24},{16,0},{24,8},{1,17},{9,25},{17,1},{25,9},{2,18},{10... | collective-permute-start | bytes 294920 | tf_op jit(solution)/shard_map/ppermute | solution.py:305
  129.2 17.0 %collective-permute-start.47 = (bf16[192,256]{1,0:T(8,128)(2,1)}, bf16[192,256]{1,0:T(8,128)(2,1)S(1)}, u32[]{:S(2)}, u32[]{:S(2)}) collective-permute-start(bf16[192,256]{1,0:T(8,128)(2,1)} %shard_map.111.refs_13_.refs_9_), channel_id=1, source_target_pairs={{0,24},{8,16},{16,8},{24,0},{1,25},{9,17},{17,9},{25,1},{2,26},{10... | collective-permute-start | bytes 294920 | tf_op jit(solution)/shard_map/ppermute | solution.py:305
  153.7 15.5 %collective-permute-start.36 = (bf16[256,256]{1,0:T(8,128)(2,1)}, bf16[256,256]{1,0:T(8,128)(2,1)S(1)}, u32[]{:S(2)}, u32[]{:S(2)}) collective-permute-start(bf16[256,256]{1,0:T(8,128)(2,1)} %get-tuple-element.124), channel_id=1, source_target_pairs={{0,3},{4,7},{1,2},{5,6},{2,1},{6,5},{3,0},{7,4},{8,11},{12,15},{9,... | collective-permute-start | bytes 393224 | tf_op jit(solution)/shard_map/ppermute | solution.py:291
  153.7 15.9 %collective-permute-start.37 = (bf16[256,256]{1,0:T(8,128)(2,1)}, bf16[256,256]{1,0:T(8,128)(2,1)S(1)}, u32[]{:S(2)}, u32[]{:S(2)}) collective-permute-start(bf16[256,256]{1,0:T(8,128)(2,1)} %get-tuple-element.125), channel_id=1, source_target_pairs={{0,7},{4,3},{1,6},{5,2},{2,5},{6,1},{3,4},{7,0},{8,15},{12,11},{9,... | collective-permute-start | bytes 393224 | tf_op jit(solution)/shard_map/ppermute | solution.py:291
  160.8 13.9 %collective-permute-start.63 = (bf16[192,256]{1,0:T(8,128)(2,1)}, bf16[192,256]{1,0:T(8,128)(2,1)S(1)}, u32[]{:S(2)}, u32[]{:S(2)}) collective-permute-start(bf16[192,256]{1,0:T(8,128)(2,1)} %shard_map.113.refs_13_.refs_12_), channel_id=1, source_target_pairs={{0,24},{8,16},{16,8},{24,0},{1,25},{9,17},{17,9},{25,1},{2,26},{10... | collective-permute-start | bytes 294920 | tf_op jit(solution)/shard_map/ppermute | solution.py:305
  174.7 19.7 %collective-permute-start.52 = (bf16[256,256]{1,0:T(8,128)(2,1)}, bf16[256,256]{1,0:T(8,128)(2,1)S(1)}, u32[]{:S(2)}, u32[]{:S(2)}) collective-permute-start(bf16[256,256]{1,0:T(8,128)(2,1)} %get-tuple-element.139), channel_id=1, source_target_pairs={{0,1},{4,5},{1,0},{5,4},{2,3},{6,7},{3,2},{7,6},{8,9},{12,13},{9,8... | collective-permute-start | bytes 393224 | tf_op jit(solution)/shard_map/ppermute | solution.py:291
  174.7 20.0 %collective-permute-start.53 = (bf16[256,256]{1,0:T(8,128)(2,1)}, bf16[256,256]{1,0:T(8,128)(2,1)S(1)}, u32[]{:S(2)}, u32[]{:S(2)}) collective-permute-start(bf16[256,256]{1,0:T(8,128)(2,1)} %get-tuple-element.140), channel_id=1, source_target_pairs={{0,5},{4,1},{1,4},{5,0},{2,7},{6,3},{3,6},{7,2},{8,13},{12,9},{9,1... | collective-permute-start | bytes 393224 | tf_op jit(solution)/shard_map/ppermute | solution.py:291
  179.9 17.0 %collective-permute-start.54 = (bf16[256,256]{1,0:T(8,128)(2,1)}, bf16[256,256]{1,0:T(8,128)(2,1)S(1)}, u32[]{:S(2)}, u32[]{:S(2)}) collective-permute-start(bf16[256,256]{1,0:T(8,128)(2,1)} %get-tuple-element.141), channel_id=1, source_target_pairs={{0,2},{4,6},{1,3},{5,7},{2,0},{6,4},{3,1},{7,5},{8,10},{12,14},{9,... | collective-permute-start | bytes 393224 | tf_op jit(solution)/shard_map/ppermute | solution.py:291
  180.8 16.6 %collective-permute-start.55 = (bf16[256,256]{1,0:T(8,128)(2,1)}, bf16[256,256]{1,0:T(8,128)(2,1)S(1)}, u32[]{:S(2)}, u32[]{:S(2)}) collective-permute-start(bf16[256,256]{1,0:T(8,128)(2,1)} %get-tuple-element.142), channel_id=1, source_target_pairs={{0,6},{4,2},{1,7},{5,3},{2,4},{6,0},{3,5},{7,1},{8,14},{12,10},{9,... | collective-permute-start | bytes 393224 | tf_op jit(solution)/shard_map/ppermute | solution.py:291
  183.0 14.6 %collective-permute-start.56 = (bf16[256,256]{1,0:T(8,128)(2,1)}, bf16[256,256]{1,0:T(8,128)(2,1)S(1)}, u32[]{:S(2)}, u32[]{:S(2)}) collective-permute-start(bf16[256,256]{1,0:T(8,128)(2,1)} %get-tuple-element.143), channel_id=1, source_target_pairs={{0,3},{4,7},{1,2},{5,6},{2,1},{6,5},{3,0},{7,4},{8,11},{12,15},{9,... | collective-permute-start | bytes 393224 | tf_op jit(solution)/shard_map/ppermute | solution.py:291
  196.9 23.8 %collective-permute-start.67 = (bf16[2,256,256]{2,1,0:T(8,128)(2,1)}, bf16[2,256,256]{2,1,0:T(8,128)(2,1)S(1)}, u32[]{:S(2)}, u32[]{:S(2)}) collective-permute-start(bf16[2,256,256]{2,1,0:T(8,128)(2,1)} %get-tuple-element.151), channel_id=1, source_target_pairs={{0,4},{4,0},{1,5},{5,1},{2,6},{6,2},{3,7},{7,3},{8,12},{12,8},{9,1... | collective-permute-start | bytes 786440 | tf_op jit(solution)/shard_map/ppermute | solution.py:291
  197.4 25.0 %collective-permute-start.68 = (bf16[2,256,256]{2,1,0:T(8,128)(2,1)}, bf16[2,256,256]{2,1,0:T(8,128)(2,1)S(1)}, u32[]{:S(2)}, u32[]{:S(2)}) collective-permute-start(bf16[2,256,256]{2,1,0:T(8,128)(2,1)} %get-tuple-element.152), channel_id=1, source_target_pairs={{0,1},{4,5},{1,0},{5,4},{2,3},{6,7},{3,2},{7,6},{8,9},{12,13},{9,8... | collective-permute-start | bytes 786440 | tf_op jit(solution)/shard_map/ppermute | solution.py:291
  197.6 25.7 %collective-permute-start.69 = (bf16[2,256,256]{2,1,0:T(8,128)(2,1)}, bf16[2,256,256]{2,1,0:T(8,128)(2,1)S(1)}, u32[]{:S(2)}, u32[]{:S(2)}) collective-permute-start(bf16[2,256,256]{2,1,0:T(8,128)(2,1)} %get-tuple-element.153), channel_id=1, source_target_pairs={{0,5},{4,1},{1,4},{5,0},{2,7},{6,3},{3,6},{7,2},{8,13},{12,9},{9,1... | collective-permute-start | bytes 786440 | tf_op jit(solution)/shard_map/ppermute | solution.py:291
  201.3 22.8 %collective-permute-start.70 = (bf16[2,256,256]{2,1,0:T(8,128)(2,1)}, bf16[2,256,256]{2,1,0:T(8,128)(2,1)S(1)}, u32[]{:S(2)}, u32[]{:S(2)}) collective-permute-start(bf16[2,256,256]{2,1,0:T(8,128)(2,1)} %get-tuple-element.154), channel_id=1, source_target_pairs={{0,2},{4,6},{1,3},{5,7},{2,0},{6,4},{3,1},{7,5},{8,10},{12,14},{9,... | collective-permute-start | bytes 786440 | tf_op jit(solution)/shard_map/ppermute | solution.py:291
  220.8 19.5 %collective-permute-start.72 = (bf16[2,256,256]{2,1,0:T(8,128)(2,1)S(1)}, bf16[2,256,256]{2,1,0:T(8,128)(2,1)S(1)}, u32[]{:S(2)}, u32[]{:S(2)}) collective-permute-start(bf16[2,256,256]{2,1,0:T(8,128)(2,1)S(1)} %copy-done.85), channel_id=1, source_target_pairs={{0,3},{4,7},{1,2},{5,6},{2,1},{6,5},{3,0},{7,4},{8,11},{12,15},{9,... | collective-permute-start | bytes 786440 | tf_op jit(solution)/shard_map/ppermute | solution.py:291
  222.4 19.2 %collective-permute-start.73 = (bf16[2,256,256]{2,1,0:T(8,128)(2,1)S(1)}, bf16[2,256,256]{2,1,0:T(8,128)(2,1)S(1)}, u32[]{:S(2)}, u32[]{:S(2)}) collective-permute-start(bf16[2,256,256]{2,1,0:T(8,128)(2,1)S(1)} %copy-done.84), channel_id=1, source_target_pairs={{0,7},{4,3},{1,6},{5,2},{2,5},{6,1},{3,4},{7,0},{8,15},{12,11},{9,... | collective-permute-start | bytes 786440 | tf_op jit(solution)/shard_map/ppermute | solution.py:291
  223.3 19.8 %collective-permute-start.74 = (bf16[2,256,256]{2,1,0:T(8,128)(2,1)}, bf16[2,256,256]{2,1,0:T(8,128)(2,1)S(1)}, u32[]{:S(2)}, u32[]{:S(2)}) collective-permute-start(bf16[2,256,256]{2,1,0:T(8,128)(2,1)} %get-tuple-element.158), channel_id=1, source_target_pairs={{0,4},{4,0},{1,5},{5,1},{2,6},{6,2},{3,7},{7,3},{8,12},{12,8},{9,1... | collective-permute-start | bytes 786440 | tf_op jit(solution)/shard_map/ppermute | solution.py:291
  224.1 19.2 %collective-permute-start.75 = (bf16[2,256,256]{2,1,0:T(8,128)(2,1)}, bf16[2,256,256]{2,1,0:T(8,128)(2,1)S(1)}, u32[]{:S(2)}, u32[]{:S(2)}) collective-permute-start(bf16[2,256,256]{2,1,0:T(8,128)(2,1)} %get-tuple-element.159), channel_id=1, source_target_pairs={{0,1},{4,5},{1,0},{5,4},{2,3},{6,7},{3,2},{7,6},{8,9},{12,13},{9,8... | collective-permute-start | bytes 786440 | tf_op jit(solution)/shard_map/ppermute | solution.py:291
  229.8 18.7 %collective-permute-start.76 = (bf16[2,256,256]{2,1,0:T(8,128)(2,1)}, bf16[2,256,256]{2,1,0:T(8,128)(2,1)S(1)}, u32[]{:S(2)}, u32[]{:S(2)}) collective-permute-start(bf16[2,256,256]{2,1,0:T(8,128)(2,1)} %get-tuple-element.160), channel_id=1, source_target_pairs={{0,5},{4,1},{1,4},{5,0},{2,7},{6,3},{3,6},{7,2},{8,13},{12,9},{9,1... | collective-permute-start | bytes 786440 | tf_op jit(solution)/shard_map/ppermute | solution.py:291
  240.3 20.6 %collective-permute-start.77 = (bf16[2,256,256]{2,1,0:T(8,128)(2,1)}, bf16[2,256,256]{2,1,0:T(8,128)(2,1)S(1)}, u32[]{:S(2)}, u32[]{:S(2)}) collective-permute-start(bf16[2,256,256]{2,1,0:T(8,128)(2,1)} %get-tuple-element.161), channel_id=1, source_target_pairs={{0,2},{4,6},{1,3},{5,7},{2,0},{6,4},{3,1},{7,5},{8,10},{12,14},{9,... | collective-permute-start | bytes 786440 | tf_op jit(solution)/shard_map/ppermute | solution.py:291
  241.6 19.3 %collective-permute-start.78 = (bf16[2,256,256]{2,1,0:T(8,128)(2,1)}, bf16[2,256,256]{2,1,0:T(8,128)(2,1)S(1)}, u32[]{:S(2)}, u32[]{:S(2)}) collective-permute-start(bf16[2,256,256]{2,1,0:T(8,128)(2,1)} %get-tuple-element.162), channel_id=1, source_target_pairs={{0,6},{4,2},{1,7},{5,3},{2,4},{6,0},{3,5},{7,1},{8,14},{12,10},{9,... | collective-permute-start | bytes 786440 | tf_op jit(solution)/shard_map/ppermute | solution.py:291
  243.1 21.9 %collective-permute-start.79 = (bf16[2,256,256]{2,1,0:T(8,128)(2,1)}, bf16[2,256,256]{2,1,0:T(8,128)(2,1)S(1)}, u32[]{:S(2)}, u32[]{:S(2)}) collective-permute-start(bf16[2,256,256]{2,1,0:T(8,128)(2,1)} %get-tuple-element.163), channel_id=1, source_target_pairs={{0,3},{4,7},{1,2},{5,6},{2,1},{6,5},{3,0},{7,4},{8,11},{12,15},{9,... | collective-permute-start | bytes 786440 | tf_op jit(solution)/shard_map/ppermute | solution.py:291
  243.3 21.7 %collective-permute-start.80 = (bf16[2,256,256]{2,1,0:T(8,128)(2,1)}, bf16[2,256,256]{2,1,0:T(8,128)(2,1)S(1)}, u32[]{:S(2)}, u32[]{:S(2)}) collective-permute-start(bf16[2,256,256]{2,1,0:T(8,128)(2,1)} %get-tuple-element.164), channel_id=1, source_target_pairs={{0,7},{4,3},{1,6},{5,2},{2,5},{6,1},{3,4},{7,0},{8,15},{12,11},{9,... | collective-permute-start | bytes 786440 | tf_op jit(solution)/shard_map/ppermute | solution.py:291
  (121 other events, 1777.4 us)

commit v4 on v3

v4 whole, which is shorter than its diff:
```python
import functools
import math

import jax
import jax.numpy as jnp
from jax import lax
from jax.experimental import pallas as pl
from jax.experimental.pallas import tpu as pltpu
from jax.sharding import Mesh, PartitionSpec as P


F32 = jnp.float32
BF16 = jnp.bfloat16
HEADS_HELD = 2


def mm(a, b):
    return lax.dot_general(a, b, (((1,), (0,)), ((), ())), preferred_element_type=F32)


def mm_nt(a, b):
    return lax.dot_general(a, b, (((1,), (1,)), ((), ())), preferred_element_type=F32)


def mm_tn(a, b):
    return lax.dot_general(a, b, (((0,), (0,)), ((), ())), preferred_element_type=F32)


def sigmoid(x):
    return jax.nn.sigmoid(x)


def by_head_kernel(n_group, at_ref, first_ref, second_ref, *outs):
    dim = outs[0].shape[-1]
    for a in range(HEADS_HELD):
        for j in range(n_group):
            head = HEADS_HELD * jnp.bitwise_xor(at_ref[0], j) + a
            columns = pl.ds(pl.multiple_of(head * dim, dim), dim)
            outs[a * n_group + j][0] = first_ref[:, columns]
            outs[a * n_group + j][1] = second_ref[:, columns]


def home_kernel(n_group, n_out, at_ref, *refs):
    outs = refs[-n_out:]
    dim = refs[0].shape[-1]
    for a in range(HEADS_HELD):
        for j in range(n_group):
            piece = refs[a * n_group + j]
            head = HEADS_HELD * jnp.bitwise_xor(at_ref[0], j) + a
            columns = pl.ds(pl.multiple_of(head * dim, dim), dim)
            if n_out == 1:
                outs[0][:, columns] = piece[...]
            else:
                for i, out in enumerate(outs):
                    out[:, columns] = piece[i]


def tall_rates(at_ref, rate_refs, n_group, dim):
    n_s = len(rate_refs)
    head = at_ref[0] // n_s
    columns = []
    for j in range(n_group):
        ref = rate_refs[j % n_s]
        row = ref[0, pl.ds(jnp.bitwise_xor(head, j // n_s), 1), :]
        columns.append(jnp.broadcast_to(row, (128, row.shape[1])).T)
    tall = jnp.concatenate(columns, axis=0)
    return jnp.concatenate([tall] * (dim // 128), axis=1)


def stacked(refs, which):
    return jnp.concatenate([ref[which] for ref in refs], axis=0)


def total_of(own_ref, other_refs):
    total = own_ref[...]
    for ref in other_refs:
        total = total + ref[...].astype(F32)
    return total


def key_kernel(n_group, n_s, at_ref, *refs):
    pieces, refs = refs[:n_group], refs[n_group:]
    rate_refs, refs = refs[:n_s], refs[n_s:]
    wg_ref, wu_ref, wd_ref, acc, sent_ref = refs
    step = pl.program_id(0)
    dim = pieces[0].shape[-1]

    @pl.when(step == 0)
    def _():
        acc[...] = jnp.zeros_like(acc)

    k = stacked(pieces, 0)
    rate = tall_rates(at_ref, rate_refs, n_group, dim)
    scaled = (rate * stacked(pieces, 1).astype(F32)).astype(BF16)
    gate = mm(k, wg_ref[0])
    up = mm(k, wu_ref[0])
    dhid = mm_nt(scaled, wd_ref[0])
    sig = sigmoid(gate)
    act = gate * sig
    hidden = (act * up).astype(BF16)
    dgate = (dhid * up * (sig * (1.0 + gate * (1.0 - sig)))).astype(BF16)
    dup = (dhid * act).astype(BF16)
    acc[:dim] += mm_tn(k, dgate)
    acc[dim : 2 * dim] += mm_tn(k, dup)
    acc[2 * dim :] += mm_tn(hidden, scaled)

    @pl.when(step == pl.num_programs(0) - 1)
    def _():
        sent_ref[...] = acc[...].astype(BF16)


def query_kernel(scale, n_group, n_other, at_ref, *refs):
    pieces, refs = refs[:n_group], refs[n_group:]
    w_refs, own_ref, other_refs = refs[:3], refs[3], refs[4 : 4 + n_other]
    refs = refs[4 + n_other :]
    grads, acc, sent_ref, fresh = refs[:n_group], refs[-3], refs[-2], refs[-1]
    step = pl.program_id(0)
    dim = pieces[0].shape[-1]

    @pl.when(step == 0)
    def _():
        acc[...] = jnp.zeros_like(acc)
        total = total_of(own_ref, other_refs)
        for i, ref in enumerate(w_refs):
            rows = slice(i * dim, (i + 1) * dim)
            fresh[rows] = (ref[0].astype(F32) + scale * total[rows]).astype(BF16)

    q = stacked(pieces, 0)
    o = stacked(pieces, 1)
    w_gate, w_up, w_down = fresh[:dim], fresh[dim : 2 * dim], fresh[2 * dim :]
    gate = mm(q, w_gate)
    up = mm(q, w_up)
    dhid = mm_nt(o, w_down)
    sig = sigmoid(gate)
    act = gate * sig
    hidden = (act * up).astype(BF16)
    dgate = (dhid * up * (sig * (1.0 + gate * (1.0 - sig)))).astype(BF16)
    dup = (dhid * act).astype(BF16)
    grad = (mm_nt(dgate, w_gate) + mm_nt(dup, w_up)).astype(BF16)
    rows = grads[0].shape[0]
    for j, ref in enumerate(grads):
        ref[...] = grad[j * rows : (j + 1) * rows]
    acc[:dim] += mm_tn(q, dgate)
    acc[dim : 2 * dim] += mm_tn(q, dup)
    acc[2 * dim :] += mm_tn(hidden, o)

    @pl.when(step == pl.num_programs(0) - 1)
    def _():
        sent_ref[...] = acc[...].astype(BF16)


def back_kernel(scale, n_group, n_s, n_other, at_ref, *refs):
    pieces, refs = refs[:n_group], refs[n_group:]
    rate_refs, refs = refs[:n_s], refs[n_s:]
    w_gate, w_up, w_down = (ref[0] for ref in refs[:3])
    own_ref, other_refs = refs[3], refs[4 : 4 + n_other]
    outs, adj = refs[4 + n_other : -1], refs[-1]
    dim = pieces[0].shape[-1]

    @pl.when(pl.program_id(0) == 0)
    def _():
        adj[...] = (scale * total_of(own_ref, other_refs)).astype(BF16)

    k = stacked(pieces, 0)
    rate = tall_rates(at_ref, rate_refs, n_group, dim)
    scaled = (rate * stacked(pieces, 1).astype(F32)).astype(BF16)
    adj_gate, adj_up, adj_down = adj[:dim], adj[dim : 2 * dim], adj[2 * dim :]
    gate = mm(k, w_gate)
    up = mm(k, w_up)
    dhid = mm_nt(scaled, w_down)
    sig = sigmoid(gate)
    act = gate * sig
    rest = 1.0 - sig
    slope = sig * (1.0 + gate * rest)
    curve = sig * rest * (2.0 + gate * (1.0 - 2.0 * sig))
    hidden = (act * up).astype(BF16)
    dgate = (dhid * up * slope).astype(BF16)
    dup = (dhid * act).astype(BF16)
    back_dgate = mm(k, adj_gate)
    back_dup = mm(k, adj_up)
    back_hidden = mm_nt(scaled, adj_down)
    back_scaled = mm(hidden, adj_down)
    back_dhid = (back_dgate * up * slope + back_dup * act).astype(BF16)
    back_gate = (
        back_dgate * dhid * up * curve + (back_dup * dhid + back_hidden * up) * slope
    ).astype(BF16)
    back_upper = (back_dgate * dhid * slope + back_hidden * act).astype(BF16)
    grad_k = mm_nt(dgate, adj_gate) + mm_nt(dup, adj_up)
    grad_k = (grad_k + mm_nt(back_gate, w_gate) + mm_nt(back_upper, w_up)).astype(BF16)
    grad_v = (rate * (back_scaled + mm(back_dhid, w_down))).astype(BF16)
    rows = outs[0].shape[1]
    for j, ref in enumerate(outs):
        ref[0] = grad_k[j * rows : (j + 1) * rows]
        ref[1] = grad_v[j * rows : (j + 1) * rows]


def body(n_t, n_s, n_head, queries, key_tokens, values, out_grad, learn_rates, w_gate, w_up, w_down):
    rows, model = queries.shape
    n_group = n_head * n_s
    dim = model // (n_group * HEADS_HELD)
    held = range(HEADS_HELD)
    hops = [1 << i for i in range(n_t.bit_length() - 1)] if n_t & (n_t - 1) == 0 else None
    tile = min(rows, 128)
    grid = (rows // tile,)
    scale = 1.0 / math.sqrt(dim * rows * n_group * n_t)
    place = lax.axis_index("head") * n_s + lax.axis_index("s")
    at = jnp.stack([place, lax.axis_index("t")]).astype(jnp.int32)

    def partners(j):
        pairs = []
        for g in range(n_group):
            ends = [(x % n_s) * n_head + x // n_s for x in (g, g ^ j)]
            pairs.append(tuple(ends))
        return pairs

    params = pltpu.CompilerParams(
        dimension_semantics=("arbitrary",), vmem_limit_bytes=56 * 1024 * 1024
    )
    free = pl.BlockSpec(memory_space=pl.ANY)

    def call(kernel, grid, in_specs, out_specs, out_shape, scratch, *args, after=()):
        n_in = len(args)
        if after:
            inner = kernel

            def kernel(*refs):
                inner(*refs[: n_in + 1], *refs[n_in + 1 + len(after) :])

        return pl.pallas_call(
            kernel,
            out_shape=out_shape,
            grid_spec=pltpu.PrefetchScalarGridSpec(
                num_scalar_prefetch=1,
                grid=grid,
                in_specs=list(in_specs) + [free] * len(after),
                out_specs=out_specs,
                scratch_shapes=scratch,
            ),
            compiler_params=params,
        )(at, *args, *after)

    flat_spec = pl.BlockSpec((tile, model), lambda i, p: (i, 0))
    flat_shape = jax.ShapeDtypeStruct((rows, model), BF16)
    piece_specs = [pl.BlockSpec((2, tile, dim), lambda i, p: (0, i, 0))] * n_group

    def by_head(first, second):
        outs = call(
            functools.partial(by_head_kernel, n_group),
            grid,
            [flat_spec, flat_spec],
            piece_specs * HEADS_HELD,
            [jax.ShapeDtypeStruct((2, rows, dim), BF16)] * (n_group * HEADS_HELD),
            [],
            first,
            second,
        )
        return [outs[a * n_group : (a + 1) * n_group] for a in held]

    def swap(pieces):
        return [pieces[0]] + [
            lax.ppermute(pieces[j], ("s", "head"), partners(j))
            for j in range(1, n_group)
        ]

    def reduce(own, sent):
        if hops is None:
            return own, [lax.psum(sent, "t")]
        others = []
        for i, hop in enumerate(hops):
            if i:
                own = own + others.pop().astype(F32)
                sent = own.astype(BF16)
            others.append(lax.ppermute(sent, "t", [(j, j ^ hop) for j in range(n_t)]))
        return own, others

    sum_spec = pl.BlockSpec((3 * dim, dim), lambda i, p: (0, 0))
    sum_specs = [sum_spec, sum_spec]
    sum_shapes = [
        jax.ShapeDtypeStruct((3 * dim, dim), F32),
        jax.ShapeDtypeStruct((3 * dim, dim), BF16),
    ]

    def rate_specs(a):
        return [pl.BlockSpec((1, n_head, tile), lambda i, p: (a, 0, i))] * n_s

    def w_specs(a):
        spec = pl.BlockSpec(
            (1, dim, dim), lambda i, p: (HEADS_HELD * lax.rem(p[0], n_s) + a, 0, 0)
        )
        return [spec] * 3

    weights = (w_gate, w_up, w_down)
    kv = by_head(key_tokens, values)
    kv = [swap(kv[a]) for a in held]
    by_column = learn_rates.T.reshape(n_s, HEADS_HELD, n_head, rows)
    rates = []
    for j in range(n_s):
        piece = by_column[jnp.bitwise_xor(lax.axis_index("s"), j)]
        if j:
            piece = lax.ppermute(piece, "s", [(i, i ^ j) for i in range(n_s)])
        rates.append(piece)
    qo = by_head(queries, out_grad)
    qo = [swap(qo[a]) for a in held]

    def key_forward(a, after=()):
        own, sent = call(
            functools.partial(key_kernel, n_group, n_s),
            grid,
            piece_specs + rate_specs(a) + w_specs(a),
            sum_specs,
            sum_shapes,
            [],
            *kv[a],
            *rates,
            *weights,
            after=after,
        )
        return own, reduce(own, sent)

    def query_side(a, own, others, after=()):
        outs = call(
            functools.partial(query_kernel, scale, n_group, len(others)),
            grid,
            piece_specs + w_specs(a) + [sum_spec] * (1 + len(others)),
            [pl.BlockSpec((tile, dim), lambda i, p: (i, 0))] * n_group + sum_specs,
            [jax.ShapeDtypeStruct((rows, dim), BF16)] * n_group + sum_shapes,
            [pltpu.VMEM((3 * dim, dim), BF16)],
            *qo[a],
            *weights,
            own,
            *others,
            after=after,
        )
        grads, own, sent = outs[:n_group], outs[n_group], outs[n_group + 1]
        return own, reduce(own, sent), swap(grads)

    def key_back(a, own, others, after=()):
        outs = call(
            functools.partial(back_kernel, scale, n_group, n_s, len(others)),
            grid,
            piece_specs + rate_specs(a) + w_specs(a) + [sum_spec] * (1 + len(others)),
            piece_specs,
            [jax.ShapeDtypeStruct((2, rows, dim), BF16)] * n_group,
            [pltpu.VMEM((3 * dim, dim), BF16)],
            *kv[a],
            *rates,
            *weights,
            own,
            *others,
            after=after,
        )
        return outs[0], swap(outs)

    delta, sums, gq, gkv = ([None] * HEADS_HELD for _ in range(4))
    mark = ()
    for a in held:
        mark, delta[a] = key_forward(a, mark)
        mark = (mark,)
    for a in held:
        mark, sums[a], gq[a] = query_side(a, *delta[a], mark)
        mark = (mark,)
    for a in held:
        mark, gkv[a] = key_back(a, *sums[a], mark)
        mark = (mark,)
    grad_q = call(
        functools.partial(home_kernel, n_group, 1),
        grid,
        [pl.BlockSpec((tile, dim), lambda i, p: (i, 0))] * (HEADS_HELD * n_group),
        [flat_spec],
        [flat_shape],
        [],
        *gq[0],
        *gq[1],
        after=mark,
    )[0]
    grad_k, grad_v = call(
        functools.partial(home_kernel, n_group, 2),
        grid,
        piece_specs * HEADS_HELD,
        [flat_spec] * 2,
        [flat_shape] * 2,
        [],
        *gkv[0],
        *gkv[1],
    )
    return grad_q, grad_k, grad_v


def solution(mesh):
    n_tok, n_head = mesh.shape["tok"], mesh.shape["head"]

    def run(queries, key_tokens, values, out_grad, learn_rates, w_gate, w_up, w_down):
        n_s = w_gate.shape[0] // (n_head * HEADS_HELD)
        n_t = n_tok // n_s
        split = Mesh(mesh.devices.reshape(n_t, n_s, n_head), ("t", "s", "head"))
        tokens = P(("t", "s", "head"), None)
        weights = P("head", None, None)
        return jax.shard_map(
            functools.partial(body, n_t, n_s, n_head),
            mesh=split,
            in_specs=(tokens,) * 4 + (P(("t", "s"), "head"),) + (weights,) * 3,
            out_specs=(tokens,) * 3,
            check_vma=False,
        )(queries, key_tokens, values, out_grad, learn_rates, w_gate, w_up, w_down)


    return run
```

time: 272 us -> 257 us (0.945)
  starting transfers between devices: 98.7 us -> 67.2 us
  waiting for transfers between devices: 90.7 us -> 117 us
  Pallas kernels: 76.1 us -> 61.6 us
  other arithmetic: 0.59 us -> 4.51 us
    ppermute x24 -> x8, starting transfers between devices: 39.2 us -> 11.5 us  [reduce(): others.append(lax.ppermute(sent, 't', [(j, j ^ hop) for j in range(n_t)]))]
    ppermute x56, waiting for transfers between devices: 62 us -> 88.3 us  [swap(): lax.ppermute(pieces[j], ('s', 'head'), partners(j))]
    pallas_call x17 -> x10, Pallas kernels: 76.1 us -> 61.6 us  [call(): pl.pallas_call(kernel, out_shape=out_shape, grid_spec=pltpu.PrefetchScala...]
    convert_element_type x0 -> x4, other arithmetic: none -> 3.93 us  [reduce(): sent = own.astype(BF16)]
    ppermute x56, starting transfers between devices: 57.6 us -> 54.1 us  [swap(): lax.ppermute(pieces[j], ('s', 'head'), partners(j))]
    ppermute x24 -> x8, waiting for transfers between devices: 20.3 us -> 20.8 us  [reduce(): others.append(lax.ppermute(sent, 't', [(j, j ^ hop) for j in range(n_t)]))]
  transfers between devices with their start and end apart: 81 -> 65, of which waited for: 20 -> 19; matrix products, arithmetic and copies ran while one was open for 0% -> 2% of each run, Pallas kernels for 25% -> 20%
where the time goes in v4:
time: 257 us
  waiting for transfers between devices  117 us (46%)
  starting transfers between devices  67.2 us (26%)
  Pallas kernels  61.6 us (24%)
  local copies, waits for them, and re-layouts  4.68 us (2%)
  other arithmetic  4.51 us (2%)
    ppermute x56, waiting for transfers between devices, swap(): lax.ppermute(pieces[j], ('s', 'head'), partners(j))  88.3 us
    pallas_call x10, Pallas kernels, call(): pl.pallas_call(kernel, out_shape=out_shape, grid_spec=pltpu.PrefetchScala...  61.6 us
    ppermute x56, starting transfers between devices, swap(): lax.ppermute(pieces[j], ('s', 'head'), partners(j))  54.1 us
    ppermute x8, waiting for transfers between devices, reduce(): others.append(lax.ppermute(sent, 't', [(j, j ^ hop) for j in range(n_t)]))  20.8 us
    ppermute x8, starting transfers between devices, reduce(): others.append(lax.ppermute(sent, 't', [(j, j ^ hop) for j in range(n_t)]))  11.5 us
    ppermute x1, waiting for transfers between devices, body(): piece = lax.ppermute(piece, 's', [(i, i ^ j) for i in range(n_s)])  8.02 us
  transfers between devices with their start and end apart: 65, of which 19 were waited for; matrix products, arithmetic and copies ran while one was open for 2% of the time, Pallas kernels for 20%

profile of v4, /device:TPU:0, one launch (start us, length us, event | category | flops | bytes accessed | tf_op | source)
XLA Modules:
  0.0 256.8 jit_solution(12576114027222880645)
XLA Ops:
  1.2 4.6 %shard_map.104 = (bf16[2,256,256]{2,1,0:T(8,128)(2,1)}, bf16[2,256,256]{2,1,0:T(8,128)(2,1)}, bf16[2,256,256]{2,1,0:T(8,128)(2,1)}, bf16[2,256,256]{2,1,0:T(8,12...) custom-call(s32[2]{0:T(128)} %pad_add_fusion.at_ref.refs_0_, ...), custom_call_target="tpu_custom_call" | custom-call | tf_op jit(solution)/shard_map/pallas_call | solution.py:229
  5.8 3.0 %collective-permute-start.7 = (bf16[2,256,256]{2,1,0:T(8,128)(2,1)}, bf16[2,256,256]{2,1,0:T(8,128)(2,1)S(1)}, u32[]{:S(2)}, u32[]{:S(2)}) collective-permute-start(bf16[2,256,256]{2,1,0:T(8,128)(2,1)} %get-tuple-element.86), channel_id=1, source_target_pairs={{0,4},{4,0},{1,5},{5,1},{2,6},{6,2},{3,7},{7,3},{8,12},{12,8},{9,1... | collective-permute-start | bytes 786440 | tf_op jit(solution)/shard_map/ppermute | solution.py:261
  9.1 2.0 collective-permute-start.10
  11.7 1.5 collective-permute-start.14
  13.2 8.0 %collective-permute-done.14.refs_9_.refs_10_ = f32[2,4,256]{2,1,0:T(4,128)S(1)} collective-permute-done((f32[2,4,256]{2,1,0:T(4,128)S(1)}, f32[2,4,256]{2,1,0:T(4,128)S(1)}, u32[]{:S(2)}, u32[]{:S(2)}) %collective-permute-start.14) | collective-permute-done | bytes 8224 | tf_op jit(solution)/shard_map/ppermute | solution.py:300
  21.2 2.7 %collective-permute-start.11 = (bf16[2,256,256]{2,1,0:T(8,128)(2,1)}, bf16[2,256,256]{2,1,0:T(8,128)(2,1)S(1)}, u32[]{:S(2)}, u32[]{:S(2)}) collective-permute-start(bf16[2,256,256]{2,1,0:T(8,128)(2,1)} %get-tuple-element.90), channel_id=1, source_target_pairs={{0,6},{4,2},{1,7},{5,3},{2,4},{6,0},{3,5},{7,1},{8,14},{12,10},{9,... | collective-permute-start | bytes 786440 | tf_op jit(solution)/shard_map/ppermute | solution.py:261
  23.9 1.7 collective-permute-start.13
  25.6 1.5 collective-permute-start.17
  27.1 4.1 %collective-permute-done.11.refs_5_.refs_6_ = bf16[2,256,256]{2,1,0:T(8,128)(2,1)S(1)} collective-permute-done((bf16[2,256,256]{2,1,0:T(8,128)(2,1)}, bf16[2,256,256]{2,1,0:T(8,128)(2,1)S(1)}, u32[]{:S(2)}, u32[]{:S(2)}) %collective-permute-start.11) | collective-permute-done | bytes 262176 | tf_op jit(solution)/shard_map/ppermute | solution.py:261
  31.3 9.6 %collective-permute-done.12.refs_6_.refs_7_ = bf16[2,256,256]{2,1,0:T(8,128)(2,1)S(1)} collective-permute-done((bf16[2,256,256]{2,1,0:T(8,128)(2,1)}, bf16[2,256,256]{2,1,0:T(8,128)(2,1)S(1)}, u32[]{:S(2)}, u32[]{:S(2)}) %collective-permute-start.12) | collective-permute-done | bytes 262176 | tf_op jit(solution)/shard_map/ppermute | solution.py:261
  44.5 6.0 %shard_map.105 = (f32[768,256]{1,0:T(8,128)}, bf16[768,256]{1,0:T(8,128)(2,1)}) custom-call(s32[2]{0:T(128)} %pad_add_fusion.at_ref.refs_0_, bf16[2,256,256]{2,1,0:T(8,128)(2,1)} %get-tuple-element.85.refs_0_.refs_1_, bf16[2,256,256]{2,1,0:T(8,128)(2,1)} %copy-done.4, bf16[2,256,256]{2,1,0:T(8,128)(2,1)} %copy-done.5, bf16[2,256,256]{2,1,0:T(8,128)(2,1)} %copy-done.6, ...), custom_call_target="tpu_custom_call" | custom-call | tf_op jit(solution)/shard_map/pallas_call | solution.py:229
  50.5 1.6 collective-permute-start.15
  53.2 4.5 %shard_map.103 = (bf16[2,256,256]{2,1,0:T(8,128)(2,1)}, bf16[2,256,256]{2,1,0:T(8,128)(2,1)}, bf16[2,256,256]{2,1,0:T(8,128)(2,1)}, bf16[2,256,256]{2,1,0:T(8,12...) custom-call(s32[2]{0:T(128)} %pad_add_fusion.at_ref.refs_0_, ...), custom_call_target="tpu_custom_call" | custom-call | tf_op jit(solution)/shard_map/pallas_call | solution.py:229
  57.8 5.1 %collective-permute-start = (bf16[2,256,256]{2,1,0:T(8,128)(2,1)}, bf16[2,256,256]{2,1,0:T(8,128)(2,1)S(1)}, u32[]{:S(2)}, u32[]{:S(2)}) collective-permute-start(bf16[2,256,256]{2,1,0:T(8,128)(2,1)} %get-tuple-element.78), channel_id=1, source_target_pairs={{0,4},{4,0},{1,5},{5,1},{2,6},{6,2},{3,7},{7,3},{8,12},{12,8},{9,1... | collective-permute-start | bytes 786440 | tf_op jit(solution)/shard_map/ppermute | solution.py:261
  62.9 2.4 collective-permute-done.22.refs_7_
  65.3 2.0 collective-permute-start.2
  67.3 1.6 collective-permute-start.3
  69.0 6.2 %shard_map.106 = (f32[768,256]{1,0:T(8,128)}, bf16[768,256]{1,0:T(8,128)(2,1)}) custom-call(s32[2]{0:T(128)} %pad_add_fusion.at_ref.refs_0_, bf16[2,256,256]{2,1,0:T(8,128)(2,1)} %get-tuple-element.95.refs_1_, bf16[2,256,256]{2,1,0:T(8,128)(2,1)} %copy-done.11, bf16[2,256,256]{2,1,0:T(8,128)(2,1)} %copy-done.12, bf16[2,256,256]{2,1,0:T(8,128)(2,1)} %copy-done.13, ...), custom_call_target="tpu_custom_call" | custom-call | tf_op jit(solution)/shard_map/pallas_call | solution.py:229
  76.3 1.6 collective-permute-start.38
  77.9 2.1 collective-permute-start.6
  81.0 2.6 %collective-permute-start.16 = (bf16[768,256]{1,0:T(8,128)(2,1)S(1)}, bf16[768,256]{1,0:T(8,128)(2,1)S(1)}, u32[]{:S(2)}, u32[]{:S(2)}) collective-permute-start(bf16[768,256]{1,0:T(8,128)(2,1)S(1)} %get-tuple-element.157), channel_id=1, source_target_pairs={{0,16},{8,24},{16,0},{24,8},{1,17},{9,25},{17,1},{25,9},{2,18},{10... | collective-permute-start | bytes 1179656 | tf_op jit(solution)/shard_map/ppermute | solution.py:273
  83.6 1.9 collective-permute-done.4.refs_6_
  86.0 8.9 %collective-permute-done.5.refs_7_ = bf16[2,256,256]{2,1,0:T(8,128)(2,1)S(1)} collective-permute-done((bf16[2,256,256]{2,1,0:T(8,128)(2,1)S(1)}, bf16[2,256,256]{2,1,0:T(8,128)(2,1)S(1)}, u32[]{:S(2)}, u32[]{:S(2)}) %collective-permute-start.5) | collective-permute-done | bytes 262176 | tf_op jit(solution)/shard_map/ppermute | solution.py:261
  98.0 3.5 %collective-permute-done.16.refs_13_ = bf16[768,256]{1,0:T(8,128)(2,1)S(1)} collective-permute-done((bf16[768,256]{1,0:T(8,128)(2,1)S(1)}, bf16[768,256]{1,0:T(8,128)(2,1)S(1)}, u32[]{:S(2)}, u32[]{:S(2)}) %collective-permute-start.16) | collective-permute-done | bytes 393248 | tf_op jit(solution)/shard_map/ppermute | solution.py:273
  102.2 7.0 %shard_map.107 = (bf16[256,256]{1,0:T(8,128)(2,1)}, bf16[256,256]{1,0:T(8,128)(2,1)}, bf16[256,256]{1,0:T(8,128)(2,1)}, bf16[256,256]{1,0:T(8,128)(2,1)}, bf16[2...) custom-call(s32[2]{0:T(128)} %pad_add_fusion.at_ref.refs_0_, ...), custom_call_target="tpu_custom_call" | custom-call | tf_op jit(solution)/shard_map/pallas_call | solution.py:229
  109.3 2.4 collective-permute-start.49
  112.8 2.5 collective-permute-start.37
  115.2 6.7 %collective-permute-done.35.refs_6_ = bf16[2,256,256]{2,1,0:T(8,128)(2,1)S(1)} collective-permute-done((bf16[2,256,256]{2,1,0:T(8,128)(2,1)S(1)}, bf16[2,256,256]{2,1,0:T(8,128)(2,1)S(1)}, u32[]{:S(2)}, u32[]{:S(2)}) %collective-permute-start.35) | collective-permute-done | bytes 262176 | tf_op jit(solution)/shard_map/ppermute | solution.py:261
  121.9 8.9 %collective-permute-done.36.refs_7_ = bf16[2,256,256]{2,1,0:T(8,128)(2,1)S(1)} collective-permute-done((bf16[2,256,256]{2,1,0:T(8,128)(2,1)S(1)}, bf16[2,256,256]{2,1,0:T(8,128)(2,1)S(1)}, u32[]{:S(2)}, u32[]{:S(2)}) %collective-permute-start.36) | collective-permute-done | bytes 262176 | tf_op jit(solution)/shard_map/ppermute | solution.py:261
  131.7 7.2 %shard_map.108 = (bf16[256,256]{1,0:T(8,128)(2,1)}, bf16[256,256]{1,0:T(8,128)(2,1)}, bf16[256,256]{1,0:T(8,128)(2,1)}, bf16[256,256]{1,0:T(8,128)(2,1)}, bf16[2...) custom-call(s32[2]{0:T(128)} %pad_add_fusion.at_ref.refs_0_, ...), custom_call_target="tpu_custom_call" | custom-call | tf_op jit(solution)/shard_map/pallas_call | solution.py:229
  139.9 1.6 collective-permute-start.26
  142.7 3.1 %collective-permute-done.24.refs_2_ = bf16[256,256]{1,0:T(8,128)(2,1)S(1)} collective-permute-done((bf16[256,256]{1,0:T(8,128)(2,1)S(1)}, bf16[256,256]{1,0:T(8,128)(2,1)S(1)}, u32[]{:S(2)}, u32[]{:S(2)}) %collective-permute-start.24) | collective-permute-done | bytes 131104 | tf_op jit(solution)/shard_map/ppermute | solution.py:261
  146.3 4.1 %collective-permute-done.47 = bf16[768,256]{1,0:T(8,128)(2,1)S(1)} collective-permute-done((bf16[768,256]{1,0:T(8,128)(2,1)}, bf16[768,256]{1,0:T(8,128)(2,1)S(1)}, u32[]{:S(2)}, u32[]{:S(2)}) %collective-permute-start.47) | collective-permute-done | bytes 393248 | tf_op jit(solution)/shard_map/ppermute | solution.py:273
  152.3 2.0 collective-permute-start.48
  155.8 5.3 %collective-permute-done.30.refs_8_ = bf16[256,256]{1,0:T(8,128)(2,1)S(1)} collective-permute-done((bf16[256,256]{1,0:T(8,128)(2,1)S(1)}, bf16[256,256]{1,0:T(8,128)(2,1)S(1)}, u32[]{:S(2)}, u32[]{:S(2)}) %collective-permute-start.30) | collective-permute-done | bytes 131104 | tf_op jit(solution)/shard_map/ppermute | solution.py:261
  162.1 2.8 %collective-permute-start.44 = (bf16[256,256]{1,0:T(8,128)(2,1)S(1)}, bf16[256,256]{1,0:T(8,128)(2,1)S(1)}, u32[]{:S(2)}, u32[]{:S(2)}) collective-permute-start(bf16[256,256]{1,0:T(8,128)(2,1)S(1)} %copy-done.83), channel_id=1, source_target_pairs={{0,6},{4,2},{1,7},{5,3},{2,4},{6,0},{3,5},{7,1},{8,14},{12,10},{9,... | collective-permute-start | bytes 393224 | tf_op jit(solution)/shard_map/ppermute | solution.py:261
  164.9 13.3 %collective-permute-done.50.refs_15_ = bf16[768,256]{1,0:T(8,128)(2,1)S(1)} collective-permute-done((bf16[768,256]{1,0:T(8,128)(2,1)S(1)}, bf16[768,256]{1,0:T(8,128)(2,1)S(1)}, u32[]{:S(2)}, u32[]{:S(2)}) %collective-permute-start.50) | collective-permute-done | bytes 393248 | tf_op jit(solution)/shard_map/ppermute | solution.py:273
  179.0 9.1 %shard_map.109 = (bf16[2,256,256]{2,1,0:T(8,128)(2,1)}, bf16[2,256,256]{2,1,0:T(8,128)(2,1)}, bf16[2,256,256]{2,1,0:T(8,128)(2,1)}, bf16[2,256,256]{2,1,0:T(8,12...) custom-call(s32[2]{0:T(128)} %pad_add_fusion.at_ref.refs_0_, ...), custom_call_target="tpu_custom_call" | custom-call | tf_op jit(solution)/shard_map/pallas_call | solution.py:229
  192.5 9.0 %shard_map.110 = (bf16[2,256,256]{2,1,0:T(8,128)(2,1)}, bf16[2,256,256]{2,1,0:T(8,128)(2,1)}, bf16[2,256,256]{2,1,0:T(8,128)(2,1)}, bf16[2,256,256]{2,1,0:T(8,12...) custom-call(s32[2]{0:T(128)} %pad_add_fusion.at_ref.refs_0_, ...), custom_call_target="tpu_custom_call" | custom-call | tf_op jit(solution)/shard_map/pallas_call | solution.py:229
  201.6 3.9 %collective-permute-done.46.refs_16_ = bf16[256,256]{1,0:T(8,128)(2,1)S(1)} collective-permute-done((bf16[256,256]{1,0:T(8,128)(2,1)S(1)}, bf16[256,256]{1,0:T(8,128)(2,1)S(1)}, u32[]{:S(2)}, u32[]{:S(2)}) %collective-permute-start.46) | collective-permute-done | bytes 131104 | tf_op jit(solution)/shard_map/ppermute | solution.py:261
  205.5 1.7 collective-permute-start.56
  209.6 6.0 %collective-permute-done.55.refs_5_ = bf16[2,256,256]{2,1,0:T(8,128)(2,1)S(1)} collective-permute-done((bf16[2,256,256]{2,1,0:T(8,128)(2,1)S(1)}, bf16[2,256,256]{2,1,0:T(8,128)(2,1)S(1)}, u32[]{:S(2)}, u32[]{:S(2)}) %collective-permute-start.55) | collective-permute-done | bytes 262176 | tf_op jit(solution)/shard_map/ppermute | solution.py:261
  215.6 9.0 %collective-permute-done.56.refs_6_ = bf16[2,256,256]{2,1,0:T(8,128)(2,1)S(1)} collective-permute-done((bf16[2,256,256]{2,1,0:T(8,128)(2,1)S(1)}, bf16[2,256,256]{2,1,0:T(8,128)(2,1)S(1)}, u32[]{:S(2)}, u32[]{:S(2)}) %collective-permute-start.56) | collective-permute-done | bytes 262176 | tf_op jit(solution)/shard_map/ppermute | solution.py:261
  224.7 1.9 collective-permute-start.61
  229.4 3.4 %shard_map.111 = bf16[256,4096]{1,0:T(8,128)(2,1)} custom-call(s32[2]{0:T(128)} %pad_add_fusion.at_ref.refs_0_, bf16[256,256]{1,0:T(8,128)(2,1)} %get-tuple-element.104.refs_1_, bf16[256,256]{1,0:T(8,128)(2,1)} %copy-done.51, bf16[256,256]{1,0:T(8,128)(2,1)} %copy-done.52, bf16[256,256]{1,0:T(8,128)(2,1)} %copy-done.53, bf16[256,256]{1,0:T(8,128)(2,1)} %copy-done.54, ...), custom_call_target="tpu_custom_call" | custom-call | tf_op jit(solution)/shard_map/pallas_call | solution.py:229
  232.9 12.4 %collective-permute-done.61.refs_12_ = bf16[2,256,256]{2,1,0:T(8,128)(2,1)S(1)} collective-permute-done((bf16[2,256,256]{2,1,0:T(8,128)(2,1)}, bf16[2,256,256]{2,1,0:T(8,128)(2,1)S(1)}, u32[]{:S(2)}, u32[]{:S(2)}) %collective-permute-start.61) | collective-permute-done | bytes 262176 | tf_op jit(solution)/shard_map/ppermute | solution.py:261
  245.3 5.3 %collective-permute-done.63.refs_14_ = bf16[2,256,256]{2,1,0:T(8,128)(2,1)S(1)} collective-permute-done((bf16[2,256,256]{2,1,0:T(8,128)(2,1)}, bf16[2,256,256]{2,1,0:T(8,128)(2,1)S(1)}, u32[]{:S(2)}, u32[]{:S(2)}) %collective-permute-start.63) | collective-permute-done | bytes 262176 | tf_op jit(solution)/shard_map/ppermute | solution.py:261
  252.0 4.6 %shard_map.112 = (bf16[256,4096]{1,0:T(8,128)(2,1)}, bf16[256,4096]{1,0:T(8,128)(2,1)}) custom-call(s32[2]{0:T(128)} %pad_add_fusion.at_ref.refs_0_, bf16[2,256,256]{2,1,0:T(8,128)(2,1)} %get-tuple-element.133.refs_16_.refs_0_, bf16[2,256,256]{2,1,0:T(8,128)(2,1)} %copy-done.22, bf16[2,256,256]{2,1,0:T(8,128)(2,1)} %copy-done.23, ...), custom_call_target="tpu_custom_call" | custom-call | tf_op jit(solution)/shard_map/pallas_call | solution.py:229
  (287 shorter events, 33.4 us)
Async XLA Ops:
  5.8 18.0 %collective-permute-start.7 = (bf16[2,256,256]{2,1,0:T(8,128)(2,1)}, bf16[2,256,256]{2,1,0:T(8,128)(2,1)S(1)}, u32[]{:S(2)}, u32[]{:S(2)}) collective-permute-start(bf16[2,256,256]{2,1,0:T(8,128)(2,1)} %get-tuple-element.86), channel_id=1, source_target_pairs={{0,4},{4,0},{1,5},{5,1},{2,6},{6,2},{3,7},{7,3},{8,12},{12,8},{9,1... | collective-permute-start | bytes 786440 | tf_op jit(solution)/shard_map/ppermute | solution.py:261
  8.9 15.0 %collective-permute-start.8 = (bf16[2,256,256]{2,1,0:T(8,128)(2,1)}, bf16[2,256,256]{2,1,0:T(8,128)(2,1)S(1)}, u32[]{:S(2)}, u32[]{:S(2)}) collective-permute-start(bf16[2,256,256]{2,1,0:T(8,128)(2,1)} %get-tuple-element.87), channel_id=1, source_target_pairs={{0,1},{4,5},{1,0},{5,4},{2,3},{6,7},{3,2},{7,6},{8,9},{12,13},{9,8... | collective-permute-start | bytes 786440 | tf_op jit(solution)/shard_map/ppermute | solution.py:261
  8.9 16.7 %collective-permute-start.9 = (bf16[2,256,256]{2,1,0:T(8,128)(2,1)}, bf16[2,256,256]{2,1,0:T(8,128)(2,1)S(1)}, u32[]{:S(2)}, u32[]{:S(2)}) collective-permute-start(bf16[2,256,256]{2,1,0:T(8,128)(2,1)} %get-tuple-element.88), channel_id=1, source_target_pairs={{0,5},{4,1},{1,4},{5,0},{2,7},{6,3},{3,6},{7,2},{8,13},{12,9},{9,1... | collective-permute-start | bytes 786440 | tf_op jit(solution)/shard_map/ppermute | solution.py:261
  9.1 18.0 %collective-permute-start.10 = (bf16[2,256,256]{2,1,0:T(8,128)(2,1)}, bf16[2,256,256]{2,1,0:T(8,128)(2,1)S(1)}, u32[]{:S(2)}, u32[]{:S(2)}) collective-permute-start(bf16[2,256,256]{2,1,0:T(8,128)(2,1)} %get-tuple-element.89), channel_id=1, source_target_pairs={{0,2},{4,6},{1,3},{5,7},{2,0},{6,4},{3,1},{7,5},{8,10},{12,14},{9,... | collective-permute-start | bytes 786440 | tf_op jit(solution)/shard_map/ppermute | solution.py:261
  23.9 16.9 %collective-permute-start.12 = (bf16[2,256,256]{2,1,0:T(8,128)(2,1)}, bf16[2,256,256]{2,1,0:T(8,128)(2,1)S(1)}, u32[]{:S(2)}, u32[]{:S(2)}) collective-permute-start(bf16[2,256,256]{2,1,0:T(8,128)(2,1)} %get-tuple-element.91), channel_id=1, source_target_pairs={{0,3},{4,7},{1,2},{5,6},{2,1},{6,5},{3,0},{7,4},{8,11},{12,15},{9,... | collective-permute-start | bytes 786440 | tf_op jit(solution)/shard_map/ppermute | solution.py:261
  23.9 18.4 %collective-permute-start.13 = (bf16[2,256,256]{2,1,0:T(8,128)(2,1)}, bf16[2,256,256]{2,1,0:T(8,128)(2,1)S(1)}, u32[]{:S(2)}, u32[]{:S(2)}) collective-permute-start(bf16[2,256,256]{2,1,0:T(8,128)(2,1)} %get-tuple-element.92), channel_id=1, source_target_pairs={{0,7},{4,3},{1,6},{5,2},{2,5},{6,1},{3,4},{7,0},{8,15},{12,11},{9,... | collective-permute-start | bytes 786440 | tf_op jit(solution)/shard_map/ppermute | solution.py:261
  25.6 18.1 %collective-permute-start.17 = (bf16[2,256,256]{2,1,0:T(8,128)(2,1)}, bf16[2,256,256]{2,1,0:T(8,128)(2,1)S(1)}, u32[]{:S(2)}, u32[]{:S(2)}) collective-permute-start(bf16[2,256,256]{2,1,0:T(8,128)(2,1)} %get-tuple-element.96), channel_id=1, source_target_pairs={{0,4},{4,0},{1,5},{5,1},{2,6},{6,2},{3,7},{7,3},{8,12},{12,8},{9,1... | collective-permute-start | bytes 786440 | tf_op jit(solution)/shard_map/ppermute | solution.py:261
  27.1 23.4 %collective-permute-start.18 = (bf16[2,256,256]{2,1,0:T(8,128)(2,1)}, bf16[2,256,256]{2,1,0:T(8,128)(2,1)S(1)}, u32[]{:S(2)}, u32[]{:S(2)}) collective-permute-start(bf16[2,256,256]{2,1,0:T(8,128)(2,1)} %get-tuple-element.97), channel_id=1, source_target_pairs={{0,1},{4,5},{1,0},{5,4},{2,3},{6,7},{3,2},{7,6},{8,9},{12,13},{9,8... | collective-permute-start | bytes 786440 | tf_op jit(solution)/shard_map/ppermute | solution.py:261
  31.2 20.9 %collective-permute-start.19 = (bf16[2,256,256]{2,1,0:T(8,128)(2,1)}, bf16[2,256,256]{2,1,0:T(8,128)(2,1)S(1)}, u32[]{:S(2)}, u32[]{:S(2)}) collective-permute-start(bf16[2,256,256]{2,1,0:T(8,128)(2,1)} %get-tuple-element.98), channel_id=1, source_target_pairs={{0,5},{4,1},{1,4},{5,0},{2,7},{6,3},{3,6},{7,2},{8,13},{12,9},{9,1... | collective-permute-start | bytes 786440 | tf_op jit(solution)/shard_map/ppermute | solution.py:261
  40.8 17.0 %collective-permute-start.20 = (bf16[2,256,256]{2,1,0:T(8,128)(2,1)}, bf16[2,256,256]{2,1,0:T(8,128)(2,1)S(1)}, u32[]{:S(2)}, u32[]{:S(2)}) collective-permute-start(bf16[2,256,256]{2,1,0:T(8,128)(2,1)} %get-tuple-element.99), channel_id=1, source_target_pairs={{0,2},{4,6},{1,3},{5,7},{2,0},{6,4},{3,1},{7,5},{8,10},{12,14},{9,... | collective-permute-start | bytes 786440 | tf_op jit(solution)/shard_map/ppermute | solution.py:261
  42.3 20.6 %collective-permute-start.21 = (bf16[2,256,256]{2,1,0:T(8,128)(2,1)}, bf16[2,256,256]{2,1,0:T(8,128)(2,1)S(1)}, u32[]{:S(2)}, u32[]{:S(2)}) collective-permute-start(bf16[2,256,256]{2,1,0:T(8,128)(2,1)} %get-tuple-element.100), channel_id=1, source_target_pairs={{0,6},{4,2},{1,7},{5,3},{2,4},{6,0},{3,5},{7,1},{8,14},{12,10},{9,... | collective-permute-start | bytes 786440 | tf_op jit(solution)/shard_map/ppermute | solution.py:261
  43.8 21.6 %collective-permute-start.22 = (bf16[2,256,256]{2,1,0:T(8,128)(2,1)}, bf16[2,256,256]{2,1,0:T(8,128)(2,1)S(1)}, u32[]{:S(2)}, u32[]{:S(2)}) collective-permute-start(bf16[2,256,256]{2,1,0:T(8,128)(2,1)} %get-tuple-element.101), channel_id=1, source_target_pairs={{0,3},{4,7},{1,2},{5,6},{2,1},{6,5},{3,0},{7,4},{8,11},{12,15},{9,... | collective-permute-start | bytes 786440 | tf_op jit(solution)/shard_map/ppermute | solution.py:261
  50.5 27.4 %collective-permute-start.15 = (bf16[768,256]{1,0:T(8,128)(2,1)}, bf16[768,256]{1,0:T(8,128)(2,1)S(1)}, u32[]{:S(2)}, u32[]{:S(2)}) collective-permute-start(bf16[768,256]{1,0:T(8,128)(2,1)} %get-tuple-element.94), channel_id=1, source_target_pairs={{0,8},{8,0},{16,24},{24,16},{1,9},{9,1},{17,25},{25,17},{2,10},{10... | collective-permute-start | bytes 1179656 | tf_op jit(solution)/shard_map/ppermute | solution.py:273
  52.2 15.1 %collective-permute-start.23 = (bf16[2,256,256]{2,1,0:T(8,128)(2,1)S(1)}, bf16[2,256,256]{2,1,0:T(8,128)(2,1)S(1)}, u32[]{:S(2)}, u32[]{:S(2)}) collective-permute-start(bf16[2,256,256]{2,1,0:T(8,128)(2,1)S(1)} %copy-done.69), channel_id=1, source_target_pairs={{0,7},{4,3},{1,6},{5,2},{2,5},{6,1},{3,4},{7,0},{8,15},{12,11},{9,... | collective-permute-start | bytes 786440 | tf_op jit(solution)/shard_map/ppermute | solution.py:261
  57.8 17.4 %collective-permute-start = (bf16[2,256,256]{2,1,0:T(8,128)(2,1)}, bf16[2,256,256]{2,1,0:T(8,128)(2,1)S(1)}, u32[]{:S(2)}, u32[]{:S(2)}) collective-permute-start(bf16[2,256,256]{2,1,0:T(8,128)(2,1)} %get-tuple-element.78), channel_id=1, source_target_pairs={{0,4},{4,0},{1,5},{5,1},{2,6},{6,2},{3,7},{7,3},{8,12},{12,8},{9,1... | collective-permute-start | bytes 786440 | tf_op jit(solution)/shard_map/ppermute | solution.py:261
  62.9 13.0 %collective-permute-start.1 = (bf16[2,256,256]{2,1,0:T(8,128)(2,1)}, bf16[2,256,256]{2,1,0:T(8,128)(2,1)S(1)}, u32[]{:S(2)}, u32[]{:S(2)}) collective-permute-start(bf16[2,256,256]{2,1,0:T(8,128)(2,1)} %get-tuple-element.79), channel_id=1, source_target_pairs={{0,1},{4,5},{1,0},{5,4},{2,3},{6,7},{3,2},{7,6},{8,9},{12,13},{9,8... | collective-permute-start | bytes 786440 | tf_op jit(solution)/shard_map/ppermute | solution.py:261
  67.3 13.6 %collective-permute-start.3 = (bf16[2,256,256]{2,1,0:T(8,128)(2,1)}, bf16[2,256,256]{2,1,0:T(8,128)(2,1)S(1)}, u32[]{:S(2)}, u32[]{:S(2)}) collective-permute-start(bf16[2,256,256]{2,1,0:T(8,128)(2,1)} %get-tuple-element.81), channel_id=1, source_target_pairs={{0,2},{4,6},{1,3},{5,7},{2,0},{6,4},{3,1},{7,5},{8,10},{12,14},{9,... | collective-permute-start | bytes 786440 | tf_op jit(solution)/shard_map/ppermute | solution.py:261
  75.9 19.0 %collective-permute-start.5 = (bf16[2,256,256]{2,1,0:T(8,128)(2,1)S(1)}, bf16[2,256,256]{2,1,0:T(8,128)(2,1)S(1)}, u32[]{:S(2)}, u32[]{:S(2)}) collective-permute-start(bf16[2,256,256]{2,1,0:T(8,128)(2,1)S(1)} %copy-done.78), channel_id=1, source_target_pairs={{0,3},{4,7},{1,2},{5,6},{2,1},{6,5},{3,0},{7,4},{8,11},{12,15},{9,... | collective-permute-start | bytes 786440 | tf_op jit(solution)/shard_map/ppermute | solution.py:261
  76.3 19.7 %collective-permute-start.38 = (bf16[768,256]{1,0:T(8,128)(2,1)}, bf16[768,256]{1,0:T(8,128)(2,1)S(1)}, u32[]{:S(2)}, u32[]{:S(2)}) collective-permute-start(bf16[768,256]{1,0:T(8,128)(2,1)} %get-tuple-element.120), channel_id=1, source_target_pairs={{0,8},{8,0},{16,24},{24,16},{1,9},{9,1},{17,25},{25,17},{2,10},{10... | collective-permute-start | bytes 1179656 | tf_op jit(solution)/shard_map/ppermute | solution.py:273
  77.9 17.1 %collective-permute-start.6 = (bf16[2,256,256]{2,1,0:T(8,128)(2,1)S(1)}, bf16[2,256,256]{2,1,0:T(8,128)(2,1)S(1)}, u32[]{:S(2)}, u32[]{:S(2)}) collective-permute-start(bf16[2,256,256]{2,1,0:T(8,128)(2,1)S(1)} %copy-done.77), channel_id=1, source_target_pairs={{0,7},{4,3},{1,6},{5,2},{2,5},{6,1},{3,4},{7,0},{8,15},{12,11},{9,... | collective-permute-start | bytes 786440 | tf_op jit(solution)/shard_map/ppermute | solution.py:261
  81.0 20.5 %collective-permute-start.16 = (bf16[768,256]{1,0:T(8,128)(2,1)S(1)}, bf16[768,256]{1,0:T(8,128)(2,1)S(1)}, u32[]{:S(2)}, u32[]{:S(2)}) collective-permute-start(bf16[768,256]{1,0:T(8,128)(2,1)S(1)} %get-tuple-element.157), channel_id=1, source_target_pairs={{0,16},{8,24},{16,0},{24,8},{1,17},{9,25},{17,1},{25,9},{2,18},{10... | collective-permute-start | bytes 1179656 | tf_op jit(solution)/shard_map/ppermute | solution.py:273
  85.5 23.8 %collective-permute-start.31 = (bf16[2,256,256]{2,1,0:T(8,128)(2,1)S(1)}, bf16[2,256,256]{2,1,0:T(8,128)(2,1)S(1)}, u32[]{:S(2)}, u32[]{:S(2)}) collective-permute-start(bf16[2,256,256]{2,1,0:T(8,128)(2,1)S(1)} %copy-done.73), channel_id=1, source_target_pairs={{0,4},{4,0},{1,5},{5,1},{2,6},{6,2},{3,7},{7,3},{8,12},{12,8},{9,1... | collective-permute-start | bytes 786440 | tf_op jit(solution)/shard_map/ppermute | solution.py:261
  94.9 16.8 %collective-permute-start.32 = (bf16[2,256,256]{2,1,0:T(8,128)(2,1)S(1)}, bf16[2,256,256]{2,1,0:T(8,128)(2,1)S(1)}, u32[]{:S(2)}, u32[]{:S(2)}) collective-permute-start(bf16[2,256,256]{2,1,0:T(8,128)(2,1)S(1)} %copy-done.72), channel_id=1, source_target_pairs={{0,1},{4,5},{1,0},{5,4},{2,3},{6,7},{3,2},{7,6},{8,9},{12,13},{9,8... | collective-permute-start | bytes 786440 | tf_op jit(solution)/shard_map/ppermute | solution.py:261
  95.0 17.6 %collective-permute-start.33 = (bf16[2,256,256]{2,1,0:T(8,128)(2,1)S(1)}, bf16[2,256,256]{2,1,0:T(8,128)(2,1)S(1)}, u32[]{:S(2)}, u32[]{:S(2)}) collective-permute-start(bf16[2,256,256]{2,1,0:T(8,128)(2,1)S(1)} %copy-done.71), channel_id=1, source_target_pairs={{0,5},{4,1},{1,4},{5,0},{2,7},{6,3},{3,6},{7,2},{8,13},{12,9},{9,1... | collective-permute-start | bytes 786440 | tf_op jit(solution)/shard_map/ppermute | solution.py:261
  96.0 16.7 %collective-permute-start.34 = (bf16[2,256,256]{2,1,0:T(8,128)(2,1)S(1)}, bf16[2,256,256]{2,1,0:T(8,128)(2,1)S(1)}, u32[]{:S(2)}, u32[]{:S(2)}) collective-permute-start(bf16[2,256,256]{2,1,0:T(8,128)(2,1)S(1)} %copy-done.70), channel_id=1, source_target_pairs={{0,2},{4,6},{1,3},{5,7},{2,0},{6,4},{3,1},{7,5},{8,10},{12,14},{9,... | collective-permute-start | bytes 786440 | tf_op jit(solution)/shard_map/ppermute | solution.py:261
  101.5 29.4 %collective-permute-start.39 = (bf16[768,256]{1,0:T(8,128)(2,1)S(1)}, bf16[768,256]{1,0:T(8,128)(2,1)S(1)}, u32[]{:S(2)}, u32[]{:S(2)}) collective-permute-start(bf16[768,256]{1,0:T(8,128)(2,1)S(1)} %get-tuple-element.155), channel_id=1, source_target_pairs={{0,16},{8,24},{16,0},{24,8},{1,17},{9,25},{17,1},{25,9},{2,18},{10... | collective-permute-start | bytes 1179656 | tf_op jit(solution)/shard_map/ppermute | solution.py:273
  109.3 32.2 %collective-permute-start.49 = (bf16[768,256]{1,0:T(8,128)(2,1)}, bf16[768,256]{1,0:T(8,128)(2,1)S(1)}, u32[]{:S(2)}, u32[]{:S(2)}) collective-permute-start(bf16[768,256]{1,0:T(8,128)(2,1)} %get-tuple-element.132), channel_id=1, source_target_pairs={{0,8},{8,0},{16,24},{24,16},{1,9},{9,1},{17,25},{25,17},{2,10},{10... | collective-permute-start | bytes 1179656 | tf_op jit(solution)/shard_map/ppermute | solution.py:273
  112.7 18.1 %collective-permute-start.36 = (bf16[2,256,256]{2,1,0:T(8,128)(2,1)S(1)}, bf16[2,256,256]{2,1,0:T(8,128)(2,1)S(1)}, u32[]{:S(2)}, u32[]{:S(2)}) collective-permute-start(bf16[2,256,256]{2,1,0:T(8,128)(2,1)S(1)} %copy-done.67), channel_id=1, source_target_pairs={{0,3},{4,7},{1,2},{5,6},{2,1},{6,5},{3,0},{7,4},{8,11},{12,15},{9,... | collective-permute-start | bytes 786440 | tf_op jit(solution)/shard_map/ppermute | solution.py:261
  112.8 18.0 %collective-permute-start.37 = (bf16[2,256,256]{2,1,0:T(8,128)(2,1)S(1)}, bf16[2,256,256]{2,1,0:T(8,128)(2,1)S(1)}, u32[]{:S(2)}, u32[]{:S(2)}) collective-permute-start(bf16[2,256,256]{2,1,0:T(8,128)(2,1)S(1)} %copy-done.66), channel_id=1, source_target_pairs={{0,7},{4,3},{1,6},{5,2},{2,5},{6,1},{3,4},{7,0},{8,15},{12,11},{9,... | collective-permute-start | bytes 786440 | tf_op jit(solution)/shard_map/ppermute | solution.py:261
  150.4 27.8 %collective-permute-start.50 = (bf16[768,256]{1,0:T(8,128)(2,1)S(1)}, bf16[768,256]{1,0:T(8,128)(2,1)S(1)}, u32[]{:S(2)}, u32[]{:S(2)}) collective-permute-start(bf16[768,256]{1,0:T(8,128)(2,1)S(1)} %get-tuple-element.151), channel_id=1, source_target_pairs={{0,16},{8,24},{16,0},{24,8},{1,17},{9,25},{17,1},{25,9},{2,18},{10... | collective-permute-start | bytes 1179656 | tf_op jit(solution)/shard_map/ppermute | solution.py:273
  152.3 38.8 %collective-permute-start.48 = (bf16[768,256]{1,0:T(8,128)(2,1)S(1)}, bf16[768,256]{1,0:T(8,128)(2,1)S(1)}, u32[]{:S(2)}, u32[]{:S(2)}) collective-permute-start(bf16[768,256]{1,0:T(8,128)(2,1)S(1)} %get-tuple-element.153), channel_id=1, source_target_pairs={{0,16},{8,24},{16,0},{24,8},{1,17},{9,25},{17,1},{25,9},{2,18},{10... | collective-permute-start | bytes 1179656 | tf_op jit(solution)/shard_map/ppermute | solution.py:273
  161.0 27.0 %collective-permute-start.42 = (bf16[256,256]{1,0:T(8,128)(2,1)S(1)}, bf16[256,256]{1,0:T(8,128)(2,1)S(1)}, u32[]{:S(2)}, u32[]{:S(2)}) collective-permute-start(bf16[256,256]{1,0:T(8,128)(2,1)S(1)} %copy-done.87), channel_id=1, source_target_pairs={{0,5},{4,1},{1,4},{5,0},{2,7},{6,3},{3,6},{7,2},{8,13},{12,9},{9,1... | collective-permute-start | bytes 393224 | tf_op jit(solution)/shard_map/ppermute | solution.py:261
  161.7 27.7 %collective-permute-start.43 = (bf16[256,256]{1,0:T(8,128)(2,1)S(1)}, bf16[256,256]{1,0:T(8,128)(2,1)S(1)}, u32[]{:S(2)}, u32[]{:S(2)}) collective-permute-start(bf16[256,256]{1,0:T(8,128)(2,1)S(1)} %copy-done.85), channel_id=1, source_target_pairs={{0,2},{4,6},{1,3},{5,7},{2,0},{6,4},{3,1},{7,5},{8,10},{12,14},{9,... | collective-permute-start | bytes 393224 | tf_op jit(solution)/shard_map/ppermute | solution.py:261
  162.1 27.3 %collective-permute-start.44 = (bf16[256,256]{1,0:T(8,128)(2,1)S(1)}, bf16[256,256]{1,0:T(8,128)(2,1)S(1)}, u32[]{:S(2)}, u32[]{:S(2)}) collective-permute-start(bf16[256,256]{1,0:T(8,128)(2,1)S(1)} %copy-done.83), channel_id=1, source_target_pairs={{0,6},{4,2},{1,7},{5,3},{2,4},{6,0},{3,5},{7,1},{8,14},{12,10},{9,... | collective-permute-start | bytes 393224 | tf_op jit(solution)/shard_map/ppermute | solution.py:261
  188.1 17.4 %collective-permute-start.51 = (bf16[2,256,256]{2,1,0:T(8,128)(2,1)}, bf16[2,256,256]{2,1,0:T(8,128)(2,1)S(1)}, u32[]{:S(2)}, u32[]{:S(2)}) collective-permute-start(bf16[2,256,256]{2,1,0:T(8,128)(2,1)} %get-tuple-element.135), channel_id=1, source_target_pairs={{0,4},{4,0},{1,5},{5,1},{2,6},{6,2},{3,7},{7,3},{8,12},{12,8},{9,1... | collective-permute-start | bytes 786440 | tf_op jit(solution)/shard_map/ppermute | solution.py:261
  189.4 17.7 %collective-permute-start.52 = (bf16[2,256,256]{2,1,0:T(8,128)(2,1)}, bf16[2,256,256]{2,1,0:T(8,128)(2,1)S(1)}, u32[]{:S(2)}, u32[]{:S(2)}) collective-permute-start(bf16[2,256,256]{2,1,0:T(8,128)(2,1)} %get-tuple-element.136), channel_id=1, source_target_pairs={{0,1},{4,5},{1,0},{5,4},{2,3},{6,7},{3,2},{7,6},{8,9},{12,13},{9,8... | collective-permute-start | bytes 786440 | tf_op jit(solution)/shard_map/ppermute | solution.py:261
  189.4 18.7 %collective-permute-start.53 = (bf16[2,256,256]{2,1,0:T(8,128)(2,1)}, bf16[2,256,256]{2,1,0:T(8,128)(2,1)S(1)}, u32[]{:S(2)}, u32[]{:S(2)}) collective-permute-start(bf16[2,256,256]{2,1,0:T(8,128)(2,1)} %get-tuple-element.137), channel_id=1, source_target_pairs={{0,5},{4,1},{1,4},{5,0},{2,7},{6,3},{3,6},{7,2},{8,13},{12,9},{9,1... | collective-permute-start | bytes 786440 | tf_op jit(solution)/shard_map/ppermute | solution.py:261
  190.3 18.5 %collective-permute-start.54 = (bf16[2,256,256]{2,1,0:T(8,128)(2,1)}, bf16[2,256,256]{2,1,0:T(8,128)(2,1)S(1)}, u32[]{:S(2)}, u32[]{:S(2)}) collective-permute-start(bf16[2,256,256]{2,1,0:T(8,128)(2,1)} %get-tuple-element.138), channel_id=1, source_target_pairs={{0,2},{4,6},{1,3},{5,7},{2,0},{6,4},{3,1},{7,5},{8,10},{12,14},{9,... | collective-permute-start | bytes 786440 | tf_op jit(solution)/shard_map/ppermute | solution.py:261
  191.1 14.3 %collective-permute-start.46 = (bf16[256,256]{1,0:T(8,128)(2,1)S(1)}, bf16[256,256]{1,0:T(8,128)(2,1)S(1)}, u32[]{:S(2)}, u32[]{:S(2)}) collective-permute-start(bf16[256,256]{1,0:T(8,128)(2,1)S(1)} %copy-done.80), channel_id=1, source_target_pairs={{0,7},{4,3},{1,6},{5,2},{2,5},{6,1},{3,4},{7,0},{8,15},{12,11},{9,... | collective-permute-start | bytes 393224 | tf_op jit(solution)/shard_map/ppermute | solution.py:261
  205.5 19.2 %collective-permute-start.56 = (bf16[2,256,256]{2,1,0:T(8,128)(2,1)S(1)}, bf16[2,256,256]{2,1,0:T(8,128)(2,1)S(1)}, u32[]{:S(2)}, u32[]{:S(2)}) collective-permute-start(bf16[2,256,256]{2,1,0:T(8,128)(2,1)S(1)} %copy-done.75), channel_id=1, source_target_pairs={{0,3},{4,7},{1,2},{5,6},{2,1},{6,5},{3,0},{7,4},{8,11},{12,15},{9,... | collective-permute-start | bytes 786440 | tf_op jit(solution)/shard_map/ppermute | solution.py:261
  207.1 19.4 %collective-permute-start.57 = (bf16[2,256,256]{2,1,0:T(8,128)(2,1)S(1)}, bf16[2,256,256]{2,1,0:T(8,128)(2,1)S(1)}, u32[]{:S(2)}, u32[]{:S(2)}) collective-permute-start(bf16[2,256,256]{2,1,0:T(8,128)(2,1)S(1)} %copy-done.74), channel_id=1, source_target_pairs={{0,7},{4,3},{1,6},{5,2},{2,5},{6,1},{3,4},{7,0},{8,15},{12,11},{9,... | collective-permute-start | bytes 786440 | tf_op jit(solution)/shard_map/ppermute | solution.py:261
  208.1 19.9 %collective-permute-start.58 = (bf16[2,256,256]{2,1,0:T(8,128)(2,1)}, bf16[2,256,256]{2,1,0:T(8,128)(2,1)S(1)}, u32[]{:S(2)}, u32[]{:S(2)}) collective-permute-start(bf16[2,256,256]{2,1,0:T(8,128)(2,1)} %get-tuple-element.142), channel_id=1, source_target_pairs={{0,4},{4,0},{1,5},{5,1},{2,6},{6,2},{3,7},{7,3},{8,12},{12,8},{9,1... | collective-permute-start | bytes 786440 | tf_op jit(solution)/shard_map/ppermute | solution.py:261
  208.8 19.2 %collective-permute-start.59 = (bf16[2,256,256]{2,1,0:T(8,128)(2,1)}, bf16[2,256,256]{2,1,0:T(8,128)(2,1)S(1)}, u32[]{:S(2)}, u32[]{:S(2)}) collective-permute-start(bf16[2,256,256]{2,1,0:T(8,128)(2,1)} %get-tuple-element.143), channel_id=1, source_target_pairs={{0,1},{4,5},{1,0},{5,4},{2,3},{6,7},{3,2},{7,6},{8,9},{12,13},{9,8... | collective-permute-start | bytes 786440 | tf_op jit(solution)/shard_map/ppermute | solution.py:261
  215.6 17.3 %collective-permute-start.60 = (bf16[2,256,256]{2,1,0:T(8,128)(2,1)}, bf16[2,256,256]{2,1,0:T(8,128)(2,1)S(1)}, u32[]{:S(2)}, u32[]{:S(2)}) collective-permute-start(bf16[2,256,256]{2,1,0:T(8,128)(2,1)} %get-tuple-element.144), channel_id=1, source_target_pairs={{0,5},{4,1},{1,4},{5,0},{2,7},{6,3},{3,6},{7,2},{8,13},{12,9},{9,1... | collective-permute-start | bytes 786440 | tf_op jit(solution)/shard_map/ppermute | solution.py:261
  224.7 20.6 %collective-permute-start.61 = (bf16[2,256,256]{2,1,0:T(8,128)(2,1)}, bf16[2,256,256]{2,1,0:T(8,128)(2,1)S(1)}, u32[]{:S(2)}, u32[]{:S(2)}) collective-permute-start(bf16[2,256,256]{2,1,0:T(8,128)(2,1)} %get-tuple-element.145), channel_id=1, source_target_pairs={{0,2},{4,6},{1,3},{5,7},{2,0},{6,4},{3,1},{7,5},{8,10},{12,14},{9,... | collective-permute-start | bytes 786440 | tf_op jit(solution)/shard_map/ppermute | solution.py:261
  226.6 18.7 %collective-permute-start.62 = (bf16[2,256,256]{2,1,0:T(8,128)(2,1)}, bf16[2,256,256]{2,1,0:T(8,128)(2,1)S(1)}, u32[]{:S(2)}, u32[]{:S(2)}) collective-permute-start(bf16[2,256,256]{2,1,0:T(8,128)(2,1)} %get-tuple-element.146), channel_id=1, source_target_pairs={{0,6},{4,2},{1,7},{5,3},{2,4},{6,0},{3,5},{7,1},{8,14},{12,10},{9,... | collective-permute-start | bytes 786440 | tf_op jit(solution)/shard_map/ppermute | solution.py:261
  228.0 22.6 %collective-permute-start.63 = (bf16[2,256,256]{2,1,0:T(8,128)(2,1)}, bf16[2,256,256]{2,1,0:T(8,128)(2,1)S(1)}, u32[]{:S(2)}, u32[]{:S(2)}) collective-permute-start(bf16[2,256,256]{2,1,0:T(8,128)(2,1)} %get-tuple-element.147), channel_id=1, source_target_pairs={{0,3},{4,7},{1,2},{5,6},{2,1},{6,5},{3,0},{7,4},{8,11},{12,15},{9,... | collective-permute-start | bytes 786440 | tf_op jit(solution)/shard_map/ppermute | solution.py:261
  228.1 22.6 %collective-permute-start.64 = (bf16[2,256,256]{2,1,0:T(8,128)(2,1)}, bf16[2,256,256]{2,1,0:T(8,128)(2,1)S(1)}, u32[]{:S(2)}, u32[]{:S(2)}) collective-permute-start(bf16[2,256,256]{2,1,0:T(8,128)(2,1)} %get-tuple-element.148), channel_id=1, source_target_pairs={{0,7},{4,3},{1,6},{5,2},{2,5},{6,1},{3,4},{7,0},{8,15},{12,11},{9,... | collective-permute-start | bytes 786440 | tf_op jit(solution)/shard_map/ppermute | solution.py:261
  (111 other events, 1954.9 us)

commit v5 on v4

--- a/solution.py
+++ b/solution.py
@@ -55,16 +55,19 @@
                     out[:, columns] = piece[i]
 
 
-def tall_rates(at_ref, rate_refs, n_group, dim):
+def fill_rates(at_ref, rate_refs, tall):
     n_s = len(rate_refs)
     head = at_ref[0] // n_s
-    columns = []
-    for j in range(n_group):
+    for j in range(tall.shape[0]):
         ref = rate_refs[j % n_s]
         row = ref[0, pl.ds(jnp.bitwise_xor(head, j // n_s), 1), :]
-        columns.append(jnp.broadcast_to(row, (128, row.shape[1])).T)
-    tall = jnp.concatenate(columns, axis=0)
-    return jnp.concatenate([tall] * (dim // 128), axis=1)
+        tall[j] = jnp.broadcast_to(row, (tall.shape[2], row.shape[1])).T
+
+
+def tall_rates(tall, rows, dim):
+    start = pl.multiple_of(pl.program_id(0) * rows, rows)
+    column = jnp.concatenate([tall[j, pl.ds(start, rows)] for j in range(tall.shape[0])], axis=0)
+    return jnp.concatenate([column] * (dim // tall.shape[2]), axis=1)
 
 
 def stacked(refs, which):
@@ -81,16 +84,17 @@
 def key_kernel(n_group, n_s, at_ref, *refs):
     pieces, refs = refs[:n_group], refs[n_group:]
     rate_refs, refs = refs[:n_s], refs[n_s:]
-    wg_ref, wu_ref, wd_ref, acc, sent_ref = refs
+    wg_ref, wu_ref, wd_ref, acc, sent_ref, tall = refs
     step = pl.program_id(0)
     dim = pieces[0].shape[-1]
 
     @pl.when(step == 0)
     def _():
         acc[...] = jnp.zeros_like(acc)
+        fill_rates(at_ref, rate_refs, tall)
 
     k = stacked(pieces, 0)
-    rate = tall_rates(at_ref, rate_refs, n_group, dim)
+    rate = tall_rates(tall, pieces[0].shape[1], dim)
     scaled = (rate * stacked(pieces, 1).astype(F32)).astype(BF16)
     gate = mm(k, wg_ref[0])
     up = mm(k, wu_ref[0])
@@ -154,15 +158,16 @@
     rate_refs, refs = refs[:n_s], refs[n_s:]
     w_gate, w_up, w_down = (ref[0] for ref in refs[:3])
     own_ref, other_refs = refs[3], refs[4 : 4 + n_other]
-    outs, adj = refs[4 + n_other : -1], refs[-1]
+    outs, adj, tall = refs[4 + n_other : -2], refs[-2], refs[-1]
     dim = pieces[0].shape[-1]
 
     @pl.when(pl.program_id(0) == 0)
     def _():
         adj[...] = (scale * total_of(own_ref, other_refs)).astype(BF16)
+        fill_rates(at_ref, rate_refs, tall)
 
     k = stacked(pieces, 0)
-    rate = tall_rates(at_ref, rate_refs, n_group, dim)
+    rate = tall_rates(tall, pieces[0].shape[1], dim)
     scaled = (rate * stacked(pieces, 1).astype(F32)).astype(BF16)
     adj_gate, adj_up, adj_down = adj[:dim], adj[dim : 2 * dim], adj[2 * dim :]
     gate = mm(k, w_gate)
@@ -202,6 +207,8 @@
     hops = [1 << i for i in range(n_t.bit_length() - 1)] if n_t & (n_t - 1) == 0 else None
     tile = min(rows, 128)
     grid = (rows // tile,)
+    fine = min(rows, 64)
+    steps = (rows // fine,)
     scale = 1.0 / math.sqrt(dim * rows * n_group * n_t)
     place = lax.axis_index("head") * n_s + lax.axis_index("s")
     at = jnp.stack([place, lax.axis_index("t")]).astype(jnp.int32)
@@ -281,7 +288,10 @@
     ]
 
     def rate_specs(a):
-        return [pl.BlockSpec((1, n_head, tile), lambda i, p: (a, 0, i))] * n_s
+        return [pl.BlockSpec((1, n_head, rows), lambda i, p: (a, 0, 0))] * n_s
+
+    fine_specs = [pl.BlockSpec((2, fine, dim), lambda i, p: (0, i, 0))] * n_group
+    rate_scratch = pltpu.VMEM((n_group, rows, 128), F32)
 
     def w_specs(a):
         spec = pl.BlockSpec(
@@ -305,11 +315,11 @@
     def key_forward(a, after=()):
         own, sent = call(
             functools.partial(key_kernel, n_group, n_s),
-            grid,
-            piece_specs + rate_specs(a) + w_specs(a),
+            steps,
+            fine_specs + rate_specs(a) + w_specs(a),
             sum_specs,
             sum_shapes,
-            [],
+            [rate_scratch],
             *kv[a],
             *rates,
             *weights,
@@ -320,9 +330,9 @@
     def query_side(a, own, others, after=()):
         outs = call(
             functools.partial(query_kernel, scale, n_group, len(others)),
-            grid,
-            piece_specs + w_specs(a) + [sum_spec] * (1 + len(others)),
-            [pl.BlockSpec((tile, dim), lambda i, p: (i, 0))] * n_group + sum_specs,
+            steps,
+            fine_specs + w_specs(a) + [sum_spec] * (1 + len(others)),
+            [pl.BlockSpec((fine, dim), lambda i, p: (i, 0))] * n_group + sum_specs,
             [jax.ShapeDtypeStruct((rows, dim), BF16)] * n_group + sum_shapes,
             [pltpu.VMEM((3 * dim, dim), BF16)],
             *qo[a],
@@ -337,11 +347,11 @@
     def key_back(a, own, others, after=()):
         outs = call(
             functools.partial(back_kernel, scale, n_group, n_s, len(others)),
-            grid,
-            piece_specs + rate_specs(a) + w_specs(a) + [sum_spec] * (1 + len(others)),
-            piece_specs,
+            steps,
+            fine_specs + rate_specs(a) + w_specs(a) + [sum_spec] * (1 + len(others)),
+            fine_specs,
             [jax.ShapeDtypeStruct((2, rows, dim), BF16)] * n_group,
-            [pltpu.VMEM((3 * dim, dim), BF16)],
+            [pltpu.VMEM((3 * dim, dim), BF16), rate_scratch],
             *kv[a],
             *rates,
             *weights,
@@ -352,7 +362,7 @@
         return outs[0], swap(outs)
 
     delta, sums, gq, gkv = ([None] * HEADS_HELD for _ in range(4))
-    mark = ()
+    mark = (qo[0][0],)
     for a in held:
         mark, delta[a] = key_forward(a, mark)
         mark = (mark,)

time: 257 us -> 262 us (1.019)
  Pallas kernels: 61.6 us -> 66.3 us
    pallas_call x10, Pallas kernels: 61.6 us -> 66.3 us  [call(): pl.pallas_call(kernel, out_shape=out_shape, grid_spec=pltpu.PrefetchScala...]
  transfers between devices with their start and end apart: 65 -> 65, of which waited for: 19 -> 19; matrix products, arithmetic and copies ran while one was open for 2% -> 2% of each run, Pallas kernels for 20% -> 22%
where the time goes in v5:
time: 262 us; the launch traced here: 260 us
  waiting for transfers between devices  118 us (45%)
  Pallas kernels  66.3 us (25%)
  starting transfers between devices  65.5 us (25%)
  local copies, waits for them, and re-layouts  4.74 us (2%)
  other arithmetic  4.5 us (2%)
    ppermute x56, waiting for transfers between devices, swap(): lax.ppermute(pieces[j], ('s', 'head'), partners(j))  88.4 us
    pallas_call x10, Pallas kernels, call(): pl.pallas_call(kernel, out_shape=out_shape, grid_spec=pltpu.PrefetchScala...  66.3 us
    ppermute x56, starting transfers between devices, swap(): lax.ppermute(pieces[j], ('s', 'head'), partners(j))  52.5 us
    ppermute x8, waiting for transfers between devices, reduce(): others.append(lax.ppermute(sent, 't', [(j, j ^ hop) for j in range(n_t)]))  21.2 us
    ppermute x8, starting transfers between devices, reduce(): others.append(lax.ppermute(sent, 't', [(j, j ^ hop) for j in range(n_t)]))  11.5 us
    ppermute x1, waiting for transfers between devices, body(): piece = lax.ppermute(piece, 's', [(i, i ^ j) for i in range(n_s)])  8.01 us
  transfers between devices with their start and end apart: 65, of which 19 were waited for; matrix products, arithmetic and copies ran while one was open for 2% of the time, Pallas kernels for 22%

profile of v5, /device:TPU:0, one launch (start us, length us, event | category | flops | bytes accessed | tf_op | source)
XLA Modules:
  0.0 260.4 jit_solution(10122013456624074298)
XLA Ops:
  1.2 4.6 %shard_map.104 = (bf16[2,256,256]{2,1,0:T(8,128)(2,1)}, bf16[2,256,256]{2,1,0:T(8,128)(2,1)}, bf16[2,256,256]{2,1,0:T(8,128)(2,1)}, bf16[2,256,256]{2,1,0:T(8,12...) custom-call(s32[2]{0:T(128)} %pad_add_fusion.at_ref.refs_0_, ...), custom_call_target="tpu_custom_call" | custom-call | tf_op jit(solution)/shard_map/pallas_call | solution.py:236
  5.8 3.0 %collective-permute-start.7 = (bf16[2,256,256]{2,1,0:T(8,128)(2,1)}, bf16[2,256,256]{2,1,0:T(8,128)(2,1)S(1)}, u32[]{:S(2)}, u32[]{:S(2)}) collective-permute-start(bf16[2,256,256]{2,1,0:T(8,128)(2,1)} %get-tuple-element.86), channel_id=1, source_target_pairs={{0,4},{4,0},{1,5},{5,1},{2,6},{6,2},{3,7},{7,3},{8,12},{12,8},{9,1... | collective-permute-start | bytes 786440 | tf_op jit(solution)/shard_map/ppermute | solution.py:268
  9.1 2.0 collective-permute-start.10
  11.7 1.5 collective-permute-start.14
  13.2 8.0 %collective-permute-done.14.refs_10_ = f32[2,4,256]{2,1,0:T(4,128)S(1)} collective-permute-done((f32[2,4,256]{2,1,0:T(4,128)S(1)}, f32[2,4,256]{2,1,0:T(4,128)S(1)}, u32[]{:S(2)}, u32[]{:S(2)}) %collective-permute-start.14) | collective-permute-done | bytes 8224 | tf_op jit(solution)/shard_map/ppermute | solution.py:310
  21.2 2.7 %collective-permute-start.11 = (bf16[2,256,256]{2,1,0:T(8,128)(2,1)}, bf16[2,256,256]{2,1,0:T(8,128)(2,1)S(1)}, u32[]{:S(2)}, u32[]{:S(2)}) collective-permute-start(bf16[2,256,256]{2,1,0:T(8,128)(2,1)} %get-tuple-element.90), channel_id=1, source_target_pairs={{0,6},{4,2},{1,7},{5,3},{2,4},{6,0},{3,5},{7,1},{8,14},{12,10},{9,... | collective-permute-start | bytes 786440 | tf_op jit(solution)/shard_map/ppermute | solution.py:268
  23.9 1.7 collective-permute-start.13
  25.6 1.5 collective-permute-start.17
  27.1 4.1 %collective-permute-done.11.refs_6_ = bf16[2,256,256]{2,1,0:T(8,128)(2,1)S(1)} collective-permute-done((bf16[2,256,256]{2,1,0:T(8,128)(2,1)}, bf16[2,256,256]{2,1,0:T(8,128)(2,1)S(1)}, u32[]{:S(2)}, u32[]{:S(2)}) %collective-permute-start.11) | collective-permute-done | bytes 262176 | tf_op jit(solution)/shard_map/ppermute | solution.py:268
  31.2 9.6 %collective-permute-done.12.refs_7_ = bf16[2,256,256]{2,1,0:T(8,128)(2,1)S(1)} collective-permute-done((bf16[2,256,256]{2,1,0:T(8,128)(2,1)}, bf16[2,256,256]{2,1,0:T(8,128)(2,1)S(1)}, u32[]{:S(2)}, u32[]{:S(2)}) %collective-permute-start.12) | collective-permute-done | bytes 262176 | tf_op jit(solution)/shard_map/ppermute | solution.py:268
  40.8 1.5 collective-permute-start.20
  42.3 1.4 collective-permute-start.21
  44.4 4.5 %shard_map.103 = (bf16[2,256,256]{2,1,0:T(8,128)(2,1)}, bf16[2,256,256]{2,1,0:T(8,128)(2,1)}, bf16[2,256,256]{2,1,0:T(8,128)(2,1)}, bf16[2,256,256]{2,1,0:T(8,12...) custom-call(s32[2]{0:T(128)} %pad_add_fusion.at_ref.refs_0_, ...), custom_call_target="tpu_custom_call" | custom-call | tf_op jit(solution)/shard_map/pallas_call | solution.py:236
  49.1 7.2 %shard_map.105 = (f32[768,256]{1,0:T(8,128)}, bf16[768,256]{1,0:T(8,128)(2,1)}) custom-call(s32[2]{0:T(128)} %pad_add_fusion.at_ref.refs_0_, bf16[2,256,256]{2,1,0:T(8,128)(2,1)} %get-tuple-element.85.refs_1_, bf16[2,256,256]{2,1,0:T(8,128)(2,1)} %copy-done.4, bf16[2,256,256]{2,1,0:T(8,128)(2,1)} %copy-done.5, bf16[2,256,256]{2,1,0:T(8,128)(2,1)} %copy-done.6, ...), custom_call_target="tpu_custom_call" | custom-call | tf_op jit(solution)/shard_map/pallas_call | solution.py:236
  56.3 1.6 collective-permute-start.15
  61.7 5.0 %collective-permute-done.23.refs_8_ = bf16[2,256,256]{2,1,0:T(8,128)(2,1)S(1)} collective-permute-done((bf16[2,256,256]{2,1,0:T(8,128)(2,1)S(1)}, bf16[2,256,256]{2,1,0:T(8,128)(2,1)S(1)}, u32[]{:S(2)}, u32[]{:S(2)}) %collective-permute-start.23) | collective-permute-done | bytes 262176 | tf_op jit(solution)/shard_map/ppermute | solution.py:268
  66.6 1.8 collective-permute-start.3
  68.6 7.2 %shard_map.106 = (f32[768,256]{1,0:T(8,128)}, bf16[768,256]{1,0:T(8,128)(2,1)}) custom-call(s32[2]{0:T(128)} %pad_add_fusion.at_ref.refs_0_, bf16[2,256,256]{2,1,0:T(8,128)(2,1)} %get-tuple-element.95.refs_1_, bf16[2,256,256]{2,1,0:T(8,128)(2,1)} %copy-done.11, bf16[2,256,256]{2,1,0:T(8,128)(2,1)} %copy-done.12, bf16[2,256,256]{2,1,0:T(8,128)(2,1)} %copy-done.13, ...), custom_call_target="tpu_custom_call" | custom-call | tf_op jit(solution)/shard_map/pallas_call | solution.py:236
  76.1 1.5 collective-permute-start.5
  79.0 2.0 collective-permute-start.6
  82.0 2.6 %collective-permute-start.16 = (bf16[768,256]{1,0:T(8,128)(2,1)S(1)}, bf16[768,256]{1,0:T(8,128)(2,1)S(1)}, u32[]{:S(2)}, u32[]{:S(2)}) collective-permute-start(bf16[768,256]{1,0:T(8,128)(2,1)S(1)} %get-tuple-element.157), channel_id=1, source_target_pairs={{0,16},{8,24},{16,0},{24,8},{1,17},{9,25},{17,1},{25,9},{2,18},{10... | collective-permute-start | bytes 1179656 | tf_op jit(solution)/shard_map/ppermute | solution.py:280
  84.6 1.5 collective-permute-done.4.refs_6_
  86.1 9.2 %collective-permute-done.5.refs_7_ = bf16[2,256,256]{2,1,0:T(8,128)(2,1)S(1)} collective-permute-done((bf16[2,256,256]{2,1,0:T(8,128)(2,1)S(1)}, bf16[2,256,256]{2,1,0:T(8,128)(2,1)S(1)}, u32[]{:S(2)}, u32[]{:S(2)}) %collective-permute-start.5) | collective-permute-done | bytes 262176 | tf_op jit(solution)/shard_map/ppermute | solution.py:268
  99.1 3.5 %collective-permute-done.16.refs_13_ = bf16[768,256]{1,0:T(8,128)(2,1)S(1)} collective-permute-done((bf16[768,256]{1,0:T(8,128)(2,1)S(1)}, bf16[768,256]{1,0:T(8,128)(2,1)S(1)}, u32[]{:S(2)}, u32[]{:S(2)}) %collective-permute-start.16) | collective-permute-done | bytes 393248 | tf_op jit(solution)/shard_map/ppermute | solution.py:280
  103.4 7.8 %shard_map.107 = (bf16[256,256]{1,0:T(8,128)(2,1)}, bf16[256,256]{1,0:T(8,128)(2,1)}, bf16[256,256]{1,0:T(8,128)(2,1)}, bf16[256,256]{1,0:T(8,128)(2,1)}, bf16[2...) custom-call(s32[2]{0:T(128)} %pad_add_fusion.at_ref.refs_0_, ...), custom_call_target="tpu_custom_call" | custom-call | tf_op jit(solution)/shard_map/pallas_call | solution.py:236
  111.1 2.6 collective-permute-start.49
  114.8 2.7 %collective-permute-start.37 = (bf16[2,256,256]{2,1,0:T(8,128)(2,1)S(1)}, bf16[2,256,256]{2,1,0:T(8,128)(2,1)S(1)}, u32[]{:S(2)}, u32[]{:S(2)}) collective-permute-start(bf16[2,256,256]{2,1,0:T(8,128)(2,1)S(1)} %copy-done.66), channel_id=1, source_target_pairs={{0,7},{4,3},{1,6},{5,2},{2,5},{6,1},{3,4},{7,0},{8,15},{12,11},{9,... | collective-permute-start | bytes 786440 | tf_op jit(solution)/shard_map/ppermute | solution.py:268
  117.5 6.5 %collective-permute-done.35.refs_6_ = bf16[2,256,256]{2,1,0:T(8,128)(2,1)S(1)} collective-permute-done((bf16[2,256,256]{2,1,0:T(8,128)(2,1)S(1)}, bf16[2,256,256]{2,1,0:T(8,128)(2,1)S(1)}, u32[]{:S(2)}, u32[]{:S(2)}) %collective-permute-start.35) | collective-permute-done | bytes 262176 | tf_op jit(solution)/shard_map/ppermute | solution.py:268
  124.0 9.2 %collective-permute-done.36.refs_7_ = bf16[2,256,256]{2,1,0:T(8,128)(2,1)S(1)} collective-permute-done((bf16[2,256,256]{2,1,0:T(8,128)(2,1)S(1)}, bf16[2,256,256]{2,1,0:T(8,128)(2,1)S(1)}, u32[]{:S(2)}, u32[]{:S(2)}) %collective-permute-start.36) | collective-permute-done | bytes 262176 | tf_op jit(solution)/shard_map/ppermute | solution.py:268
  134.1 7.8 %shard_map.108 = (bf16[256,256]{1,0:T(8,128)(2,1)}, bf16[256,256]{1,0:T(8,128)(2,1)}, bf16[256,256]{1,0:T(8,128)(2,1)}, bf16[256,256]{1,0:T(8,128)(2,1)}, bf16[2...) custom-call(s32[2]{0:T(128)} %pad_add_fusion.at_ref.refs_0_, ...), custom_call_target="tpu_custom_call" | custom-call | tf_op jit(solution)/shard_map/pallas_call | solution.py:236
  142.8 1.6 collective-permute-start.26
  146.0 2.6 %collective-permute-done.24.refs_2_ = bf16[256,256]{1,0:T(8,128)(2,1)S(1)} collective-permute-done((bf16[256,256]{1,0:T(8,128)(2,1)S(1)}, bf16[256,256]{1,0:T(8,128)(2,1)S(1)}, u32[]{:S(2)}, u32[]{:S(2)}) %collective-permute-start.24) | collective-permute-done | bytes 131104 | tf_op jit(solution)/shard_map/ppermute | solution.py:268
  148.8 4.5 %collective-permute-done.47 = bf16[768,256]{1,0:T(8,128)(2,1)S(1)} collective-permute-done((bf16[768,256]{1,0:T(8,128)(2,1)}, bf16[768,256]{1,0:T(8,128)(2,1)S(1)}, u32[]{:S(2)}, u32[]{:S(2)}) %collective-permute-start.47) | collective-permute-done | bytes 393248 | tf_op jit(solution)/shard_map/ppermute | solution.py:280
  155.2 2.0 collective-permute-start.48
  159.1 4.8 %collective-permute-done.30.refs_8_ = bf16[256,256]{1,0:T(8,128)(2,1)S(1)} collective-permute-done((bf16[256,256]{1,0:T(8,128)(2,1)S(1)}, bf16[256,256]{1,0:T(8,128)(2,1)S(1)}, u32[]{:S(2)}, u32[]{:S(2)}) %collective-permute-start.30) | collective-permute-done | bytes 131104 | tf_op jit(solution)/shard_map/ppermute | solution.py:268
  165.0 2.8 %collective-permute-start.44 = (bf16[256,256]{1,0:T(8,128)(2,1)S(1)}, bf16[256,256]{1,0:T(8,128)(2,1)S(1)}, u32[]{:S(2)}, u32[]{:S(2)}) collective-permute-start(bf16[256,256]{1,0:T(8,128)(2,1)S(1)} %copy-done.87), channel_id=1, source_target_pairs={{0,6},{4,2},{1,7},{5,3},{2,4},{6,0},{3,5},{7,1},{8,14},{12,10},{9,... | collective-permute-start | bytes 393224 | tf_op jit(solution)/shard_map/ppermute | solution.py:268
  167.8 13.3 %collective-permute-done.50.refs_15_ = bf16[768,256]{1,0:T(8,128)(2,1)S(1)} collective-permute-done((bf16[768,256]{1,0:T(8,128)(2,1)S(1)}, bf16[768,256]{1,0:T(8,128)(2,1)S(1)}, u32[]{:S(2)}, u32[]{:S(2)}) %collective-permute-start.50) | collective-permute-done | bytes 393248 | tf_op jit(solution)/shard_map/ppermute | solution.py:280
  181.9 9.8 %shard_map.109 = (bf16[2,256,256]{2,1,0:T(8,128)(2,1)}, bf16[2,256,256]{2,1,0:T(8,128)(2,1)}, bf16[2,256,256]{2,1,0:T(8,128)(2,1)}, bf16[2,256,256]{2,1,0:T(8,12...) custom-call(s32[2]{0:T(128)} %pad_add_fusion.at_ref.refs_0_, ...), custom_call_target="tpu_custom_call" | custom-call | tf_op jit(solution)/shard_map/pallas_call | solution.py:236
  196.1 9.6 %shard_map.110 = (bf16[2,256,256]{2,1,0:T(8,128)(2,1)}, bf16[2,256,256]{2,1,0:T(8,128)(2,1)}, bf16[2,256,256]{2,1,0:T(8,128)(2,1)}, bf16[2,256,256]{2,1,0:T(8,12...) custom-call(s32[2]{0:T(128)} %pad_add_fusion.at_ref.refs_0_, ...), custom_call_target="tpu_custom_call" | custom-call | tf_op jit(solution)/shard_map/pallas_call | solution.py:236
  205.6 3.4 %collective-permute-done.46.refs_16_ = bf16[256,256]{1,0:T(8,128)(2,1)S(1)} collective-permute-done((bf16[256,256]{1,0:T(8,128)(2,1)S(1)}, bf16[256,256]{1,0:T(8,128)(2,1)S(1)}, u32[]{:S(2)}, u32[]{:S(2)}) %collective-permute-start.46) | collective-permute-done | bytes 131104 | tf_op jit(solution)/shard_map/ppermute | solution.py:268
  209.5 2.1 collective-permute-start.56
  213.5 5.7 %collective-permute-done.55.refs_5_ = bf16[2,256,256]{2,1,0:T(8,128)(2,1)S(1)} collective-permute-done((bf16[2,256,256]{2,1,0:T(8,128)(2,1)S(1)}, bf16[2,256,256]{2,1,0:T(8,128)(2,1)S(1)}, u32[]{:S(2)}, u32[]{:S(2)}) %collective-permute-start.55) | collective-permute-done | bytes 262176 | tf_op jit(solution)/shard_map/ppermute | solution.py:268
  219.2 10.3 %collective-permute-done.56.refs_6_ = bf16[2,256,256]{2,1,0:T(8,128)(2,1)S(1)} collective-permute-done((bf16[2,256,256]{2,1,0:T(8,128)(2,1)S(1)}, bf16[2,256,256]{2,1,0:T(8,128)(2,1)S(1)}, u32[]{:S(2)}, u32[]{:S(2)}) %collective-permute-start.56) | collective-permute-done | bytes 262176 | tf_op jit(solution)/shard_map/ppermute | solution.py:268
  231.9 2.3 collective-permute-start.64
  234.3 3.4 %shard_map.111 = bf16[256,4096]{1,0:T(8,128)(2,1)} custom-call(s32[2]{0:T(128)} %pad_add_fusion.at_ref.refs_0_, bf16[256,256]{1,0:T(8,128)(2,1)} %get-tuple-element.104.refs_1_, bf16[256,256]{1,0:T(8,128)(2,1)} %copy-done.51, bf16[256,256]{1,0:T(8,128)(2,1)} %copy-done.52, bf16[256,256]{1,0:T(8,128)(2,1)} %copy-done.53, bf16[256,256]{1,0:T(8,128)(2,1)} %copy-done.54, ...), custom_call_target="tpu_custom_call" | custom-call | tf_op jit(solution)/shard_map/pallas_call | solution.py:236
  237.8 12.4 %collective-permute-done.61.refs_12_ = bf16[2,256,256]{2,1,0:T(8,128)(2,1)S(1)} collective-permute-done((bf16[2,256,256]{2,1,0:T(8,128)(2,1)}, bf16[2,256,256]{2,1,0:T(8,128)(2,1)S(1)}, u32[]{:S(2)}, u32[]{:S(2)}) %collective-permute-start.61) | collective-permute-done | bytes 262176 | tf_op jit(solution)/shard_map/ppermute | solution.py:268
  250.1 4.1 %collective-permute-done.63.refs_14_ = bf16[2,256,256]{2,1,0:T(8,128)(2,1)S(1)} collective-permute-done((bf16[2,256,256]{2,1,0:T(8,128)(2,1)}, bf16[2,256,256]{2,1,0:T(8,128)(2,1)S(1)}, u32[]{:S(2)}, u32[]{:S(2)}) %collective-permute-start.63) | collective-permute-done | bytes 262176 | tf_op jit(solution)/shard_map/ppermute | solution.py:268
  255.7 4.6 %shard_map.112 = (bf16[256,4096]{1,0:T(8,128)(2,1)}, bf16[256,4096]{1,0:T(8,128)(2,1)}) custom-call(s32[2]{0:T(128)} %pad_add_fusion.at_ref.refs_0_, bf16[2,256,256]{2,1,0:T(8,128)(2,1)} %get-tuple-element.133.refs_16_.refs_0_, bf16[2,256,256]{2,1,0:T(8,128)(2,1)} %copy-done.22, bf16[2,256,256]{2,1,0:T(8,128)(2,1)} %copy-done.23, ...), custom_call_target="tpu_custom_call" | custom-call | tf_op jit(solution)/shard_map/pallas_call | solution.py:236
  (295 shorter events, 34.1 us)
Async XLA Ops:
  5.8 18.0 %collective-permute-start.7 = (bf16[2,256,256]{2,1,0:T(8,128)(2,1)}, bf16[2,256,256]{2,1,0:T(8,128)(2,1)S(1)}, u32[]{:S(2)}, u32[]{:S(2)}) collective-permute-start(bf16[2,256,256]{2,1,0:T(8,128)(2,1)} %get-tuple-element.86), channel_id=1, source_target_pairs={{0,4},{4,0},{1,5},{5,1},{2,6},{6,2},{3,7},{7,3},{8,12},{12,8},{9,1... | collective-permute-start | bytes 786440 | tf_op jit(solution)/shard_map/ppermute | solution.py:268
  8.9 15.0 %collective-permute-start.8 = (bf16[2,256,256]{2,1,0:T(8,128)(2,1)}, bf16[2,256,256]{2,1,0:T(8,128)(2,1)S(1)}, u32[]{:S(2)}, u32[]{:S(2)}) collective-permute-start(bf16[2,256,256]{2,1,0:T(8,128)(2,1)} %get-tuple-element.87), channel_id=1, source_target_pairs={{0,1},{4,5},{1,0},{5,4},{2,3},{6,7},{3,2},{7,6},{8,9},{12,13},{9,8... | collective-permute-start | bytes 786440 | tf_op jit(solution)/shard_map/ppermute | solution.py:268
  8.9 16.7 %collective-permute-start.9 = (bf16[2,256,256]{2,1,0:T(8,128)(2,1)}, bf16[2,256,256]{2,1,0:T(8,128)(2,1)S(1)}, u32[]{:S(2)}, u32[]{:S(2)}) collective-permute-start(bf16[2,256,256]{2,1,0:T(8,128)(2,1)} %get-tuple-element.88), channel_id=1, source_target_pairs={{0,5},{4,1},{1,4},{5,0},{2,7},{6,3},{3,6},{7,2},{8,13},{12,9},{9,1... | collective-permute-start | bytes 786440 | tf_op jit(solution)/shard_map/ppermute | solution.py:268
  9.1 18.0 %collective-permute-start.10 = (bf16[2,256,256]{2,1,0:T(8,128)(2,1)}, bf16[2,256,256]{2,1,0:T(8,128)(2,1)S(1)}, u32[]{:S(2)}, u32[]{:S(2)}) collective-permute-start(bf16[2,256,256]{2,1,0:T(8,128)(2,1)} %get-tuple-element.89), channel_id=1, source_target_pairs={{0,2},{4,6},{1,3},{5,7},{2,0},{6,4},{3,1},{7,5},{8,10},{12,14},{9,... | collective-permute-start | bytes 786440 | tf_op jit(solution)/shard_map/ppermute | solution.py:268
  23.9 16.9 %collective-permute-start.12 = (bf16[2,256,256]{2,1,0:T(8,128)(2,1)}, bf16[2,256,256]{2,1,0:T(8,128)(2,1)S(1)}, u32[]{:S(2)}, u32[]{:S(2)}) collective-permute-start(bf16[2,256,256]{2,1,0:T(8,128)(2,1)} %get-tuple-element.91), channel_id=1, source_target_pairs={{0,3},{4,7},{1,2},{5,6},{2,1},{6,5},{3,0},{7,4},{8,11},{12,15},{9,... | collective-permute-start | bytes 786440 | tf_op jit(solution)/shard_map/ppermute | solution.py:268
  23.9 18.4 %collective-permute-start.13 = (bf16[2,256,256]{2,1,0:T(8,128)(2,1)}, bf16[2,256,256]{2,1,0:T(8,128)(2,1)S(1)}, u32[]{:S(2)}, u32[]{:S(2)}) collective-permute-start(bf16[2,256,256]{2,1,0:T(8,128)(2,1)} %get-tuple-element.92), channel_id=1, source_target_pairs={{0,7},{4,3},{1,6},{5,2},{2,5},{6,1},{3,4},{7,0},{8,15},{12,11},{9,... | collective-permute-start | bytes 786440 | tf_op jit(solution)/shard_map/ppermute | solution.py:268
  25.6 18.1 %collective-permute-start.17 = (bf16[2,256,256]{2,1,0:T(8,128)(2,1)}, bf16[2,256,256]{2,1,0:T(8,128)(2,1)S(1)}, u32[]{:S(2)}, u32[]{:S(2)}) collective-permute-start(bf16[2,256,256]{2,1,0:T(8,128)(2,1)} %get-tuple-element.96), channel_id=1, source_target_pairs={{0,4},{4,0},{1,5},{5,1},{2,6},{6,2},{3,7},{7,3},{8,12},{12,8},{9,1... | collective-permute-start | bytes 786440 | tf_op jit(solution)/shard_map/ppermute | solution.py:268
  27.1 29.2 %collective-permute-start.18 = (bf16[2,256,256]{2,1,0:T(8,128)(2,1)}, bf16[2,256,256]{2,1,0:T(8,128)(2,1)S(1)}, u32[]{:S(2)}, u32[]{:S(2)}) collective-permute-start(bf16[2,256,256]{2,1,0:T(8,128)(2,1)} %get-tuple-element.97), channel_id=1, source_target_pairs={{0,1},{4,5},{1,0},{5,4},{2,3},{6,7},{3,2},{7,6},{8,9},{12,13},{9,8... | collective-permute-start | bytes 786440 | tf_op jit(solution)/shard_map/ppermute | solution.py:268
  31.2 26.7 %collective-permute-start.19 = (bf16[2,256,256]{2,1,0:T(8,128)(2,1)}, bf16[2,256,256]{2,1,0:T(8,128)(2,1)S(1)}, u32[]{:S(2)}, u32[]{:S(2)}) collective-permute-start(bf16[2,256,256]{2,1,0:T(8,128)(2,1)} %get-tuple-element.98), channel_id=1, source_target_pairs={{0,5},{4,1},{1,4},{5,0},{2,7},{6,3},{3,6},{7,2},{8,13},{12,9},{9,1... | collective-permute-start | bytes 786440 | tf_op jit(solution)/shard_map/ppermute | solution.py:268
  40.8 18.2 %collective-permute-start.20 = (bf16[2,256,256]{2,1,0:T(8,128)(2,1)}, bf16[2,256,256]{2,1,0:T(8,128)(2,1)S(1)}, u32[]{:S(2)}, u32[]{:S(2)}) collective-permute-start(bf16[2,256,256]{2,1,0:T(8,128)(2,1)} %get-tuple-element.99), channel_id=1, source_target_pairs={{0,2},{4,6},{1,3},{5,7},{2,0},{6,4},{3,1},{7,5},{8,10},{12,14},{9,... | collective-permute-start | bytes 786440 | tf_op jit(solution)/shard_map/ppermute | solution.py:268
  42.3 18.0 %collective-permute-start.21 = (bf16[2,256,256]{2,1,0:T(8,128)(2,1)}, bf16[2,256,256]{2,1,0:T(8,128)(2,1)S(1)}, u32[]{:S(2)}, u32[]{:S(2)}) collective-permute-start(bf16[2,256,256]{2,1,0:T(8,128)(2,1)} %get-tuple-element.100), channel_id=1, source_target_pairs={{0,6},{4,2},{1,7},{5,3},{2,4},{6,0},{3,5},{7,1},{8,14},{12,10},{9,... | collective-permute-start | bytes 786440 | tf_op jit(solution)/shard_map/ppermute | solution.py:268
  43.8 16.6 %collective-permute-start.22 = (bf16[2,256,256]{2,1,0:T(8,128)(2,1)}, bf16[2,256,256]{2,1,0:T(8,128)(2,1)S(1)}, u32[]{:S(2)}, u32[]{:S(2)}) collective-permute-start(bf16[2,256,256]{2,1,0:T(8,128)(2,1)} %get-tuple-element.101), channel_id=1, source_target_pairs={{0,3},{4,7},{1,2},{5,6},{2,1},{6,5},{3,0},{7,4},{8,11},{12,15},{9,... | collective-permute-start | bytes 786440 | tf_op jit(solution)/shard_map/ppermute | solution.py:268
  56.3 22.7 %collective-permute-start.15 = (bf16[768,256]{1,0:T(8,128)(2,1)}, bf16[768,256]{1,0:T(8,128)(2,1)S(1)}, u32[]{:S(2)}, u32[]{:S(2)}) collective-permute-start(bf16[768,256]{1,0:T(8,128)(2,1)} %get-tuple-element.94), channel_id=1, source_target_pairs={{0,8},{8,0},{16,24},{24,16},{1,9},{9,1},{17,25},{25,17},{2,10},{10... | collective-permute-start | bytes 1179656 | tf_op jit(solution)/shard_map/ppermute | solution.py:280
  59.0 16.8 %collective-permute-start = (bf16[2,256,256]{2,1,0:T(8,128)(2,1)S(1)}, bf16[2,256,256]{2,1,0:T(8,128)(2,1)S(1)}, u32[]{:S(2)}, u32[]{:S(2)}) collective-permute-start(bf16[2,256,256]{2,1,0:T(8,128)(2,1)S(1)} %copy-done.83), channel_id=1, source_target_pairs={{0,4},{4,0},{1,5},{5,1},{2,6},{6,2},{3,7},{7,3},{8,12},{12,8},{9,1... | collective-permute-start | bytes 786440 | tf_op jit(solution)/shard_map/ppermute | solution.py:268
  60.3 15.8 %collective-permute-start.1 = (bf16[2,256,256]{2,1,0:T(8,128)(2,1)S(1)}, bf16[2,256,256]{2,1,0:T(8,128)(2,1)S(1)}, u32[]{:S(2)}, u32[]{:S(2)}) collective-permute-start(bf16[2,256,256]{2,1,0:T(8,128)(2,1)S(1)} %copy-done.82), channel_id=1, source_target_pairs={{0,1},{4,5},{1,0},{5,4},{2,3},{6,7},{3,2},{7,6},{8,9},{12,13},{9,8... | collective-permute-start | bytes 786440 | tf_op jit(solution)/shard_map/ppermute | solution.py:268
  60.4 17.2 %collective-permute-start.2 = (bf16[2,256,256]{2,1,0:T(8,128)(2,1)S(1)}, bf16[2,256,256]{2,1,0:T(8,128)(2,1)S(1)}, u32[]{:S(2)}, u32[]{:S(2)}) collective-permute-start(bf16[2,256,256]{2,1,0:T(8,128)(2,1)S(1)} %copy-done.81), channel_id=1, source_target_pairs={{0,5},{4,1},{1,4},{5,0},{2,7},{6,3},{3,6},{7,2},{8,13},{12,9},{9,1... | collective-permute-start | bytes 786440 | tf_op jit(solution)/shard_map/ppermute | solution.py:268
  66.6 15.4 %collective-permute-start.3 = (bf16[2,256,256]{2,1,0:T(8,128)(2,1)S(1)}, bf16[2,256,256]{2,1,0:T(8,128)(2,1)S(1)}, u32[]{:S(2)}, u32[]{:S(2)}) collective-permute-start(bf16[2,256,256]{2,1,0:T(8,128)(2,1)S(1)} %copy-done.80), channel_id=1, source_target_pairs={{0,2},{4,6},{1,3},{5,7},{2,0},{6,4},{3,1},{7,5},{8,10},{12,14},{9,... | collective-permute-start | bytes 786440 | tf_op jit(solution)/shard_map/ppermute | solution.py:268
  76.1 19.2 %collective-permute-start.5 = (bf16[2,256,256]{2,1,0:T(8,128)(2,1)S(1)}, bf16[2,256,256]{2,1,0:T(8,128)(2,1)S(1)}, u32[]{:S(2)}, u32[]{:S(2)}) collective-permute-start(bf16[2,256,256]{2,1,0:T(8,128)(2,1)S(1)} %copy-done.77), channel_id=1, source_target_pairs={{0,3},{4,7},{1,2},{5,6},{2,1},{6,5},{3,0},{7,4},{8,11},{12,15},{9,... | collective-permute-start | bytes 786440 | tf_op jit(solution)/shard_map/ppermute | solution.py:268
  77.6 19.6 %collective-permute-start.38 = (bf16[768,256]{1,0:T(8,128)(2,1)}, bf16[768,256]{1,0:T(8,128)(2,1)S(1)}, u32[]{:S(2)}, u32[]{:S(2)}) collective-permute-start(bf16[768,256]{1,0:T(8,128)(2,1)} %get-tuple-element.120), channel_id=1, source_target_pairs={{0,8},{8,0},{16,24},{24,16},{1,9},{9,1},{17,25},{25,17},{2,10},{10... | collective-permute-start | bytes 1179656 | tf_op jit(solution)/shard_map/ppermute | solution.py:280
  79.0 17.1 %collective-permute-start.6 = (bf16[2,256,256]{2,1,0:T(8,128)(2,1)S(1)}, bf16[2,256,256]{2,1,0:T(8,128)(2,1)S(1)}, u32[]{:S(2)}, u32[]{:S(2)}) collective-permute-start(bf16[2,256,256]{2,1,0:T(8,128)(2,1)S(1)} %copy-done.75), channel_id=1, source_target_pairs={{0,7},{4,3},{1,6},{5,2},{2,5},{6,1},{3,4},{7,0},{8,15},{12,11},{9,... | collective-permute-start | bytes 786440 | tf_op jit(solution)/shard_map/ppermute | solution.py:268
  82.0 20.6 %collective-permute-start.16 = (bf16[768,256]{1,0:T(8,128)(2,1)S(1)}, bf16[768,256]{1,0:T(8,128)(2,1)S(1)}, u32[]{:S(2)}, u32[]{:S(2)}) collective-permute-start(bf16[768,256]{1,0:T(8,128)(2,1)S(1)} %get-tuple-element.157), channel_id=1, source_target_pairs={{0,16},{8,24},{16,0},{24,8},{1,17},{9,25},{17,1},{25,9},{2,18},{10... | collective-permute-start | bytes 1179656 | tf_op jit(solution)/shard_map/ppermute | solution.py:280
  86.1 25.0 %collective-permute-start.31 = (bf16[2,256,256]{2,1,0:T(8,128)(2,1)S(1)}, bf16[2,256,256]{2,1,0:T(8,128)(2,1)S(1)}, u32[]{:S(2)}, u32[]{:S(2)}) collective-permute-start(bf16[2,256,256]{2,1,0:T(8,128)(2,1)S(1)} %copy-done.73), channel_id=1, source_target_pairs={{0,4},{4,0},{1,5},{5,1},{2,6},{6,2},{3,7},{7,3},{8,12},{12,8},{9,1... | collective-permute-start | bytes 786440 | tf_op jit(solution)/shard_map/ppermute | solution.py:268
  95.3 18.4 %collective-permute-start.32 = (bf16[2,256,256]{2,1,0:T(8,128)(2,1)S(1)}, bf16[2,256,256]{2,1,0:T(8,128)(2,1)S(1)}, u32[]{:S(2)}, u32[]{:S(2)}) collective-permute-start(bf16[2,256,256]{2,1,0:T(8,128)(2,1)S(1)} %copy-done.71), channel_id=1, source_target_pairs={{0,1},{4,5},{1,0},{5,4},{2,3},{6,7},{3,2},{7,6},{8,9},{12,13},{9,8... | collective-permute-start | bytes 786440 | tf_op jit(solution)/shard_map/ppermute | solution.py:268
  96.1 18.5 %collective-permute-start.33 = (bf16[2,256,256]{2,1,0:T(8,128)(2,1)S(1)}, bf16[2,256,256]{2,1,0:T(8,128)(2,1)S(1)}, u32[]{:S(2)}, u32[]{:S(2)}) collective-permute-start(bf16[2,256,256]{2,1,0:T(8,128)(2,1)S(1)} %copy-done.70), channel_id=1, source_target_pairs={{0,5},{4,1},{1,4},{5,0},{2,7},{6,3},{3,6},{7,2},{8,13},{12,9},{9,1... | collective-permute-start | bytes 786440 | tf_op jit(solution)/shard_map/ppermute | solution.py:268
  97.2 17.5 %collective-permute-start.34 = (bf16[2,256,256]{2,1,0:T(8,128)(2,1)S(1)}, bf16[2,256,256]{2,1,0:T(8,128)(2,1)S(1)}, u32[]{:S(2)}, u32[]{:S(2)}) collective-permute-start(bf16[2,256,256]{2,1,0:T(8,128)(2,1)S(1)} %copy-done.69), channel_id=1, source_target_pairs={{0,2},{4,6},{1,3},{5,7},{2,0},{6,4},{3,1},{7,5},{8,10},{12,14},{9,... | collective-permute-start | bytes 786440 | tf_op jit(solution)/shard_map/ppermute | solution.py:268
  102.6 30.5 %collective-permute-start.39 = (bf16[768,256]{1,0:T(8,128)(2,1)S(1)}, bf16[768,256]{1,0:T(8,128)(2,1)S(1)}, u32[]{:S(2)}, u32[]{:S(2)}) collective-permute-start(bf16[768,256]{1,0:T(8,128)(2,1)S(1)} %get-tuple-element.155), channel_id=1, source_target_pairs={{0,16},{8,24},{16,0},{24,8},{1,17},{9,25},{17,1},{25,9},{2,18},{10... | collective-permute-start | bytes 1179656 | tf_op jit(solution)/shard_map/ppermute | solution.py:280
  111.1 33.3 %collective-permute-start.49 = (bf16[768,256]{1,0:T(8,128)(2,1)}, bf16[768,256]{1,0:T(8,128)(2,1)S(1)}, u32[]{:S(2)}, u32[]{:S(2)}) collective-permute-start(bf16[768,256]{1,0:T(8,128)(2,1)} %get-tuple-element.132), channel_id=1, source_target_pairs={{0,8},{8,0},{16,24},{24,16},{1,9},{9,1},{17,25},{25,17},{2,10},{10... | collective-permute-start | bytes 1179656 | tf_op jit(solution)/shard_map/ppermute | solution.py:280
  114.7 18.4 %collective-permute-start.36 = (bf16[2,256,256]{2,1,0:T(8,128)(2,1)S(1)}, bf16[2,256,256]{2,1,0:T(8,128)(2,1)S(1)}, u32[]{:S(2)}, u32[]{:S(2)}) collective-permute-start(bf16[2,256,256]{2,1,0:T(8,128)(2,1)S(1)} %copy-done.67), channel_id=1, source_target_pairs={{0,3},{4,7},{1,2},{5,6},{2,1},{6,5},{3,0},{7,4},{8,11},{12,15},{9,... | collective-permute-start | bytes 786440 | tf_op jit(solution)/shard_map/ppermute | solution.py:268
  114.8 18.3 %collective-permute-start.37 = (bf16[2,256,256]{2,1,0:T(8,128)(2,1)S(1)}, bf16[2,256,256]{2,1,0:T(8,128)(2,1)S(1)}, u32[]{:S(2)}, u32[]{:S(2)}) collective-permute-start(bf16[2,256,256]{2,1,0:T(8,128)(2,1)S(1)} %copy-done.66), channel_id=1, source_target_pairs={{0,7},{4,3},{1,6},{5,2},{2,5},{6,1},{3,4},{7,0},{8,15},{12,11},{9,... | collective-permute-start | bytes 786440 | tf_op jit(solution)/shard_map/ppermute | solution.py:268
  153.2 27.8 %collective-permute-start.50 = (bf16[768,256]{1,0:T(8,128)(2,1)S(1)}, bf16[768,256]{1,0:T(8,128)(2,1)S(1)}, u32[]{:S(2)}, u32[]{:S(2)}) collective-permute-start(bf16[768,256]{1,0:T(8,128)(2,1)S(1)} %get-tuple-element.151), channel_id=1, source_target_pairs={{0,16},{8,24},{16,0},{24,8},{1,17},{9,25},{17,1},{25,9},{2,18},{10... | collective-permute-start | bytes 1179656 | tf_op jit(solution)/shard_map/ppermute | solution.py:280
  155.2 39.5 %collective-permute-start.48 = (bf16[768,256]{1,0:T(8,128)(2,1)S(1)}, bf16[768,256]{1,0:T(8,128)(2,1)S(1)}, u32[]{:S(2)}, u32[]{:S(2)}) collective-permute-start(bf16[768,256]{1,0:T(8,128)(2,1)S(1)} %get-tuple-element.153), channel_id=1, source_target_pairs={{0,16},{8,24},{16,0},{24,8},{1,17},{9,25},{17,1},{25,9},{2,18},{10... | collective-permute-start | bytes 1179656 | tf_op jit(solution)/shard_map/ppermute | solution.py:280
  163.9 27.7 %collective-permute-start.42 = (bf16[256,256]{1,0:T(8,128)(2,1)S(1)}, bf16[256,256]{1,0:T(8,128)(2,1)S(1)}, u32[]{:S(2)}, u32[]{:S(2)}) collective-permute-start(bf16[256,256]{1,0:T(8,128)(2,1)S(1)} %copy-done.91), channel_id=1, source_target_pairs={{0,5},{4,1},{1,4},{5,0},{2,7},{6,3},{3,6},{7,2},{8,13},{12,9},{9,1... | collective-permute-start | bytes 393224 | tf_op jit(solution)/shard_map/ppermute | solution.py:268
  164.1 28.8 %collective-permute-start.43 = (bf16[256,256]{1,0:T(8,128)(2,1)S(1)}, bf16[256,256]{1,0:T(8,128)(2,1)S(1)}, u32[]{:S(2)}, u32[]{:S(2)}) collective-permute-start(bf16[256,256]{1,0:T(8,128)(2,1)S(1)} %copy-done.89), channel_id=1, source_target_pairs={{0,2},{4,6},{1,3},{5,7},{2,0},{6,4},{3,1},{7,5},{8,10},{12,14},{9,... | collective-permute-start | bytes 393224 | tf_op jit(solution)/shard_map/ppermute | solution.py:268
  165.0 27.9 %collective-permute-start.44 = (bf16[256,256]{1,0:T(8,128)(2,1)S(1)}, bf16[256,256]{1,0:T(8,128)(2,1)S(1)}, u32[]{:S(2)}, u32[]{:S(2)}) collective-permute-start(bf16[256,256]{1,0:T(8,128)(2,1)S(1)} %copy-done.87), channel_id=1, source_target_pairs={{0,6},{4,2},{1,7},{5,3},{2,4},{6,0},{3,5},{7,1},{8,14},{12,10},{9,... | collective-permute-start | bytes 393224 | tf_op jit(solution)/shard_map/ppermute | solution.py:268
  191.7 17.8 %collective-permute-start.51 = (bf16[2,256,256]{2,1,0:T(8,128)(2,1)}, bf16[2,256,256]{2,1,0:T(8,128)(2,1)S(1)}, u32[]{:S(2)}, u32[]{:S(2)}) collective-permute-start(bf16[2,256,256]{2,1,0:T(8,128)(2,1)} %get-tuple-element.135), channel_id=1, source_target_pairs={{0,4},{4,0},{1,5},{5,1},{2,6},{6,2},{3,7},{7,3},{8,12},{12,8},{9,1... | collective-permute-start | bytes 786440 | tf_op jit(solution)/shard_map/ppermute | solution.py:268
  192.9 18.6 %collective-permute-start.52 = (bf16[2,256,256]{2,1,0:T(8,128)(2,1)}, bf16[2,256,256]{2,1,0:T(8,128)(2,1)S(1)}, u32[]{:S(2)}, u32[]{:S(2)}) collective-permute-start(bf16[2,256,256]{2,1,0:T(8,128)(2,1)} %get-tuple-element.136), channel_id=1, source_target_pairs={{0,1},{4,5},{1,0},{5,4},{2,3},{6,7},{3,2},{7,6},{8,9},{12,13},{9,8... | collective-permute-start | bytes 786440 | tf_op jit(solution)/shard_map/ppermute | solution.py:268
  193.0 18.9 %collective-permute-start.53 = (bf16[2,256,256]{2,1,0:T(8,128)(2,1)}, bf16[2,256,256]{2,1,0:T(8,128)(2,1)S(1)}, u32[]{:S(2)}, u32[]{:S(2)}) collective-permute-start(bf16[2,256,256]{2,1,0:T(8,128)(2,1)} %get-tuple-element.137), channel_id=1, source_target_pairs={{0,5},{4,1},{1,4},{5,0},{2,7},{6,3},{3,6},{7,2},{8,13},{12,9},{9,1... | collective-permute-start | bytes 786440 | tf_op jit(solution)/shard_map/ppermute | solution.py:268
  193.9 19.2 %collective-permute-start.54 = (bf16[2,256,256]{2,1,0:T(8,128)(2,1)}, bf16[2,256,256]{2,1,0:T(8,128)(2,1)S(1)}, u32[]{:S(2)}, u32[]{:S(2)}) collective-permute-start(bf16[2,256,256]{2,1,0:T(8,128)(2,1)} %get-tuple-element.138), channel_id=1, source_target_pairs={{0,2},{4,6},{1,3},{5,7},{2,0},{6,4},{3,1},{7,5},{8,10},{12,14},{9,... | collective-permute-start | bytes 786440 | tf_op jit(solution)/shard_map/ppermute | solution.py:268
  194.7 14.3 %collective-permute-start.46 = (bf16[256,256]{1,0:T(8,128)(2,1)S(1)}, bf16[256,256]{1,0:T(8,128)(2,1)S(1)}, u32[]{:S(2)}, u32[]{:S(2)}) collective-permute-start(bf16[256,256]{1,0:T(8,128)(2,1)S(1)} %copy-done.84), channel_id=1, source_target_pairs={{0,7},{4,3},{1,6},{5,2},{2,5},{6,1},{3,4},{7,0},{8,15},{12,11},{9,... | collective-permute-start | bytes 393224 | tf_op jit(solution)/shard_map/ppermute | solution.py:268
  209.5 20.0 %collective-permute-start.56 = (bf16[2,256,256]{2,1,0:T(8,128)(2,1)S(1)}, bf16[2,256,256]{2,1,0:T(8,128)(2,1)S(1)}, u32[]{:S(2)}, u32[]{:S(2)}) collective-permute-start(bf16[2,256,256]{2,1,0:T(8,128)(2,1)S(1)} %copy-done.76), channel_id=1, source_target_pairs={{0,3},{4,7},{1,2},{5,6},{2,1},{6,5},{3,0},{7,4},{8,11},{12,15},{9,... | collective-permute-start | bytes 786440 | tf_op jit(solution)/shard_map/ppermute | solution.py:268
  211.5 18.6 %collective-permute-start.57 = (bf16[2,256,256]{2,1,0:T(8,128)(2,1)S(1)}, bf16[2,256,256]{2,1,0:T(8,128)(2,1)S(1)}, u32[]{:S(2)}, u32[]{:S(2)}) collective-permute-start(bf16[2,256,256]{2,1,0:T(8,128)(2,1)S(1)} %copy-done.74), channel_id=1, source_target_pairs={{0,7},{4,3},{1,6},{5,2},{2,5},{6,1},{3,4},{7,0},{8,15},{12,11},{9,... | collective-permute-start | bytes 786440 | tf_op jit(solution)/shard_map/ppermute | solution.py:268
  211.9 19.5 %collective-permute-start.58 = (bf16[2,256,256]{2,1,0:T(8,128)(2,1)}, bf16[2,256,256]{2,1,0:T(8,128)(2,1)S(1)}, u32[]{:S(2)}, u32[]{:S(2)}) collective-permute-start(bf16[2,256,256]{2,1,0:T(8,128)(2,1)} %get-tuple-element.142), channel_id=1, source_target_pairs={{0,4},{4,0},{1,5},{5,1},{2,6},{6,2},{3,7},{7,3},{8,12},{12,8},{9,1... | collective-permute-start | bytes 786440 | tf_op jit(solution)/shard_map/ppermute | solution.py:268
  213.1 18.8 %collective-permute-start.59 = (bf16[2,256,256]{2,1,0:T(8,128)(2,1)}, bf16[2,256,256]{2,1,0:T(8,128)(2,1)S(1)}, u32[]{:S(2)}, u32[]{:S(2)}) collective-permute-start(bf16[2,256,256]{2,1,0:T(8,128)(2,1)} %get-tuple-element.143), channel_id=1, source_target_pairs={{0,1},{4,5},{1,0},{5,4},{2,3},{6,7},{3,2},{7,6},{8,9},{12,13},{9,8... | collective-permute-start | bytes 786440 | tf_op jit(solution)/shard_map/ppermute | solution.py:268
  219.2 18.5 %collective-permute-start.60 = (bf16[2,256,256]{2,1,0:T(8,128)(2,1)}, bf16[2,256,256]{2,1,0:T(8,128)(2,1)S(1)}, u32[]{:S(2)}, u32[]{:S(2)}) collective-permute-start(bf16[2,256,256]{2,1,0:T(8,128)(2,1)} %get-tuple-element.144), channel_id=1, source_target_pairs={{0,5},{4,1},{1,4},{5,0},{2,7},{6,3},{3,6},{7,2},{8,13},{12,9},{9,1... | collective-permute-start | bytes 786440 | tf_op jit(solution)/shard_map/ppermute | solution.py:268
  229.5 20.6 %collective-permute-start.61 = (bf16[2,256,256]{2,1,0:T(8,128)(2,1)}, bf16[2,256,256]{2,1,0:T(8,128)(2,1)S(1)}, u32[]{:S(2)}, u32[]{:S(2)}) collective-permute-start(bf16[2,256,256]{2,1,0:T(8,128)(2,1)} %get-tuple-element.145), channel_id=1, source_target_pairs={{0,2},{4,6},{1,3},{5,7},{2,0},{6,4},{3,1},{7,5},{8,10},{12,14},{9,... | collective-permute-start | bytes 786440 | tf_op jit(solution)/shard_map/ppermute | solution.py:268
  230.1 20.0 %collective-permute-start.62 = (bf16[2,256,256]{2,1,0:T(8,128)(2,1)}, bf16[2,256,256]{2,1,0:T(8,128)(2,1)S(1)}, u32[]{:S(2)}, u32[]{:S(2)}) collective-permute-start(bf16[2,256,256]{2,1,0:T(8,128)(2,1)} %get-tuple-element.146), channel_id=1, source_target_pairs={{0,6},{4,2},{1,7},{5,3},{2,4},{6,0},{3,5},{7,1},{8,14},{12,10},{9,... | collective-permute-start | bytes 786440 | tf_op jit(solution)/shard_map/ppermute | solution.py:268
  231.4 22.8 %collective-permute-start.63 = (bf16[2,256,256]{2,1,0:T(8,128)(2,1)}, bf16[2,256,256]{2,1,0:T(8,128)(2,1)S(1)}, u32[]{:S(2)}, u32[]{:S(2)}) collective-permute-start(bf16[2,256,256]{2,1,0:T(8,128)(2,1)} %get-tuple-element.147), channel_id=1, source_target_pairs={{0,3},{4,7},{1,2},{5,6},{2,1},{6,5},{3,0},{7,4},{8,11},{12,15},{9,... | collective-permute-start | bytes 786440 | tf_op jit(solution)/shard_map/ppermute | solution.py:268
  231.9 22.3 %collective-permute-start.64 = (bf16[2,256,256]{2,1,0:T(8,128)(2,1)}, bf16[2,256,256]{2,1,0:T(8,128)(2,1)S(1)}, u32[]{:S(2)}, u32[]{:S(2)}) collective-permute-start(bf16[2,256,256]{2,1,0:T(8,128)(2,1)} %get-tuple-element.148), channel_id=1, source_target_pairs={{0,7},{4,3},{1,6},{5,2},{2,5},{6,1},{3,4},{7,0},{8,15},{12,11},{9,... | collective-permute-start | bytes 786440 | tf_op jit(solution)/shard_map/ppermute | solution.py:268
  (115 other events, 2051.9 us)
